TPU v7x, 32 devices: a whole 2x2x4 slice. The times are simulated.
32 devices in a mesh: groups: 2 (over x), ctx: 16 (over z, y, core).
Axes of the slice: x: 2, y: 2, z: 4, core: 2. Of those that a mesh axis runs over, the one named last changes fastest.
Arguments:
- gate_out: bfloat16 [8192, 2048], P(('groups', 'ctx')), parts along dimension 0, may hold values from -6 to 6
- gate_in: bfloat16 [8192, 2048], P(('groups', 'ctx')), parts along dimension 0, may hold values from -6 to 6
- values: bfloat16 [8192, 2048], P(('groups', 'ctx')), parts along dimension 0, may hold values from -6 to 6
- filter_taps: bfloat16 [1024, 2048], P(None, 'ctx'), may hold values from -0.1875 to 0.1875
- skip_gain: float32 [2048], replicated, may hold values from -4 to 4
Outputs:
- operator_out: bfloat16 [8192, 2048], P(('groups', 'ctx')), parts along dimension 0
There are 2 independent parts, one for each index of `groups`. A program takes and returns all parts, laid end to end along the dimension named above; an argument that names none is the same for every part. Nothing has to cross between parts.
All inputs are finite; a program needn't handle non-finite values.
Results may differ from a plain program's by a relative error of at most 0.005.
Values may be sent and summed in bfloat16 or wider, within the bound.
No kernel may reach another device: no remote copies, remote signals or barrier semaphores. Data moves between devices by JAX's collectives and lax.ppermute only.
A program may use at most 128 MiB of HBM per device.

v0:
```python
import math

import jax
import jax.numpy as jnp
from jax import lax
from jax.sharding import PartitionSpec as P


def shifted(value, axis, by):
    length = lax.axis_size(axis)
    return lax.ppermute(value, axis, [(i, (i + by) % length) for i in range(length)])


def forward_table(rows):
    bins = lax.broadcasted_iota(jnp.int32, (rows + 1, rows), 0)
    places = lax.broadcasted_iota(jnp.int32, (rows + 1, rows), 1)
    angle = (bins * places % (2 * rows)).astype(jnp.float32) * (math.pi / rows)
    return jnp.concatenate([jnp.cos(angle), -jnp.sin(angle)], axis=0)


def inverse_table(rows):
    places = lax.broadcasted_iota(jnp.int32, (2 * rows, rows + 1), 0)
    bins = lax.broadcasted_iota(jnp.int32, (2 * rows, rows + 1), 1)
    angle = (bins * places % (2 * rows)).astype(jnp.float32) * (math.pi / rows)
    weight = jnp.where((bins == 0) | (bins == rows), 1.0, 2.0) / (2.0 * rows)
    return jnp.concatenate([weight * jnp.cos(angle), -weight * jnp.sin(angle)], axis=1)


def spectrum(table, block):
    return jnp.dot(table, block.astype(jnp.float32), precision=lax.Precision.HIGHEST)


def complex_product(first, second):
    split_at = first.shape[0] // 2
    first_real, first_imag = (first[:split_at], first[split_at:])
    second_real, second_imag = (second[:split_at], second[split_at:])
    real_part = first_real * second_real - first_imag * second_imag
    imag_part = first_real * second_imag + first_imag * second_real
    return jnp.concatenate([real_part, imag_part], axis=0)


def fetch_blocks(product, count):
    return [shifted(product, "ctx", distance) for distance in range(1, count + 1)]


def on_device(gate_out, gate_in, values, filter_taps, skip_gain):
    rows = values.shape[0]
    product = (gate_in.astype(jnp.float32) * values.astype(jnp.float32)).astype(jnp.bfloat16)
    all_taps = lax.all_gather(filter_taps, "ctx", axis=1, tiled=True)
    count = all_taps.shape[0] // rows
    forward = forward_table(rows)
    backward = inverse_table(rows)
    own_spectrum = spectrum(forward, product)
    received = [spectrum(forward, block) for block in fetch_blocks(product, count)]
    spectra = [own_spectrum] + received
    current_sum = jnp.zeros_like(own_spectrum)
    previous_sum = jnp.zeros_like(own_spectrum)
    for lag_block in range(count):
        tap_spectrum = spectrum(forward, all_taps[lag_block * rows : (lag_block + 1) * rows])
        current_sum = current_sum + complex_product(tap_spectrum, spectra[lag_block])
        previous_sum = previous_sum + complex_product(tap_spectrum, spectra[lag_block + 1])
    convolved = jnp.dot(backward[:rows], current_sum, precision=lax.Precision.HIGHEST)
    convolved = convolved + jnp.dot(backward[rows:], previous_sum, precision=lax.Precision.HIGHEST)
    mixed = gate_out.astype(jnp.float32) * (
        convolved + skip_gain[None, :] * product.astype(jnp.float32)
    )
    return mixed.astype(jnp.bfloat16)


def solution(mesh):
    in_specs = (
        P(("groups", "ctx"), None),
        P(("groups", "ctx"), None),
        P(("groups", "ctx"), None),
        P(None, "ctx"),
        P(),
    )
    out_specs = P(("groups", "ctx"), None)
    return jax.shard_map(
        on_device, mesh=mesh, in_specs=in_specs, out_specs=out_specs, check_vma=False
    )
```

profile of v0, /device:TPU:0, one launch (start us, length us, event | category | flops | bytes accessed | tf_op | source)
XLA Modules:
  0.0 200.9 jit_solution(11566956663517549847)
XLA Ops:
  6.5 0.7 all-gather.2.cloned.1.call-update
  7.3 1.9 multiply_convert_fusion
  9.2 0.0 copy-start.1
  9.2 2.5 %collective-permute-start.2 = (bf16[256,2048]{1,0:T(8,128)(2,1)S(1)}, bf16[256,2048]{1,0:T(8,128)(2,1)S(1)}, u32[]{:S(2)}, u32[]{:S(2)}) collective-permute-start(bf16[256,2048]{1,0:T(8,128)(2,1)S(1)} %multiply_convert_fusion), channel_id=1, source_target_pairs={{0,3},{1,4},{2,5},{3,6},{4,7},{5,8},{6,9},{7,10},{8,11},{9,12},{10... | collective-permute-start | bytes 3145736 | tf_op jit(solution)/shard_map/ppermute | solution.py:11
  11.7 1.6 collective-permute-start.3
  13.2 1.5 collective-permute-start.1
  14.8 0.2 collective-permute-start
  14.9 1.1 sine_negate_fusion
  16.0 4.0 %sine_multiply_fusion = (f32[512,257]{1,0:T(8,128)}, f32[512,257]{1,0:T(8,128)}) fusion(f32[257]{0:T(512)S(1)} %fusion.67, f32[257]{0:T(512)S(1)} %select_multiply_fusion), kind=kLoop, calls=%fused_computation.67 | loop fusion | flops 2105344 | bytes 1054728 | tf_op jit(solution)/shard_map/mul | solution.py:26
  20.0 3.9 %fusion.74 = f32[514,2048]{1,0:T(8,128)} fusion(bf16[256,2048]{1,0:T(8,128)(2,1)S(1)} %multiply_convert_fusion, f32[257,256]{1,0:T(8,128)S(1)} %get-tuple-element.29, f32[257,256]{1,0:T(8,128)S(1)} %get-tuple-element.30), kind=kOutput, calls=%fused_computation.98 | convolution fusion | flops 3233939968 | bytes 5785600 | tf_op jit(solution)/shard_map/dot_general | solution.py:30
  23.9 19.9 %collective-permute-done.2 = bf16[256,2048]{1,0:T(8,128)(2,1)S(1)} collective-permute-done((bf16[256,2048]{1,0:T(8,128)(2,1)S(1)}, bf16[256,2048]{1,0:T(8,128)(2,1)S(1)}, u32[]{:S(2)}, u32[]{:S(2)}) %collective-permute-start.2) | collective-permute-done | bytes 1048608 | tf_op jit(solution)/shard_map/ppermute | solution.py:11
  43.9 3.8 %fusion.71 = f32[514,2048]{1,0:T(8,128)} fusion(bf16[256,2048]{1,0:T(8,128)(2,1)S(1)} %collective-permute-done.2, f32[257,256]{1,0:T(8,128)S(1)} %get-tuple-element.29, f32[257,256]{1,0:T(8,128)S(1)} %get-tuple-element.30), kind=kOutput, calls=%fused_computation.95 | convolution fusion | flops 3233939968 | bytes 5785600 | tf_op jit(solution)/shard_map/dot_general | solution.py:30
  47.7 0.4 collective-permute-done.3
  48.1 3.8 %fusion.70 = f32[514,2048]{1,0:T(8,128)} fusion(bf16[256,2048]{1,0:T(8,128)(2,1)S(1)} %collective-permute-done.3, f32[257,256]{1,0:T(8,128)S(1)} %get-tuple-element.29, f32[257,256]{1,0:T(8,128)S(1)} %get-tuple-element.30), kind=kOutput, calls=%fused_computation.94 | convolution fusion | flops 3233939968 | bytes 5785600 | tf_op jit(solution)/shard_map/dot_general | solution.py:30
  51.9 57.6 %collective-permute-done.1 = bf16[256,2048]{1,0:T(8,128)(2,1)S(1)} collective-permute-done((bf16[256,2048]{1,0:T(8,128)(2,1)S(1)}, bf16[256,2048]{1,0:T(8,128)(2,1)S(1)}, u32[]{:S(2)}, u32[]{:S(2)}) %collective-permute-start.1) | collective-permute-done | bytes 1048608 | tf_op jit(solution)/shard_map/ppermute | solution.py:11
  109.5 3.9 %fusion.72 = f32[514,2048]{1,0:T(8,128)} fusion(bf16[256,2048]{1,0:T(8,128)(2,1)S(1)} %collective-permute-done.1, f32[257,256]{1,0:T(8,128)S(1)} %get-tuple-element.29, f32[257,256]{1,0:T(8,128)S(1)} %get-tuple-element.30), kind=kOutput, calls=%fused_computation.96 | convolution fusion | flops 3233939968 | bytes 5785600 | tf_op jit(solution)/shard_map/dot_general | solution.py:30
  113.4 7.1 %collective-permute-done = bf16[256,2048]{1,0:T(8,128)(2,1)S(1)} collective-permute-done((bf16[256,2048]{1,0:T(8,128)(2,1)S(1)}, bf16[256,2048]{1,0:T(8,128)(2,1)S(1)}, u32[]{:S(2)}, u32[]{:S(2)}) %collective-permute-start) | collective-permute-done | bytes 1048608 | tf_op jit(solution)/shard_map/ppermute | solution.py:11
  120.5 3.9 %fusion.73 = f32[514,2048]{1,0:T(8,128)} fusion(bf16[256,2048]{1,0:T(8,128)(2,1)S(1)} %collective-permute-done, f32[257,256]{1,0:T(8,128)S(1)} %get-tuple-element.29, f32[257,256]{1,0:T(8,128)S(1)} %get-tuple-element.30), kind=kOutput, calls=%fused_computation.97 | convolution fusion | flops 3233939968 | bytes 5785600 | tf_op jit(solution)/shard_map/dot_general | solution.py:30
  124.4 3.3 %fusion.42 = f32[514,2048]{1,0:T(8,128)S(1)} fusion(bf16[1024,2048]{1,0:T(8,128)(2,1)} %all-gather.2.cloned.1.call-done, f32[257,256]{1,0:T(8,128)S(1)} %get-tuple-element.29, f32[257,256]{1,0:T(8,128)} %copy-done), kind=kOutput, calls=%fused_computation.56 | convolution fusion | flops 3233939968 | bytes 5792768 | tf_op jit(solution)/shard_map/dot_general | solution.py:30
  127.7 0.0 slice-start.3
  127.7 9.7 %multiply_subtract_fusion = (f32[257,2048]{1,0:T(8,128)}, f32[257,2048]{1,0:T(8,128)}, f32[257,2048]{1,0:T(8,128)}, f32[257,2048]{1,0:T(8,128)}) fusion(f32[514,2048]{1,0:T(8,128)} %fusion.70, f32[514,2048]{1,0:T(8,128)S(1)} %fusion.42, f32[514,2048]{1,0:T(8,128)} %fusion.71), kind=kLoop, calls=%fused_computation.35 | loop fusion | flops 6316032 | bytes 21053440 | tf_op jit(solution)/shard_map/sub | solution.py:37
  137.4 5.3 %fusion.44 = f32[514,2048]{1,0:T(8,128)} fusion(bf16[1024,2048]{1,0:T(8,128)(2,1)} %all-gather.2.cloned.1.call-done, f32[257,256]{1,0:T(8,128)S(1)} %get-tuple-element.29, f32[257,256]{1,0:T(8,128)} %copy-done), kind=kOutput, calls=%fused_computation.58 | convolution fusion | flops 3233939968 | bytes 5792768 | tf_op jit(solution)/shard_map/dot_general | solution.py:30
  142.7 8.1 %multiply_subtract_fusion.1 = (f32[257,2048]{1,0:T(8,128)}, f32[257,2048]{1,0:T(8,128)}, f32[257,2048]{1,0:T(8,128)}, f32[257,2048]{1,0:T(8,128)}) fusion(f32[514,2048]{1,0:T(8,128)S(1)} %bitcast.8, f32[514,2048]{1,0:T(8,128)} %fusion.44, f32[514,2048]{1,0:T(8,128)S(1)} %bitcast.10), kind=kLoop, calls=%fused_computation.37 | loop fusion | flops 6316032 | bytes 21053440 | tf_op jit(solution)/shard_map/sub | solution.py:37
  150.8 5.3 %fusion.46 = f32[514,2048]{1,0:T(8,128)} fusion(bf16[1024,2048]{1,0:T(8,128)(2,1)} %all-gather.2.cloned.1.call-done, f32[257,256]{1,0:T(8,128)S(1)} %get-tuple-element.29, f32[257,256]{1,0:T(8,128)} %copy-done), kind=kOutput, calls=%fused_computation.60 | convolution fusion | flops 3233939968 | bytes 5792768 | tf_op jit(solution)/shard_map/dot_general | solution.py:30
  156.1 8.2 %multiply_subtract_fusion.2 = (f32[257,2048]{1,0:T(8,128)}, f32[257,2048]{1,0:T(8,128)}, f32[257,2048]{1,0:T(8,128)}, f32[257,2048]{1,0:T(8,128)}) fusion(f32[514,2048]{1,0:T(8,128)S(1)} %bitcast.10, f32[514,2048]{1,0:T(8,128)} %fusion.46, f32[514,2048]{1,0:T(8,128)S(1)} %bitcast.6), kind=kLoop, calls=%fused_computation.39 | loop fusion | flops 6316032 | bytes 21053440 | tf_op jit(solution)/shard_map/sub | solution.py:37
  164.2 3.1 %fusion.48 = f32[514,2048]{1,0:T(8,128)S(1)} fusion(bf16[1024,2048]{1,0:T(8,128)(2,1)} %all-gather.2.cloned.1.call-done, f32[257,256]{1,0:T(8,128)S(1)} %get-tuple-element.29, f32[257,256]{1,0:T(8,128)} %copy-done), kind=kOutput, calls=%fused_computation.62 | convolution fusion | flops 3233939968 | bytes 5792768 | tf_op jit(solution)/shard_map/dot_general | solution.py:30
  167.4 6.1 %multiply_subtract_fusion.3 = (f32[257,2048]{1,0:T(8,128)}, f32[257,2048]{1,0:T(8,128)}, f32[257,2048]{1,0:T(8,128)}, f32[257,2048]{1,0:T(8,128)}) fusion(f32[514,2048]{1,0:T(8,128)S(1)} %bitcast.6, f32[514,2048]{1,0:T(8,128)S(1)} %fusion.48, f32[514,2048]{1,0:T(8,128)S(1)} %bitcast.12), kind=kLoop, calls=%fused_computation.41 | loop fusion | flops 6316032 | bytes 21053440 | tf_op jit(solution)/shard_map/sub | solution.py:37
  173.5 0.0 copy-start.11
  173.6 10.5 %fusion.2 = f32[256,2048]{1,0:T(8,128)S(1)} fusion(f32[257,2048]{1,0:T(8,128)} %get-tuple-element.27, f32[257,2048]{1,0:T(8,128)} %get-tuple-element.28, f32[257,2048]{1,0:T(8,128)} %get-tuple-element.25, f32[257,2048]{1,0:T(8,128)} %get-tuple-element.26, f32[257,2048]{1,0:T(8,128)} %get-tuple-element.23, f32[257,2048]{1,0:T(8,128)} %get-tuple-element.24, ...), kind=kOutput, calls=%fused_computation.3 | convolution fusion | flops 3241308672 | bytes 19992576 | tf_op jit(solution)/shard_map/dot_general | solution.py:62
  184.2 0.2 copy-done.9
  184.4 0.6 copy-done.10
  185.0 9.0 %fusion.39 = bf16[256,2048]{1,0:T(8,128)(2,1)} fusion(f32[256,2048]{1,0:T(8,128)S(1)} %fusion.2, f32[257,2048]{1,0:T(8,128)S(1)} %copy-done.10, f32[257,2048]{1,0:T(8,128)S(1)} %copy-done.9, f32[257,2048]{1,0:T(8,128)S(1)} %copy-done.8, f32[257,2048]{1,0:T(8,128)S(1)} %copy-done.7, f32[257,2048]{1,0:T(8,128)S(1)} %copy-done.6, ...), kind=kOutput, calls=%fused_computation.33 | convolution fusion | flops 3244978688 | bytes 23146496 | tf_op jit(solution)/shard_map/dot_general | solution.py:63
  (43 shorter events, 0.1 us)
Async XLA Ops:
  6.5 117.9 %all-gather.2.cloned.1.call-start = ((), (), s32[]{:S(2)}) async-start(), calls=%async_computation | async-start | bytes 4456448 | tf_op jit(solution)/shard_map/all_gather | solution.py:49
  9.2 14.7 %copy-start.1 = (bf16[256,2048]{1,0:T(8,128)(2,1)}, bf16[256,2048]{1,0:T(8,128)(2,1)S(1)}, u32[]{:S(2)}) copy-start(bf16[256,2048]{1,0:T(8,128)(2,1)S(1)} %multiply_convert_fusion) | copy-start | bytes 3145732
  9.2 34.7 %collective-permute-start.2 = (bf16[256,2048]{1,0:T(8,128)(2,1)S(1)}, bf16[256,2048]{1,0:T(8,128)(2,1)S(1)}, u32[]{:S(2)}, u32[]{:S(2)}) collective-permute-start(bf16[256,2048]{1,0:T(8,128)(2,1)S(1)} %multiply_convert_fusion), channel_id=1, source_target_pairs={{0,3},{1,4},{2,5},{3,6},{4,7},{5,8},{6,9},{7,10},{8,11},{9,12},{10... | collective-permute-start | bytes 3145736 | tf_op jit(solution)/shard_map/ppermute | solution.py:11
  11.7 36.4 %collective-permute-start.3 = (bf16[256,2048]{1,0:T(8,128)(2,1)S(1)}, bf16[256,2048]{1,0:T(8,128)(2,1)S(1)}, u32[]{:S(2)}, u32[]{:S(2)}) collective-permute-start(bf16[256,2048]{1,0:T(8,128)(2,1)S(1)} %multiply_convert_fusion), channel_id=1, source_target_pairs={{0,4},{1,5},{2,6},{3,7},{4,8},{5,9},{6,10},{7,11},{8,12},{9,13},{1... | collective-permute-start | bytes 3145736 | tf_op jit(solution)/shard_map/ppermute | solution.py:11
  13.2 96.2 %collective-permute-start.1 = (bf16[256,2048]{1,0:T(8,128)(2,1)S(1)}, bf16[256,2048]{1,0:T(8,128)(2,1)S(1)}, u32[]{:S(2)}, u32[]{:S(2)}) collective-permute-start(bf16[256,2048]{1,0:T(8,128)(2,1)S(1)} %multiply_convert_fusion), channel_id=1, source_target_pairs={{0,2},{1,3},{2,4},{3,5},{4,6},{5,7},{6,8},{7,9},{8,10},{9,11},{10,... | collective-permute-start | bytes 3145736 | tf_op jit(solution)/shard_map/ppermute | solution.py:11
  14.8 105.7 %collective-permute-start = (bf16[256,2048]{1,0:T(8,128)(2,1)S(1)}, bf16[256,2048]{1,0:T(8,128)(2,1)S(1)}, u32[]{:S(2)}, u32[]{:S(2)}) collective-permute-start(bf16[256,2048]{1,0:T(8,128)(2,1)S(1)} %multiply_convert_fusion), channel_id=1, source_target_pairs={{0,1},{1,2},{2,3},{3,4},{4,5},{5,6},{6,7},{7,8},{8,9},{9,10},{10,1... | collective-permute-start | bytes 3145736 | tf_op jit(solution)/shard_map/ppermute | solution.py:11
  16.0 104.4 %copy-start = (f32[257,256]{1,0:T(8,128)}, f32[257,256]{1,0:T(8,128)S(1)}, u32[]{:S(2)}) copy-start(f32[257,256]{1,0:T(8,128)S(1)} %get-tuple-element.30) | copy-start | bytes 789508
  124.4 18.3 %slice-start.2 = ((s8[4259840]{0:T(1024)(128)(4,1)}), s8[4194304]{0:T(1024)(128)(4,1)S(1)}, s32[]{:S(2)}) async-start(s8[4259840]{0:T(1024)(128)(4,1)} %bitcast.7), calls=%async_computation.3 | async-start | bytes 8388608
  124.4 18.3 %slice-start.4 = ((s8[4259840]{0:T(1024)(128)(4,1)}), s8[4194304]{0:T(1024)(128)(4,1)S(1)}, s32[]{:S(2)}) async-start(s8[4259840]{0:T(1024)(128)(4,1)} %bitcast.9), calls=%async_computation.5 | async-start | bytes 8388608
  127.7 15.0 %slice-start.3 = ((s8[4259840]{0:T(1024)(128)(4,1)}), s8[65536]{0:T(1024)(128)(4,1)S(1)}, s32[]{:S(2)}) async-start(s8[4259840]{0:T(1024)(128)(4,1)} %bitcast.7), calls=%async_computation.4 | async-start | bytes 131072
  127.7 15.0 %slice-start.5 = ((s8[4259840]{0:T(1024)(128)(4,1)}), s8[65536]{0:T(1024)(128)(4,1)S(1)}, s32[]{:S(2)}) async-start(s8[4259840]{0:T(1024)(128)(4,1)} %bitcast.9), calls=%async_computation.6 | async-start | bytes 131072
  137.4 18.7 %slice-start = ((s8[4259840]{0:T(1024)(128)(4,1)}), s8[4194304]{0:T(1024)(128)(4,1)S(1)}, s32[]{:S(2)}) async-start(s8[4259840]{0:T(1024)(128)(4,1)} %bitcast.5), calls=%async_computation.1 | async-start | bytes 8388608
  142.7 13.4 %slice-start.1 = ((s8[4259840]{0:T(1024)(128)(4,1)}), s8[65536]{0:T(1024)(128)(4,1)S(1)}, s32[]{:S(2)}) async-start(s8[4259840]{0:T(1024)(128)(4,1)} %bitcast.5), calls=%async_computation.2 | async-start | bytes 131072
  150.8 16.6 %slice-start.6 = ((s8[4259840]{0:T(1024)(128)(4,1)}), s8[4194304]{0:T(1024)(128)(4,1)S(1)}, s32[]{:S(2)}) async-start(s8[4259840]{0:T(1024)(128)(4,1)} %bitcast.11), calls=%async_computation.7 | async-start | bytes 8388608
  156.1 11.3 %slice-start.7 = ((s8[4259840]{0:T(1024)(128)(4,1)}), s8[65536]{0:T(1024)(128)(4,1)S(1)}, s32[]{:S(2)}) async-start(s8[4259840]{0:T(1024)(128)(4,1)} %bitcast.11), calls=%async_computation.8 | async-start | bytes 131072
  173.5 10.6 %copy-start.2 = (bf16[256,2048]{1,0:T(8,128)(2,1)S(1)}, bf16[256,2048]{1,0:T(8,128)(2,1)}, u32[]{:S(2)}) copy-start(bf16[256,2048]{1,0:T(8,128)(2,1)} %copy-done.1) | copy-start | bytes 3145732
  173.5 10.6 %copy-start.3 = (f32[257,2048]{1,0:T(8,128)S(1)}, f32[257,2048]{1,0:T(8,128)}, u32[]{:S(2)}) copy-start(f32[257,2048]{1,0:T(8,128)} %get-tuple-element.5) | copy-start | bytes 6316036
  173.5 10.6 %copy-start.4 = (f32[257,2048]{1,0:T(8,128)S(1)}, f32[257,2048]{1,0:T(8,128)}, u32[]{:S(2)}) copy-start(f32[257,2048]{1,0:T(8,128)} %get-tuple-element.6) | copy-start | bytes 6316036
  173.5 10.7 %copy-start.5 = (f32[257,2048]{1,0:T(8,128)S(1)}, f32[257,2048]{1,0:T(8,128)}, u32[]{:S(2)}) copy-start(f32[257,2048]{1,0:T(8,128)} %get-tuple-element.7) | copy-start | bytes 6316036
  173.5 10.7 %copy-start.6 = (f32[257,2048]{1,0:T(8,128)S(1)}, f32[257,2048]{1,0:T(8,128)}, u32[]{:S(2)}) copy-start(f32[257,2048]{1,0:T(8,128)} %get-tuple-element.8) | copy-start | bytes 6316036
  173.5 10.7 %copy-start.7 = (f32[257,2048]{1,0:T(8,128)S(1)}, f32[257,2048]{1,0:T(8,128)}, u32[]{:S(2)}) copy-start(f32[257,2048]{1,0:T(8,128)} %get-tuple-element.9) | copy-start | bytes 6316036
  173.5 10.7 %copy-start.8 = (f32[257,2048]{1,0:T(8,128)S(1)}, f32[257,2048]{1,0:T(8,128)}, u32[]{:S(2)}) copy-start(f32[257,2048]{1,0:T(8,128)} %get-tuple-element.10) | copy-start | bytes 6316036
  173.5 10.9 %copy-start.9 = (f32[257,2048]{1,0:T(8,128)S(1)}, f32[257,2048]{1,0:T(8,128)}, u32[]{:S(2)}) copy-start(f32[257,2048]{1,0:T(8,128)} %get-tuple-element.11) | copy-start | bytes 6316036
  173.5 11.5 %copy-start.10 = (f32[257,2048]{1,0:T(8,128)S(1)}, f32[257,2048]{1,0:T(8,128)}, u32[]{:S(2)}) copy-start(f32[257,2048]{1,0:T(8,128)} %get-tuple-element.12) | copy-start | bytes 6316036
  173.5 11.5 %copy-start.11 = (f32[2048]{0:T(1024)S(1)}, f32[2048]{0:T(1024)}, u32[]{:S(2)}) copy-start(f32[2048]{0:T(1024)} %param.9) | copy-start | bytes 24580
Sparse Core Ops, SparseCore 0:
  9.5 66.9 all-gather.1
where the time goes:
time: 201 us
  waiting for transfers between devices  85.7 us (43%)
  matrix products  55.8 us (28%)
  other arithmetic  39 us (19%)
  between operations  13.6 us (7%)
  starting transfers between devices  5.73 us (3%)
    ppermute x4, waiting for transfers between devices, shifted(): lax.ppermute(value, axis, [(i, (i + by) % length) for i in range(length)])  85 us
    dot_general x9, matrix products, spectrum(): jnp.dot(table, block.astype(jnp.float32), precision=lax.Precision.HIGHEST)  36.3 us
    sub x4, other arithmetic, complex_product(): real_part = first_real * second_real - first_imag * second_imag  32 us
    dot_general x1, matrix products, on_device(): jnp.dot(backward[:rows], current_sum, precision=lax.Precision.HIGHEST)  10.5 us
    dot_general x1, matrix products, on_device(): jnp.dot(backward[rows:], previous_sum, precision=lax.Precision.HIGHEST)  9 us
    ppermute x4, starting transfers between devices, shifted(): lax.ppermute(value, axis, [(i, (i + by) % length) for i in range(length)])  5.73 us
  transfers between devices with their start and end apart: 5, of which 4 were waited for; matrix products, arithmetic and copies ran while one was open for 13% of the time, Pallas kernels for 0%

commit v1 on v0

v1 whole, which is shorter than its diff:
```python
import functools

import jax
import jax.numpy as jnp
import ml_dtypes
import numpy as np
from jax import lax
from jax.experimental import pallas as pl
from jax.experimental.pallas import tpu as pltpu
from jax.sharding import PartitionSpec as P

LANES = 128
BF16 = jnp.bfloat16
F32 = jnp.float32


def two_parts(table):
    high = table.astype(ml_dtypes.bfloat16)
    low = (table - high.astype(np.float64)).astype(ml_dtypes.bfloat16)
    return high, low


def bin_order(rows):
    return np.concatenate([np.arange(0, rows, 2), np.arange(1, rows, 2)])


def forward_tables(rows):
    bins = bin_order(rows)[:, None] + 0.5
    angle = bins * np.arange(rows)[None, :] * (np.pi / rows)
    return two_parts(np.concatenate([np.cos(angle), -np.sin(angle)], axis=0))


def inverse_tables(rows):
    bins = bin_order(rows)[None, :] + 0.5
    angle = bins * (np.arange(rows)[:, None] + rows) * (np.pi / rows)
    return two_parts(np.concatenate([np.cos(angle), -np.sin(angle)], axis=1) / rows)


def matmul(a, b):
    return jnp.dot(a, b, preferred_element_type=F32)


def scalar_spec():
    return pl.BlockSpec(memory_space=pltpu.SMEM)


def params():
    return pltpu.CompilerParams(vmem_limit_bytes=56 << 20)


def product_kernel(layers, members, where_ref, gate_ref, values_ref, *piece_refs):
    member = where_ref[0]
    for apart in range(members):
        held = member ^ apart
        for layer in range(layers):
            lanes = pl.ds(pl.multiple_of((layer * members + held) * LANES, LANES), LANES)
            gated = gate_ref[:, lanes].astype(F32) * values_ref[:, lanes].astype(F32)
            piece_refs[apart][:, layer * LANES : (layer + 1) * LANES] = gated.astype(BF16)


def product_pieces(where, gate_in, values, layers, members):
    rows, channels = values.shape
    width = channels // (layers * members)
    held = channels // members
    if width != LANES:
        product = (gate_in.astype(F32) * values.astype(F32)).astype(BF16)
        product = product.reshape(rows, layers, members, width).transpose(2, 0, 1, 3)
        product = product.reshape(members, rows, held)
        return [lax.dynamic_index_in_dim(product, where[0] ^ d, 0, False) for d in range(members)]
    step = rows // 4
    return pl.pallas_call(
        functools.partial(product_kernel, layers, members),
        grid=(4,),
        in_specs=[scalar_spec()] + [pl.BlockSpec((step, channels), lambda r: (r, 0))] * 2,
        out_specs=[pl.BlockSpec((step, held), lambda r: (r, 0))] * members,
        out_shape=[jax.ShapeDtypeStruct((rows, held), BF16)] * members,
        compiler_params=params(),
        cost_estimate=pl.CostEstimate(
            flops=rows * channels, bytes_accessed=rows * channels * 6, transcendentals=0
        ),
    )(where, gate_in, values)


def taps_kernel(layers, where_ref, high_ref, low_ref, own_ref, *refs):
    count = layers - 1
    near_refs, far_refs, (out_ref, taps) = refs[:count], refs[count : 2 * count], refs[2 * count :]
    layer, group = where_ref[1], where_ref[2]
    rows = high_ref.shape[1]
    half = near_refs[0].shape[0]
    near = pl.ds(pl.multiple_of(group * half, half), half)
    far = pl.ds(pl.multiple_of((1 - group) * half, half), half)
    taps[:, pl.ds(pl.multiple_of(layer * LANES, LANES), LANES)] = own_ref[...]
    for apart in range(1, layers):
        source = lax.rem(layer + layers - apart, layers)
        lanes = pl.ds(pl.multiple_of(source * LANES, LANES), LANES)
        taps[near, lanes] = near_refs[apart - 1][...]
        taps[far, lanes] = far_refs[apart - 1][...]
    for lag in range(out_ref.shape[0]):
        block = taps[lag * rows : (lag + 1) * rows]
        out_ref[lag] = matmul(high_ref[...], block) + matmul(low_ref[...], block)


def plain_taps_kernel(high_ref, low_ref, taps_ref, out_ref):
    rows = high_ref.shape[1]
    for lag in range(out_ref.shape[0]):
        block = taps_ref[lag * rows : (lag + 1) * rows]
        out_ref[lag] = matmul(high_ref[...], block) + matmul(low_ref[...], block)


def own_kernel(members, where_ref, high_ref, low_ref, *refs):
    block_refs, out_ref = refs[:members], refs[members]
    member = where_ref[0]
    for apart in range(members):
        block = block_refs[apart][...]
        out_ref[member ^ apart] = matmul(high_ref[...], block) + matmul(low_ref[...], block)


def own_spectra(where, tables, blocks):
    members = len(blocks)
    rows, held = blocks[0].shape
    chunk = min(256, held)
    whole = pl.BlockSpec((2 * rows, rows), lambda c: (0, 0))
    return pl.pallas_call(
        functools.partial(own_kernel, members),
        grid=(held // chunk,),
        in_specs=[scalar_spec(), whole, whole]
        + [pl.BlockSpec((rows, chunk), lambda c: (0, c))] * members,
        out_specs=pl.BlockSpec((members, 2 * rows, chunk), lambda c: (0, 0, c)),
        out_shape=jax.ShapeDtypeStruct((members, 2 * rows, held), F32),
        compiler_params=params(),
        cost_estimate=pl.CostEstimate(
            flops=members * 8 * rows * rows * held,
            bytes_accessed=members * rows * held * 10,
            transcendentals=0,
        ),
    )(where, *tables, *blocks)


def mix_kernel(
    members, where_ref, high_ref, low_ref, back_high_ref, back_low_ref, skip_ref, taps_ref, own_ref, *refs
):
    halo_refs, block_refs = refs[:members], refs[members : 2 * members]
    out_refs, (halo, sums) = refs[2 * members : 3 * members], refs[3 * members :]
    member = where_ref[0]
    rows = high_ref.shape[1]
    for apart in range(members):
        block = halo_refs[apart][...]
        halo[member ^ apart] = matmul(high_ref[...], block) + matmul(low_ref[...], block)

    def spectrum(position, at):
        source = halo if position < 0 else own_ref
        return source[position % members, pl.ds(at, 8), :], source[position % members, pl.ds(at + rows, 8), :]

    def one(at, sign):
        blocks = [spectrum(position, at) for position in range(-members, members)]
        windows = []
        for (before_real, before_imag), (real, imag) in zip(blocks, blocks[1:]):
            if sign > 0:
                windows.append((before_real + imag, before_imag - real))
            else:
                windows.append((before_real - imag, before_imag + real))
        taps = [
            (taps_ref[lag, pl.ds(at, 8), :], taps_ref[lag, pl.ds(at + rows, 8), :])
            for lag in range(members)
        ]
        for output in range(members):
            real_sum, imag_sum = None, None
            for lag in range(members):
                real, imag = windows[members - 1 + output - lag]
                tap_real, tap_imag = taps[lag]
                real_part = tap_real * real - tap_imag * imag
                imag_part = tap_real * imag + tap_imag * real
                real_sum = real_part if real_sum is None else real_sum + real_part
                imag_sum = imag_part if imag_sum is None else imag_sum + imag_part
            sums[output, pl.ds(at, 8), :] = real_sum
            sums[output, pl.ds(at + rows, 8), :] = imag_sum

    count = rows // 16

    @pl.loop(0, count)
    def _(step):
        one(pl.multiple_of(step * 8, 8), 1)

    @pl.loop(count, 2 * count)
    def _(step):
        one(pl.multiple_of(step * 8, 8), -1)

    for apart in range(members):
        total = sums[member ^ apart]
        high = total.astype(BF16)
        low = (total - high.astype(F32)).astype(BF16)
        convolved = matmul(back_high_ref[...], high) + (
            matmul(back_high_ref[...], low) + matmul(back_low_ref[...], high)
        )
        mixed = convolved + skip_ref[...] * block_refs[apart][...].astype(F32)
        out_refs[apart][...] = mixed.astype(BF16)


def mixed_pieces(where, tables, back_tables, skip, taps, own, halo, blocks):
    members = len(blocks)
    rows, held = blocks[0].shape
    chunk = min(256, held)
    forward = pl.BlockSpec((2 * rows, rows), lambda c: (0, 0))
    backward = pl.BlockSpec((rows, 2 * rows), lambda c: (0, 0))
    spectra = pl.BlockSpec((members, 2 * rows, chunk), lambda c: (0, 0, c))
    piece = pl.BlockSpec((rows, chunk), lambda c: (0, c))
    return pl.pallas_call(
        functools.partial(mix_kernel, members),
        grid=(held // chunk,),
        in_specs=[scalar_spec(), forward, forward, backward, backward]
        + [pl.BlockSpec((1, chunk), lambda c: (0, c)), spectra, spectra]
        + [piece] * (2 * members),
        out_specs=[piece] * members,
        out_shape=[jax.ShapeDtypeStruct((rows, held), BF16)] * members,
        scratch_shapes=[pltpu.VMEM((members, 2 * rows, chunk), F32)] * 2,
        compiler_params=params(),
        cost_estimate=pl.CostEstimate(
            flops=members * 20 * rows * rows * held,
            bytes_accessed=members * rows * held * 22,
            transcendentals=0,
        ),
    )(where, *tables, *back_tables, skip, taps, own, *halo, *blocks)


def gate_kernel(layers, members, where_ref, gate_ref, *refs):
    piece_refs, out_ref = refs[:members], refs[members]
    member = where_ref[0]
    for apart in range(members):
        held = member ^ apart
        for layer in range(layers):
            lanes = pl.ds(pl.multiple_of((layer * members + held) * LANES, LANES), LANES)
            mixed = piece_refs[apart][:, layer * LANES : (layer + 1) * LANES].astype(F32)
            out_ref[:, lanes] = (gate_ref[:, lanes].astype(F32) * mixed).astype(BF16)


def gated_output(where, gate_out, pieces, layers, members):
    rows, channels = gate_out.shape
    held = channels // members
    width = held // layers
    if width != LANES:
        stacked = jnp.stack(pieces)
        stacked = jnp.stack(
            [lax.dynamic_index_in_dim(stacked, where[0] ^ d, 0, False) for d in range(members)]
        )
        mixed = stacked.reshape(members, rows, layers, width).transpose(1, 2, 0, 3)
        mixed = mixed.reshape(rows, channels).astype(F32)
        return (gate_out.astype(F32) * mixed).astype(BF16)
    step = rows // 4
    return pl.pallas_call(
        functools.partial(gate_kernel, layers, members),
        grid=(4,),
        in_specs=[scalar_spec(), pl.BlockSpec((step, channels), lambda r: (r, 0))]
        + [pl.BlockSpec((step, held), lambda r: (r, 0))] * members,
        out_specs=pl.BlockSpec((step, channels), lambda r: (r, 0)),
        out_shape=jax.ShapeDtypeStruct((rows, channels), BF16),
        compiler_params=params(),
    )(where, gate_out, *pieces)


def tap_spectra(where, tables, filter_taps, layers, members, groups):
    count, width = filter_taps.shape
    rows = tables[0].shape[1]
    held = width * layers
    length = layers * members
    out_shape = jax.ShapeDtypeStruct((count // rows, 2 * rows, held), F32)
    cost = pl.CostEstimate(
        flops=8 * count * rows * held, bytes_accessed=count * held * 10, transcendentals=0
    )
    if width != LANES or groups != 2:
        ring = [[layer * members + member for layer in range(layers)] for member in range(members)]
        taps = lax.all_gather(filter_taps, "ctx", axis=1, tiled=True, axis_index_groups=ring)
        return pl.pallas_call(
            plain_taps_kernel, out_shape=out_shape, compiler_params=params(), cost_estimate=cost
        )(*tables, taps)
    half = lax.dynamic_slice_in_dim(filter_taps, where[2] * (count // 2), count // 2, 0)
    near = [
        lax.ppermute(half, "ctx", [(i, (i + apart * members) % length) for i in range(length)])
        for apart in range(1, layers)
    ]
    far = [lax.ppermute(part, "groups", [(0, 1), (1, 0)]) for part in near]
    return pl.pallas_call(
        functools.partial(taps_kernel, layers),
        in_specs=[scalar_spec()] + [pl.BlockSpec(memory_space=pltpu.VMEM)] * (2 * layers + 1),
        out_specs=pl.BlockSpec(memory_space=pltpu.VMEM),
        out_shape=out_shape,
        scratch_shapes=[pltpu.VMEM((count, held), BF16)],
        compiler_params=params(),
        cost_estimate=cost,
    )(where, *tables, filter_taps, *near, *far)


def on_device(gate_out, gate_in, values, filter_taps, skip_gain):
    rows, channels = values.shape
    length = lax.axis_size("ctx")
    members = filter_taps.shape[0] // rows
    layers = length // members
    width = channels // length
    index = lax.axis_index("ctx")
    where = jnp.stack([index % members, index // members, lax.axis_index("groups")]).astype(jnp.int32)
    tables = [jnp.asarray(t) for t in forward_tables(rows)]
    back_tables = [jnp.asarray(t) for t in inverse_tables(rows)]

    def to_member(value, apart, ahead):
        pairs = [
            (i, (i // members + ahead) % layers * members + (i % members ^ apart))
            for i in range(length)
        ]
        return lax.ppermute(value, "ctx", pairs)

    pieces = product_pieces(where, gate_in, values, layers, members)
    halo = [to_member(pieces[d], d, 1) for d in range(members)]
    blocks = [pieces[0]] + [to_member(pieces[d], d, 0) for d in range(1, members)]
    taps = tap_spectra(where, tables, filter_taps, layers, members, lax.axis_size("groups"))
    own = own_spectra(where, tables, blocks)
    skip = skip_gain.reshape(layers, members, width)
    skip = lax.dynamic_index_in_dim(skip, where[0], 1, False).reshape(1, layers * width)
    mixed = mixed_pieces(where, tables, back_tables, skip, taps, own, halo, blocks)
    mixed = [mixed[0]] + [to_member(mixed[d], d, 0) for d in range(1, members)]
    return gated_output(where, gate_out, mixed, layers, members)


def solution(mesh):
    in_specs = (
        P(("groups", "ctx"), None),
        P(("groups", "ctx"), None),
        P(("groups", "ctx"), None),
        P(None, "ctx"),
        P(),
    )
    out_specs = P(("groups", "ctx"), None)
    return jax.shard_map(
        on_device, mesh=mesh, in_specs=in_specs, out_specs=out_specs, check_vma=False
    )
```

time: 201 us -> 79.4 us (0.40)
  waiting for transfers between devices: 85.7 us -> 29 us
  matrix products: 55.8 us -> 0 us
  other arithmetic: 39 us -> 0.6 us
  Pallas kernels: 0 us -> 27.8 us
  between operations: 13.6 us -> 0.13 us
  starting transfers between devices: 5.73 us -> 17.7 us
  local copies, waits for them, and re-layouts: 0.93 us -> 3.64 us
    ppermute x4 -> x16, waiting for transfers between devices: 85 us -> 29 us  [the longest x10 20.8 us: to_member(): return lax.ppermute(value, 'ctx', pairs)]
    dot_general x11 -> x0, matrix products: 55.8 us -> none  [the longest x9 36.3 us: spectrum(): jnp.dot(table, block.astype(jnp.float32), precision=lax.Precision.HIGHEST)]
    sub x4 -> x0, other arithmetic: 32 us -> none  [complex_product(): real_part = first_real * second_real - first_imag * second_imag]
    pallas_call x0 -> x5, Pallas kernels: none -> 27.8 us  [the longest x1 11 us: mixed_pieces(): pl.pallas_call(functools.partial(mix_kernel, members), grid=(held // chun...]
    ppermute x4 -> x16, starting transfers between devices: 5.73 us -> 17.7 us  [the longest x10 8.08 us: to_member(): return lax.ppermute(value, 'ctx', pairs)]
    mul x1 -> x0, other arithmetic: 4 us -> none  [inverse_table(): -weight * jnp.sin(angle)]
  transfers between devices with their start and end apart: 5 -> 16, of which waited for: 4 -> 7; matrix products, arithmetic and copies ran while one was open for 13% -> 1% of each run, Pallas kernels for 0% -> 17%
where the time goes in v1:
time: 79.4 us; the launch traced here: 78.9 us
  waiting for transfers between devices  29 us (37%)
  Pallas kernels  27.8 us (35%)
  starting transfers between devices  17.7 us (22%)
  local copies, waits for them, and re-layouts  3.64 us (5%)
    ppermute x10, waiting for transfers between devices, to_member(): return lax.ppermute(value, 'ctx', pairs)  20.8 us
    pallas_call x1, Pallas kernels, mixed_pieces(): pl.pallas_call(functools.partial(mix_kernel, members), grid=(held // chun...  11 us
    ppermute x10, starting transfers between devices, to_member(): return lax.ppermute(value, 'ctx', pairs)  8.08 us
    ppermute x3, starting transfers between devices, tap_spectra(): lax.ppermute(half, 'ctx', [(i, (i + apart * members) % length) for i in r...  6.11 us
    ppermute x3, waiting for transfers between devices, tap_spectra(): far = [lax.ppermute(part, 'groups', [(0, 1), (1, 0)]) for part in near]  5.51 us
    pallas_call x1, Pallas kernels, tap_spectra(): pl.pallas_call(functools.partial(taps_kernel, layers), in_specs=[scalar_s...  4.82 us
    pallas_call x1, Pallas kernels, own_spectra(): pl.pallas_call(functools.partial(own_kernel, members), grid=(held // chun...  4.43 us
    pallas_call x1, Pallas kernels, product_pieces(): pl.pallas_call(functools.partial(product_kernel, layers, members), grid=(...  3.79 us
  transfers between devices with their start and end apart: 16, of which 7 were waited for; matrix products, arithmetic and copies ran while one was open for 1% of the time, Pallas kernels for 17%

profile of v1, /device:TPU:0, one launch (start us, length us, event | category | flops | bytes accessed | tf_op | source)
XLA Modules:
  0.0 78.9 jit_solution(11852332667658548909)
XLA Ops:
  0.0 0.9 %constant_dynamic-slice_fusion = bf16[512,128]{1,0:T(8,128)(2,1)S(1)} fusion(bf16[1024,128]{1,0:T(8,128)(2,1)} %own_ref.1, s32[]{:T(128)S(6)} %select_n.21), kind=kLoop, calls=%fused_computation.2 | loop fusion | bytes 262148 | tf_op jit(solution)/shard_map/dynamic_slice | solution.py:275
  0.9 5.1 %collective-permute-start.2 = (bf16[512,128]{1,0:T(8,128)(2,1)S(1)}, bf16[512,128]{1,0:T(8,128)(2,1)S(1)}, u32[]{:S(2)}, u32[]{:S(2)}) collective-permute-start(bf16[512,128]{1,0:T(8,128)(2,1)S(1)} %constant_dynamic-slice_fusion), channel_id=1, source_target_pairs={{0,12},{1,13},{2,14},{3,15},{4,0},{5,1},{6,2},{7,3},{8,4},{9,5},{1... | collective-permute-start | bytes 393224 | tf_op jit(solution)/shard_map/ppermute | solution.py:277
  6.0 0.0 collective-permute-start.1
  6.0 1.0 %collective-permute-start = (bf16[512,128]{1,0:T(8,128)(2,1)S(1)}, bf16[512,128]{1,0:T(8,128)(2,1)S(1)}, u32[]{:S(2)}, u32[]{:S(2)}) collective-permute-start(bf16[512,128]{1,0:T(8,128)(2,1)S(1)} %constant_dynamic-slice_fusion), channel_id=1, source_target_pairs={{0,4},{1,5},{2,6},{3,7},{4,8},{5,9},{6,10},{7,11},{8,12},{9,13},{1... | collective-permute-start | bytes 393224 | tf_op jit(solution)/shard_map/ppermute | solution.py:277
  7.0 0.6 pad_add_fusion.where_ref
  7.7 3.8 %shard_map.92 = (bf16[256,512]{1,0:T(8,128)(2,1)}, bf16[256,512]{1,0:T(8,128)(2,1)}, bf16[256,512]{1,0:T(8,128)(2,1)}, bf16[256,512]{1,0:T(8,128)(2,1)}) custom-call(s32[3]{0:T(128)} %pad_add_fusion.where_ref, bf16[256,2048]{1,0:T(8,128)(2,1)} %gate_ref.2, bf16[256,2048]{1,0:T(8,128)(2,1)} %values_ref.1), custom_call_target="tpu_custom_call" | custom-call | flops 524288 | bytes 3145728 | tf_op jit(solution)/shard_map/pallas_call | solution.py:71
  11.4 0.0 collective-permute-start.6
  11.5 1.6 %collective-permute-start.7 = (bf16[256,512]{1,0:T(8,128)(2,1)}, bf16[256,512]{1,0:T(8,128)(2,1)S(1)}, u32[]{:S(2)}, u32[]{:S(2)}) collective-permute-start(bf16[256,512]{1,0:T(8,128)(2,1)} %get-tuple-element.15), channel_id=1, source_target_pairs={{0,2},{1,3},{2,0},{3,1},{4,6},{5,7},{6,4},{7,5},{8,10},{9,11},{10,... | collective-permute-start | bytes 786440 | tf_op jit(solution)/shard_map/ppermute | solution.py:308
  13.1 1.5 %collective-permute-start.5 = (bf16[512,128]{1,0:T(8,128)(2,1)S(1)}, bf16[512,128]{1,0:T(8,128)(2,1)S(1)}, u32[]{:S(2)}, u32[]{:S(2)}) collective-permute-start(bf16[512,128]{1,0:T(8,128)(2,1)S(1)} %collective-permute-done.2.refs_2_), channel_id=1, source_target_pairs={{0,16},{16,0},{1,17},{17,1},{2,18},{18,2},{3,19},{19,3},{4,20},{20... | collective-permute-start | bytes 393224 | tf_op jit(solution)/shard_map/ppermute | solution.py:280
  14.6 2.7 %collective-permute-done.1.refs_1_ = bf16[512,128]{1,0:T(8,128)(2,1)S(1)} collective-permute-done((bf16[512,128]{1,0:T(8,128)(2,1)S(1)}, bf16[512,128]{1,0:T(8,128)(2,1)S(1)}, u32[]{:S(2)}, u32[]{:S(2)}) %collective-permute-start.1) | collective-permute-done | bytes 131104 | tf_op jit(solution)/shard_map/ppermute | solution.py:277
  17.2 1.5 %collective-permute-start.4 = (bf16[512,128]{1,0:T(8,128)(2,1)S(1)}, bf16[512,128]{1,0:T(8,128)(2,1)S(1)}, u32[]{:S(2)}, u32[]{:S(2)}) collective-permute-start(bf16[512,128]{1,0:T(8,128)(2,1)S(1)} %collective-permute-done.1.refs_1_), channel_id=1, source_target_pairs={{0,16},{16,0},{1,17},{17,1},{2,18},{18,2},{3,19},{19,3},{4,20},{20... | collective-permute-start | bytes 393224 | tf_op jit(solution)/shard_map/ppermute | solution.py:280
  18.7 0.5 collective-permute-start.3
  19.3 4.1 %collective-permute-done.4.refs_4_ = bf16[512,128]{1,0:T(8,128)(2,1)S(1)} collective-permute-done((bf16[512,128]{1,0:T(8,128)(2,1)S(1)}, bf16[512,128]{1,0:T(8,128)(2,1)S(1)}, u32[]{:S(2)}, u32[]{:S(2)}) %collective-permute-start.4) | collective-permute-done | bytes 131104 | tf_op jit(solution)/shard_map/ppermute | solution.py:280
  23.4 1.4 %collective-permute-done.3.refs_3_ = bf16[512,128]{1,0:T(8,128)(2,1)S(1)} collective-permute-done((bf16[512,128]{1,0:T(8,128)(2,1)S(1)}, bf16[512,128]{1,0:T(8,128)(2,1)S(1)}, u32[]{:S(2)}, u32[]{:S(2)}) %collective-permute-start.3) | collective-permute-done | bytes 131104 | tf_op jit(solution)/shard_map/ppermute | solution.py:280
  24.8 1.9 %collective-permute-start.11 = (bf16[256,512]{1,0:T(8,128)(2,1)}, bf16[256,512]{1,0:T(8,128)(2,1)S(1)}, u32[]{:S(2)}, u32[]{:S(2)}) collective-permute-start(bf16[256,512]{1,0:T(8,128)(2,1)} %get-tuple-element.15), channel_id=1, source_target_pairs={{0,6},{1,7},{2,4},{3,5},{4,10},{5,11},{6,8},{7,9},{8,14},{9,15},{1... | collective-permute-start | bytes 786440 | tf_op jit(solution)/shard_map/ppermute | solution.py:308
  26.7 0.1 collective-permute-start.12
  26.8 1.9 %collective-permute-start.9 = (bf16[256,512]{1,0:T(8,128)(2,1)}, bf16[256,512]{1,0:T(8,128)(2,1)S(1)}, u32[]{:S(2)}, u32[]{:S(2)}) collective-permute-start(bf16[256,512]{1,0:T(8,128)(2,1)} %get-tuple-element.13.refs_0_.refs_4_), channel_id=1, source_target_pairs={{0,4},{1,5},{2,6},{3,7},{4,8},{5,9},{6,10},{7,11},{8,12},{9,13},{1... | collective-permute-start | bytes 786440 | tf_op jit(solution)/shard_map/ppermute | solution.py:308
  28.7 0.5 dynamic-slice_bitcast_fusion.skip_ref
  29.3 4.8 %shard_map.91.taps_ref = f32[4,512,512]{2,1,0:T(8,128)} custom-call(s32[3]{0:T(128)} %pad_add_fusion.where_ref, bf16[512,256]{1,0:T(8,128)(2,1)} %constant.52.clone.high_ref, bf16[512,256]{1,0:T(8,128)(2,1)} %constant.53.clone.low_ref, bf16[1024,128]{1,0:T(8,128)(2,1)} %own_ref.1, bf16[512,128]{1,0:T(8,128)(2,1)} %copy-done.13, bf16[512,128]{1,0:T(8,128)(2,1)} %copy-done.12, ...), custom_call_target="tpu_custom_call" | custom-call | flops 1073741824 | bytes 5242880 | tf_op jit(solution)/shard_map/pallas_call | solution.py:281
  34.1 0.7 copy-done.3
  34.8 4.4 %shard_map.93.own_ref = f32[4,512,512]{2,1,0:T(8,128)} custom-call(s32[3]{0:T(128)} %pad_add_fusion.where_ref, bf16[512,256]{1,0:T(8,128)(2,1)} %constant.52.clone.high_ref, bf16[512,256]{1,0:T(8,128)(2,1)} %constant.53.clone.low_ref, bf16[256,512]{1,0:T(8,128)(2,1)} %get-tuple-element.13.refs_0_.refs_4_, bf16[256,512]{1,0:T(8,128)(2,1)} %copy-done.1, ...), custom_call_target="tpu_custom_call" | custom-call | flops 1073741824 | bytes 5242880 | tf_op jit(solution)/shard_map/pallas_call | solution.py:123
  39.3 6.5 %collective-permute-done.12.refs_3_ = bf16[256,512]{1,0:T(8,128)(2,1)S(1)} collective-permute-done((bf16[256,512]{1,0:T(8,128)(2,1)}, bf16[256,512]{1,0:T(8,128)(2,1)S(1)}, u32[]{:S(2)}, u32[]{:S(2)}) %collective-permute-start.12) | collective-permute-done | bytes 262176 | tf_op jit(solution)/shard_map/ppermute | solution.py:308
  45.8 2.4 %collective-permute-done.9.refs_0_ = bf16[256,512]{1,0:T(8,128)(2,1)S(1)} collective-permute-done((bf16[256,512]{1,0:T(8,128)(2,1)}, bf16[256,512]{1,0:T(8,128)(2,1)S(1)}, u32[]{:S(2)}, u32[]{:S(2)}) %collective-permute-start.9) | collective-permute-done | bytes 262176 | tf_op jit(solution)/shard_map/ppermute | solution.py:308
  48.3 0.7 copy-done.7
  49.0 11.0 %shard_map.94 = (bf16[256,512]{1,0:T(8,128)(2,1)}, bf16[256,512]{1,0:T(8,128)(2,1)}, bf16[256,512]{1,0:T(8,128)(2,1)}, bf16[256,512]{1,0:T(8,128)(2,1)}) custom-call(s32[3]{0:T(128)} %pad_add_fusion.where_ref, bf16[512,256]{1,0:T(8,128)(2,1)} %constant.52.clone.high_ref, bf16[512,256]{1,0:T(8,128)(2,1)} %constant.53.clone.low_ref, ...), custom_call_target="tpu_custom_call" | custom-call | flops 2684354560 | bytes 11534336 | tf_op jit(solution)/shard_map/pallas_call | solution.py:207
  60.0 1.1 %collective-permute-start.13 = (bf16[256,512]{1,0:T(8,128)(2,1)}, bf16[256,512]{1,0:T(8,128)(2,1)S(1)}, u32[]{:S(2)}, u32[]{:S(2)}) collective-permute-start(bf16[256,512]{1,0:T(8,128)(2,1)} %get-tuple-element.18), channel_id=1, source_target_pairs={{0,1},{1,0},{2,3},{3,2},{4,5},{5,4},{6,7},{7,6},{8,9},{9,8},{10,11... | collective-permute-start | bytes 786440 | tf_op jit(solution)/shard_map/ppermute | solution.py:308
  61.2 0.9 %collective-permute-start.14 = (bf16[256,512]{1,0:T(8,128)(2,1)}, bf16[256,512]{1,0:T(8,128)(2,1)S(1)}, u32[]{:S(2)}, u32[]{:S(2)}) collective-permute-start(bf16[256,512]{1,0:T(8,128)(2,1)} %get-tuple-element.19), channel_id=1, source_target_pairs={{0,2},{1,3},{2,0},{3,1},{4,6},{5,7},{6,4},{7,5},{8,10},{9,11},{10,... | collective-permute-start | bytes 786440 | tf_op jit(solution)/shard_map/ppermute | solution.py:308
  62.1 0.5 collective-permute-start.15
  62.6 7.9 %collective-permute-done.14.refs_2_ = bf16[256,512]{1,0:T(8,128)(2,1)S(1)} collective-permute-done((bf16[256,512]{1,0:T(8,128)(2,1)}, bf16[256,512]{1,0:T(8,128)(2,1)S(1)}, u32[]{:S(2)}, u32[]{:S(2)}) %collective-permute-start.14) | collective-permute-done | bytes 262176 | tf_op jit(solution)/shard_map/ppermute | solution.py:308
  70.5 3.9 %collective-permute-done.15.refs_3_ = bf16[256,512]{1,0:T(8,128)(2,1)S(1)} collective-permute-done((bf16[256,512]{1,0:T(8,128)(2,1)}, bf16[256,512]{1,0:T(8,128)(2,1)S(1)}, u32[]{:S(2)}, u32[]{:S(2)}) %collective-permute-start.15) | collective-permute-done | bytes 262176 | tf_op jit(solution)/shard_map/ppermute | solution.py:308
  74.4 0.7 copy-done.10
  75.1 3.7 %shard_map.95 = bf16[256,2048]{1,0:T(8,128)(2,1)} custom-call(s32[3]{0:T(128)} %pad_add_fusion.where_ref, bf16[256,2048]{1,0:T(8,128)(2,1)} %gate_ref.3, bf16[256,512]{1,0:T(8,128)(2,1)} %get-tuple-element.17.refs_0_, bf16[256,512]{1,0:T(8,128)(2,1)} %copy-done.8, bf16[256,512]{1,0:T(8,128)(2,1)} %copy-done.9, bf16[256,512]{1,0:T(8,128)(2,1)} %copy-done.10), custom_call_target="tpu_custom_call" | custom-call | tf_op jit(solution)/shard_map/pallas_call | solution.py:249
  (42 shorter events, 0.1 us)
Async XLA Ops:
  0.0 28.7 %copy-start = (f32[2048]{0:T(1024)S(1)}, f32[2048]{0:T(1024)}, u32[]{:S(2)}) copy-start(f32[2048]{0:T(1024)} %param.13) | copy-start | bytes 24580
  0.9 12.1 %collective-permute-start.2 = (bf16[512,128]{1,0:T(8,128)(2,1)S(1)}, bf16[512,128]{1,0:T(8,128)(2,1)S(1)}, u32[]{:S(2)}, u32[]{:S(2)}) collective-permute-start(bf16[512,128]{1,0:T(8,128)(2,1)S(1)} %constant_dynamic-slice_fusion), channel_id=1, source_target_pairs={{0,12},{1,13},{2,14},{3,15},{4,0},{5,1},{6,2},{7,3},{8,4},{9,5},{1... | collective-permute-start | bytes 393224 | tf_op jit(solution)/shard_map/ppermute | solution.py:277
  6.0 11.2 %collective-permute-start.1 = (bf16[512,128]{1,0:T(8,128)(2,1)S(1)}, bf16[512,128]{1,0:T(8,128)(2,1)S(1)}, u32[]{:S(2)}, u32[]{:S(2)}) collective-permute-start(bf16[512,128]{1,0:T(8,128)(2,1)S(1)} %constant_dynamic-slice_fusion), channel_id=1, source_target_pairs={{0,8},{1,9},{2,10},{3,11},{4,12},{5,13},{6,14},{7,15},{8,0},{9,1},... | collective-permute-start | bytes 393224 | tf_op jit(solution)/shard_map/ppermute | solution.py:277
  6.0 12.7 %collective-permute-start = (bf16[512,128]{1,0:T(8,128)(2,1)S(1)}, bf16[512,128]{1,0:T(8,128)(2,1)S(1)}, u32[]{:S(2)}, u32[]{:S(2)}) collective-permute-start(bf16[512,128]{1,0:T(8,128)(2,1)S(1)} %constant_dynamic-slice_fusion), channel_id=1, source_target_pairs={{0,4},{1,5},{2,6},{3,7},{4,8},{5,9},{6,10},{7,11},{8,12},{9,13},{1... | collective-permute-start | bytes 393224 | tf_op jit(solution)/shard_map/ppermute | solution.py:277
  11.4 15.2 %collective-permute-start.6 = (bf16[256,512]{1,0:T(8,128)(2,1)}, bf16[256,512]{1,0:T(8,128)(2,1)S(1)}, u32[]{:S(2)}, u32[]{:S(2)}) collective-permute-start(bf16[256,512]{1,0:T(8,128)(2,1)} %get-tuple-element.14), channel_id=1, source_target_pairs={{0,1},{1,0},{2,3},{3,2},{4,5},{5,4},{6,7},{7,6},{8,9},{9,8},{10,11... | collective-permute-start | bytes 786440 | tf_op jit(solution)/shard_map/ppermute | solution.py:308
  11.5 15.3 %collective-permute-start.7 = (bf16[256,512]{1,0:T(8,128)(2,1)}, bf16[256,512]{1,0:T(8,128)(2,1)S(1)}, u32[]{:S(2)}, u32[]{:S(2)}) collective-permute-start(bf16[256,512]{1,0:T(8,128)(2,1)} %get-tuple-element.15), channel_id=1, source_target_pairs={{0,2},{1,3},{2,0},{3,1},{4,6},{5,7},{6,4},{7,5},{8,10},{9,11},{10,... | collective-permute-start | bytes 786440 | tf_op jit(solution)/shard_map/ppermute | solution.py:308
  13.1 16.2 %copy-start.11 = (bf16[512,128]{1,0:T(8,128)(2,1)}, bf16[512,128]{1,0:T(8,128)(2,1)S(1)}, u32[]{:S(2)}) copy-start(bf16[512,128]{1,0:T(8,128)(2,1)S(1)} %collective-permute-done.2.refs_2_) | copy-start | bytes 393220
  13.1 6.2 %collective-permute-start.5 = (bf16[512,128]{1,0:T(8,128)(2,1)S(1)}, bf16[512,128]{1,0:T(8,128)(2,1)S(1)}, u32[]{:S(2)}, u32[]{:S(2)}) collective-permute-start(bf16[512,128]{1,0:T(8,128)(2,1)S(1)} %collective-permute-done.2.refs_2_), channel_id=1, source_target_pairs={{0,16},{16,0},{1,17},{17,1},{2,18},{18,2},{3,19},{19,3},{4,20},{20... | collective-permute-start | bytes 393224 | tf_op jit(solution)/shard_map/ppermute | solution.py:280
  17.2 12.0 %copy-start.12 = (bf16[512,128]{1,0:T(8,128)(2,1)}, bf16[512,128]{1,0:T(8,128)(2,1)S(1)}, u32[]{:S(2)}) copy-start(bf16[512,128]{1,0:T(8,128)(2,1)S(1)} %collective-permute-done.1.refs_1_) | copy-start | bytes 393220
  17.2 6.2 %collective-permute-start.4 = (bf16[512,128]{1,0:T(8,128)(2,1)S(1)}, bf16[512,128]{1,0:T(8,128)(2,1)S(1)}, u32[]{:S(2)}, u32[]{:S(2)}) collective-permute-start(bf16[512,128]{1,0:T(8,128)(2,1)S(1)} %collective-permute-done.1.refs_1_), channel_id=1, source_target_pairs={{0,16},{16,0},{1,17},{17,1},{2,18},{18,2},{3,19},{19,3},{4,20},{20... | collective-permute-start | bytes 393224 | tf_op jit(solution)/shard_map/ppermute | solution.py:280
  18.7 10.5 %copy-start.13 = (bf16[512,128]{1,0:T(8,128)(2,1)}, bf16[512,128]{1,0:T(8,128)(2,1)S(1)}, u32[]{:S(2)}) copy-start(bf16[512,128]{1,0:T(8,128)(2,1)S(1)} %collective-permute-done.refs_0_) | copy-start | bytes 393220
  18.7 6.1 %collective-permute-start.3 = (bf16[512,128]{1,0:T(8,128)(2,1)S(1)}, bf16[512,128]{1,0:T(8,128)(2,1)S(1)}, u32[]{:S(2)}, u32[]{:S(2)}) collective-permute-start(bf16[512,128]{1,0:T(8,128)(2,1)S(1)} %collective-permute-done.refs_0_), channel_id=1, source_target_pairs={{0,16},{16,0},{1,17},{17,1},{2,18},{18,2},{3,19},{19,3},{4,20},{20... | collective-permute-start | bytes 393224 | tf_op jit(solution)/shard_map/ppermute | solution.py:280
  19.3 10.0 %copy-start.14 = (bf16[512,128]{1,0:T(8,128)(2,1)}, bf16[512,128]{1,0:T(8,128)(2,1)S(1)}, u32[]{:S(2)}) copy-start(bf16[512,128]{1,0:T(8,128)(2,1)S(1)} %collective-permute-done.5.refs_5_) | copy-start | bytes 393220
  19.3 14.8 %collective-permute-start.8 = (bf16[256,512]{1,0:T(8,128)(2,1)}, bf16[256,512]{1,0:T(8,128)(2,1)S(1)}, u32[]{:S(2)}, u32[]{:S(2)}) collective-permute-start(bf16[256,512]{1,0:T(8,128)(2,1)} %get-tuple-element.16), channel_id=1, source_target_pairs={{0,3},{1,2},{2,1},{3,0},{4,7},{5,6},{6,5},{7,4},{8,11},{9,10},{10,... | collective-permute-start | bytes 786440 | tf_op jit(solution)/shard_map/ppermute | solution.py:308
  23.4 5.9 %copy-start.15 = (bf16[512,128]{1,0:T(8,128)(2,1)}, bf16[512,128]{1,0:T(8,128)(2,1)S(1)}, u32[]{:S(2)}) copy-start(bf16[512,128]{1,0:T(8,128)(2,1)S(1)} %collective-permute-done.4.refs_4_) | copy-start | bytes 393220
  23.4 15.9 %collective-permute-start.10 = (bf16[256,512]{1,0:T(8,128)(2,1)}, bf16[256,512]{1,0:T(8,128)(2,1)S(1)}, u32[]{:S(2)}, u32[]{:S(2)}) collective-permute-start(bf16[256,512]{1,0:T(8,128)(2,1)} %get-tuple-element.14), channel_id=1, source_target_pairs={{0,5},{1,4},{2,7},{3,6},{4,9},{5,8},{6,11},{7,10},{8,13},{9,12},{1... | collective-permute-start | bytes 786440 | tf_op jit(solution)/shard_map/ppermute | solution.py:308
  24.8 4.5 %copy-start.16 = (bf16[512,128]{1,0:T(8,128)(2,1)}, bf16[512,128]{1,0:T(8,128)(2,1)S(1)}, u32[]{:S(2)}) copy-start(bf16[512,128]{1,0:T(8,128)(2,1)S(1)} %collective-permute-done.3.refs_3_) | copy-start | bytes 393220
  24.8 14.5 %collective-permute-start.11 = (bf16[256,512]{1,0:T(8,128)(2,1)}, bf16[256,512]{1,0:T(8,128)(2,1)S(1)}, u32[]{:S(2)}, u32[]{:S(2)}) collective-permute-start(bf16[256,512]{1,0:T(8,128)(2,1)} %get-tuple-element.15), channel_id=1, source_target_pairs={{0,6},{1,7},{2,4},{3,5},{4,10},{5,11},{6,8},{7,9},{8,14},{9,15},{1... | collective-permute-start | bytes 786440 | tf_op jit(solution)/shard_map/ppermute | solution.py:308
  26.7 7.4 %copy-start.1 = (bf16[256,512]{1,0:T(8,128)(2,1)}, bf16[256,512]{1,0:T(8,128)(2,1)S(1)}, u32[]{:S(2)}) copy-start(bf16[256,512]{1,0:T(8,128)(2,1)S(1)} %collective-permute-done.6.refs_1_.refs_5_) | copy-start | bytes 786436
  26.7 19.2 %collective-permute-start.12 = (bf16[256,512]{1,0:T(8,128)(2,1)}, bf16[256,512]{1,0:T(8,128)(2,1)S(1)}, u32[]{:S(2)}, u32[]{:S(2)}) collective-permute-start(bf16[256,512]{1,0:T(8,128)(2,1)} %get-tuple-element.16), channel_id=1, source_target_pairs={{0,7},{1,6},{2,5},{3,4},{4,11},{5,10},{6,9},{7,8},{8,15},{9,14},{1... | collective-permute-start | bytes 786440 | tf_op jit(solution)/shard_map/ppermute | solution.py:308
  26.8 7.4 %copy-start.2 = (bf16[256,512]{1,0:T(8,128)(2,1)}, bf16[256,512]{1,0:T(8,128)(2,1)S(1)}, u32[]{:S(2)}) copy-start(bf16[256,512]{1,0:T(8,128)(2,1)S(1)} %collective-permute-done.7.refs_2_.refs_6_) | copy-start | bytes 786436
  26.8 21.5 %collective-permute-start.9 = (bf16[256,512]{1,0:T(8,128)(2,1)}, bf16[256,512]{1,0:T(8,128)(2,1)S(1)}, u32[]{:S(2)}, u32[]{:S(2)}) collective-permute-start(bf16[256,512]{1,0:T(8,128)(2,1)} %get-tuple-element.13.refs_0_.refs_4_), channel_id=1, source_target_pairs={{0,4},{1,5},{2,6},{3,7},{4,8},{5,9},{6,10},{7,11},{8,12},{9,13},{1... | collective-permute-start | bytes 786440 | tf_op jit(solution)/shard_map/ppermute | solution.py:308
  39.3 9.0 %copy-start.4 = (bf16[256,512]{1,0:T(8,128)(2,1)}, bf16[256,512]{1,0:T(8,128)(2,1)S(1)}, u32[]{:S(2)}) copy-start(bf16[256,512]{1,0:T(8,128)(2,1)S(1)} %collective-permute-done.10.refs_1_) | copy-start | bytes 786436
  39.3 9.0 %copy-start.5 = (bf16[256,512]{1,0:T(8,128)(2,1)}, bf16[256,512]{1,0:T(8,128)(2,1)S(1)}, u32[]{:S(2)}) copy-start(bf16[256,512]{1,0:T(8,128)(2,1)S(1)} %collective-permute-done.11.refs_2_) | copy-start | bytes 786436
  45.8 2.4 %copy-start.6 = (bf16[256,512]{1,0:T(8,128)(2,1)}, bf16[256,512]{1,0:T(8,128)(2,1)S(1)}, u32[]{:S(2)}) copy-start(bf16[256,512]{1,0:T(8,128)(2,1)S(1)} %collective-permute-done.12.refs_3_) | copy-start | bytes 786436
  48.3 0.7 copy-start.7
  60.0 2.6 %collective-permute-start.13 = (bf16[256,512]{1,0:T(8,128)(2,1)}, bf16[256,512]{1,0:T(8,128)(2,1)S(1)}, u32[]{:S(2)}, u32[]{:S(2)}) collective-permute-start(bf16[256,512]{1,0:T(8,128)(2,1)} %get-tuple-element.18), channel_id=1, source_target_pairs={{0,1},{1,0},{2,3},{3,2},{4,5},{5,4},{6,7},{7,6},{8,9},{9,8},{10,11... | collective-permute-start | bytes 786440 | tf_op jit(solution)/shard_map/ppermute | solution.py:308
  61.2 9.4 %collective-permute-start.14 = (bf16[256,512]{1,0:T(8,128)(2,1)}, bf16[256,512]{1,0:T(8,128)(2,1)S(1)}, u32[]{:S(2)}, u32[]{:S(2)}) collective-permute-start(bf16[256,512]{1,0:T(8,128)(2,1)} %get-tuple-element.19), channel_id=1, source_target_pairs={{0,2},{1,3},{2,0},{3,1},{4,6},{5,7},{6,4},{7,5},{8,10},{9,11},{10,... | collective-permute-start | bytes 786440 | tf_op jit(solution)/shard_map/ppermute | solution.py:308
  62.1 12.4 %collective-permute-start.15 = (bf16[256,512]{1,0:T(8,128)(2,1)}, bf16[256,512]{1,0:T(8,128)(2,1)S(1)}, u32[]{:S(2)}, u32[]{:S(2)}) collective-permute-start(bf16[256,512]{1,0:T(8,128)(2,1)} %get-tuple-element.20), channel_id=1, source_target_pairs={{0,3},{1,2},{2,1},{3,0},{4,7},{5,6},{6,5},{7,4},{8,11},{9,10},{10,... | collective-permute-start | bytes 786440 | tf_op jit(solution)/shard_map/ppermute | solution.py:308
  62.6 11.8 %copy-start.8 = (bf16[256,512]{1,0:T(8,128)(2,1)}, bf16[256,512]{1,0:T(8,128)(2,1)S(1)}, u32[]{:S(2)}) copy-start(bf16[256,512]{1,0:T(8,128)(2,1)S(1)} %collective-permute-done.13.refs_1_) | copy-start | bytes 786436
  70.5 3.9 %copy-start.9 = (bf16[256,512]{1,0:T(8,128)(2,1)}, bf16[256,512]{1,0:T(8,128)(2,1)S(1)}, u32[]{:S(2)}) copy-start(bf16[256,512]{1,0:T(8,128)(2,1)S(1)} %collective-permute-done.14.refs_2_) | copy-start | bytes 786436
  74.4 0.7 copy-start.10
  (1 other events, 0.7 us)

commit v2 on v0

v2 whole, which is shorter than its diff:
```python
import functools

import jax
import jax.numpy as jnp
import ml_dtypes
import numpy as np
from jax import lax
from jax.experimental import pallas as pl
from jax.experimental.pallas import tpu as pltpu
from jax.sharding import PartitionSpec as P

LANES = 128
CHUNKS = 2
BF16 = jnp.bfloat16
F32 = jnp.float32
VMEM = pl.BlockSpec(memory_space=pltpu.VMEM)
SMALL = pl.CostEstimate(flops=1000, bytes_accessed=1000, transcendentals=0)


def two_parts(table):
    high = table.astype(ml_dtypes.bfloat16)
    low = (table - high.astype(np.float64)).astype(ml_dtypes.bfloat16)
    return jnp.asarray(high), jnp.asarray(low)


def bin_order(rows):
    return np.concatenate([np.arange(0, rows, 2), np.arange(1, rows, 2)])


def forward_tables(rows):
    bins = bin_order(rows)[:, None] + 0.5
    angle = bins * np.arange(rows)[None, :] * (np.pi / rows)
    return two_parts(np.concatenate([np.cos(angle), -np.sin(angle)], axis=0))


def inverse_tables(rows):
    bins = bin_order(rows)[None, :] + 0.5
    angle = bins * (np.arange(rows)[:, None] + rows) * (np.pi / rows)
    return two_parts(np.concatenate([np.cos(angle), -np.sin(angle)], axis=1) / rows)


def matmul(a, b):
    return jnp.dot(a, b, preferred_element_type=F32)


def params(mib):
    return pltpu.CompilerParams(vmem_limit_bytes=mib << 20)


def place(members):
    index = lax.axis_index("ctx")
    return lax.rem(index, members), lax.div(index, members)


def aligned(position, size):
    return pl.ds(pl.multiple_of(position * size, size), size)


def product_kernel(
    layers, members, gate_hbm, values_hbm, half_ref, keep_same_ref, keep_other_ref, *more
):
    del half_ref
    send_refs, (gate, values, sems) = more[:-3], more[-3:]
    member, _ = place(members)
    per_chunk = layers // CHUNKS
    count = sems.shape[1]
    step = gate.shape[0] // count

    def copies(index):
        rows = slice(index * step, (index + 1) * step)
        return [
            pltpu.make_async_copy(source.at[rows], target.at[rows], sems.at[which, index])
            for which, (source, target) in enumerate(((gate_hbm, gate), (values_hbm, values)))
        ]

    for index in range(count):
        for copy in copies(index):
            copy.start()
    refs = [
        lambda chunk, rows, lanes: keep_same_ref.at[chunk, rows, lanes],
        lambda chunk, rows, lanes: send_refs[2 * chunk].at[rows, lanes],
        lambda chunk, rows, lanes: keep_other_ref.at[chunk, rows, lanes],
        lambda chunk, rows, lanes: send_refs[2 * chunk + 1].at[rows, lanes],
    ]
    for index in range(count):
        rows = slice(index * step, (index + 1) * step)
        for copy in copies(index):
            copy.wait()
        for apart in range(members):
            held = member ^ apart
            for layer in range(layers):
                lanes = aligned(layer * members + held, LANES)
                gated = gate[rows, lanes].astype(F32) * values[rows, lanes].astype(F32)
                at = layer % per_chunk * LANES
                target = refs[apart](layer // per_chunk, rows, slice(at, at + LANES))
                target[...] = gated.astype(BF16)


def product_pieces(gate_in, values, half, layers, members):
    rows, channels = values.shape
    width = channels // (layers * members)
    chunk = channels // members // CHUNKS
    if width != LANES:
        member, _ = place(members)
        product = (gate_in.astype(F32) * values.astype(F32)).astype(BF16)
        product = product.reshape(rows, CHUNKS, layers // CHUNKS, members, width)
        product = product.transpose(3, 1, 0, 2, 4).reshape(members, CHUNKS, rows, chunk)
        pieces = [lax.dynamic_index_in_dim(product, member ^ d, 0, False) for d in range(members)]
        return pieces[0], pieces[2], pieces[1][0], pieces[3][0], pieces[1][1], pieces[3][1]
    count = 4
    there = pl.BlockSpec(memory_space=pltpu.HBM)
    return pl.pallas_call(
        functools.partial(product_kernel, layers, members),
        in_specs=[there, there, pl.BlockSpec(memory_space=pl.ANY)],
        out_specs=[VMEM] * (2 + 2 * CHUNKS),
        out_shape=[jax.ShapeDtypeStruct((CHUNKS, rows, chunk), BF16)] * 2
        + [jax.ShapeDtypeStruct((rows, chunk), BF16)] * (2 * CHUNKS),
        scratch_shapes=[pltpu.VMEM((rows, channels), BF16)] * 2 + [pltpu.SemaphoreType.DMA((2, count))],
        compiler_params=params(8),
        cost_estimate=SMALL,
    )(gate_in, values, half)


def pack_kernel(same_ref, other_ref, *refs):
    core_refs, (mine_ref, across_ref, *beyond_refs) = refs[: 2 * CHUNKS], refs[2 * CHUNKS :]
    for part in range(CHUNKS):
        mine_ref[part, 0] = same_ref[part]
        mine_ref[part, 1] = core_refs[2 * part][...]
        for target in (across_ref.at[part], beyond_refs[part]):
            target[0] = other_ref[part]
            target[1] = core_refs[2 * part + 1][...]


def payloads(same, other, core):
    _, rows, chunk = same.shape
    return pl.pallas_call(
        pack_kernel,
        in_specs=[VMEM] * (2 + len(core)),
        out_specs=[VMEM] * (2 + CHUNKS),
        out_shape=[jax.ShapeDtypeStruct((CHUNKS, 2, rows, chunk), BF16)] * 2
        + [jax.ShapeDtypeStruct((2, rows, chunk), BF16)] * CHUNKS,
        compiler_params=params(8),
        cost_estimate=SMALL,
    )(same, other, *core)


def join_kernel(*refs):
    at = 0
    for ref in refs[:-1]:
        count = ref.shape[0]
        refs[-1][at : at + count] = ref[...]
        at += count


def joined(pieces):
    return pl.pallas_call(
        join_kernel,
        in_specs=[VMEM] * len(pieces),
        out_specs=VMEM,
        out_shape=jax.ShapeDtypeStruct((sum(p.shape[0] for p in pieces), *pieces[0].shape[1:]), BF16),
        compiler_params=params(8),
        cost_estimate=SMALL,
    )(*pieces)


def put_tap_spectra(high_ref, low_ref, taps, out_ref):
    rows = high_ref.shape[1]
    chunk = out_ref.shape[-1]
    for part in range(CHUNKS):
        for lag in range(out_ref.shape[1]):
            block = taps[lag * rows : (lag + 1) * rows, part * chunk : (part + 1) * chunk]
            out_ref[part, lag] = matmul(high_ref[...], block) + matmul(low_ref[...], block)


def taps_kernel(layers, members, high_ref, low_ref, own_ref, near_ref, far_ref, out_ref, taps):
    _, layer = place(members)
    group = lax.axis_index("groups")
    half = near_ref.shape[1]
    near, far = aligned(group, half), aligned(1 - group, half)
    taps[:, aligned(layer, LANES)] = own_ref[...]
    for apart in range(1, layers):
        lanes = aligned(layer ^ apart, LANES)
        at = (None, 0, 2, 1)[apart]
        taps[near, lanes] = near_ref[at]
        taps[far, lanes] = far_ref[at]
    put_tap_spectra(high_ref, low_ref, taps, out_ref)


def near_half(filter_taps, layers, groups):
    count, width = filter_taps.shape
    if width != LANES or groups != 2 or layers != 4:
        return None
    start = lax.axis_index("groups") * (count // 2)
    return lax.dynamic_slice_in_dim(filter_taps, start, count // 2, 0)[None]


def tap_spectra(tables, filter_taps, near, layers, members):
    count, width = filter_taps.shape
    rows = tables[0].shape[1]
    held = width * layers
    out_shape = jax.ShapeDtypeStruct((CHUNKS, count // rows, 2 * rows, held // CHUNKS), F32)
    if near is None:
        ring = [[layer * members + member for layer in range(layers)] for member in range(members)]
        taps = lax.all_gather(filter_taps, "ctx", axis=1, tiled=True, axis_index_groups=ring)
        return pl.pallas_call(
            put_tap_spectra,
            in_specs=[VMEM] * 3,
            out_specs=VMEM,
            out_shape=out_shape,
            compiler_params=params(20),
            cost_estimate=SMALL,
        )(*tables, taps)
    far = lax.ppermute(near, "groups", [(0, 1), (1, 0)])
    return pl.pallas_call(
        functools.partial(taps_kernel, layers, members),
        in_specs=[VMEM] * 5,
        out_specs=VMEM,
        out_shape=out_shape,
        scratch_shapes=[pltpu.VMEM((count, held), BF16)],
        compiler_params=params(20),
        cost_estimate=SMALL,
    )(*tables, filter_taps, near, far)


def window(before, after, sign):
    (before_real, before_imag), (real, imag) = before, after
    if sign > 0:
        return before_real + imag, before_imag - real
    return before_real - imag, before_imag + real


def sum_products(pairs):
    real_sum = imag_sum = None
    for (tap_real, tap_imag), (real, imag) in pairs:
        real_part = tap_real * real - tap_imag * imag
        imag_part = tap_real * imag + tap_imag * real
        real_sum = real_part if real_sum is None else real_sum + real_part
        imag_sum = imag_part if imag_sum is None else imag_sum + imag_part
    return real_sum, imag_sum


def for_bins(rows, step, body):
    count = rows // (2 * step)
    for sign, first in ((1, 0), (-1, count)):

        @pl.loop(first, first + count)
        def _(index):
            body(pl.multiple_of(index * step, step), sign)


def reader(ref, rows, at, step):
    def read(*index):
        return ref[*index, pl.ds(at, step), :], ref[*index, pl.ds(at + rows, step), :]

    return read


def own_kernel(
    members, high_ref, low_ref, taps_ref, mine_ref, across_ref, part_ref, first_ref, spectra
):
    member, _ = place(members)
    rows = high_ref.shape[1]
    for part in range(CHUNKS):
        blocks = [mine_ref[part, 0], mine_ref[part, 1], across_ref[part, 0], across_ref[part, 1]]
        for apart, block in enumerate(blocks):
            spectra[member ^ apart] = matmul(high_ref[...], block) + matmul(low_ref[...], block)
        first_ref[part] = spectra[0]

        def body(at, sign):
            read = reader(spectra, rows, at, 8)
            taps_read = reader(taps_ref, rows, at, 8)
            taps = [taps_read(part, lag) for lag in range(members - 1)]
            blocks = [read(position) for position in range(members)]
            windows = [window(a, b, sign) for a, b in zip(blocks, blocks[1:])]
            for output in range(1, members):
                total = sum_products([(taps[lag], windows[output - 1 - lag]) for lag in range(output)])
                part_ref[part, output - 1, pl.ds(at, 8), :] = total[0]
                part_ref[part, output - 1, pl.ds(at + rows, 8), :] = total[1]

        for_bins(rows, 8, body)


def own_partials(tables, taps, mine, across):
    members = taps.shape[1]
    chunk = taps.shape[-1]
    rows = tables[0].shape[1]
    return pl.pallas_call(
        functools.partial(own_kernel, members),
        in_specs=[VMEM] * 5,
        out_specs=[VMEM] * 2,
        out_shape=[
            jax.ShapeDtypeStruct((CHUNKS, members - 1, 2 * rows, chunk), F32),
            jax.ShapeDtypeStruct((CHUNKS, 2 * rows, chunk), F32),
        ],
        scratch_shapes=[pltpu.VMEM((members, 2 * rows, chunk), F32)],
        compiler_params=params(20),
        cost_estimate=SMALL,
    )(*tables, taps, mine, across)


def mix_kernel(
    members,
    part,
    high_ref,
    low_ref,
    back_high_ref,
    back_low_ref,
    skip_ref,
    taps_ref,
    part_ref,
    first_ref,
    mine_ref,
    across_ref,
    ahead_ref,
    beyond_ref,
    *refs,
):
    out_refs, (halo, sums) = refs[:members], refs[members:]
    member, _ = place(members)
    rows = high_ref.shape[1]
    halo_blocks = [ahead_ref[part, 0], ahead_ref[part, 1], beyond_ref[0], beyond_ref[1]]
    for apart, block in enumerate(halo_blocks):
        halo[member ^ apart] = matmul(high_ref[...], block) + matmul(low_ref[...], block)

    def body(at, sign):
        read = reader(halo, rows, at, 8)
        taps_read = reader(taps_ref, rows, at, 8)
        taps = [taps_read(part, lag) for lag in range(members)]
        blocks = [read(position) for position in range(members)]
        blocks.append(reader(first_ref, rows, at, 8)(part))
        windows = [window(a, b, sign) for a, b in zip(blocks, blocks[1:])]
        for output in range(members):
            total = sum_products(
                [(taps[lag], windows[members - 1 + output - lag]) for lag in range(output, members)]
            )
            if output:
                before = reader(part_ref, rows, at, 8)(part, output - 1)
                total = total[0] + before[0], total[1] + before[1]
            sums[output, pl.ds(at, 8), :] = total[0]
            sums[output, pl.ds(at + rows, 8), :] = total[1]

    for_bins(rows, 8, body)
    blocks = [mine_ref[part, 0], mine_ref[part, 1], across_ref[part, 0], across_ref[part, 1]]
    for apart, block in enumerate(blocks):
        total = sums[member ^ apart]
        high = total.astype(BF16)
        low = (total - high.astype(F32)).astype(BF16)
        convolved = matmul(back_high_ref[...], high) + (
            matmul(back_high_ref[...], low) + matmul(back_low_ref[...], high)
        )
        mixed = convolved + skip_ref[part] * block.astype(F32)
        out_refs[apart][...] = mixed.astype(BF16)


def mixed_pieces(part, tables, back_tables, skip, taps, partial, first, *blocks):
    members, chunk = taps.shape[1], taps.shape[-1]
    rows = tables[0].shape[1]
    return pl.pallas_call(
        functools.partial(mix_kernel, members, part),
        in_specs=[VMEM] * 12,
        out_specs=[VMEM] * members,
        out_shape=[jax.ShapeDtypeStruct((rows, chunk), BF16)] * members,
        scratch_shapes=[pltpu.VMEM((members, 2 * rows, chunk), F32)] * 2,
        compiler_params=params(20),
        cost_estimate=SMALL,
    )(*tables, *back_tables, skip, taps, partial, first, *blocks)


def gate_kernel(layers, members, part, gate_ref, *refs):
    piece_refs, out_ref = refs[:members], refs[-1]
    member, _ = place(members)
    for apart in range(members):
        held = member ^ apart
        for layer in range(layers):
            lanes = aligned(layer * members + held, LANES)
            mixed = piece_refs[apart][:, layer * LANES : (layer + 1) * LANES].astype(F32)
            out_ref[:, lanes] = (gate_ref[:, lanes].astype(F32) * mixed).astype(BF16)


def gated_output(part, gate_out, pieces, layers, members, out):
    rows, channels = gate_out.shape
    chunk = channels // members // CHUNKS
    width = channels // (layers * members)
    wide = channels // CHUNKS
    if width != LANES:
        member, _ = place(members)
        stacked = jnp.stack(pieces)
        stacked = jnp.stack(
            [lax.dynamic_index_in_dim(stacked, member ^ d, 0, False) for d in range(members)]
        )
        mixed = stacked.reshape(members, rows, layers // CHUNKS, width).transpose(1, 2, 0, 3)
        gate = gate_out[:, part * wide : (part + 1) * wide].astype(F32)
        gated = (gate * mixed.reshape(rows, wide).astype(F32)).astype(BF16)
        return gated if out is None else jnp.concatenate([out, gated], axis=1)
    step = rows // 2
    there = pl.BlockSpec((step, wide), lambda r: (r, part))
    more = [] if out is None else [out]
    return pl.pallas_call(
        functools.partial(gate_kernel, layers // CHUNKS, members, part),
        grid=(2,),
        in_specs=[there]
        + [pl.BlockSpec((step, chunk), lambda r: (r, 0))] * members
        + [pl.BlockSpec(memory_space=pl.ANY)] * len(more),
        out_specs=there,
        out_shape=jax.ShapeDtypeStruct((rows, channels), BF16),
        input_output_aliases={members + 1: 0} if more else {},
        compiler_params=params(16),
        cost_estimate=SMALL,
    )(gate_out, *pieces, *more)


def on_device(gate_out, gate_in, values, filter_taps, skip_gain):
    rows, channels = values.shape
    length = lax.axis_size("ctx")
    members = filter_taps.shape[0] // rows
    layers = length // members
    width = channels // length
    member, _ = place(members)
    tables, back_tables = forward_tables(rows), inverse_tables(rows)

    def to_member(value, apart, ahead):
        pairs = [
            (i, (i // members + ahead) % layers * members + (i % members ^ apart))
            for i in range(length)
        ]
        return lax.ppermute(value, "ctx", pairs)

    def to_layer(value, apart):
        pairs = [(i, (i // members ^ apart) * members + i % members) for i in range(length)]
        return lax.ppermute(value, "ctx", pairs)

    half = near_half(filter_taps, layers, lax.axis_size("groups"))
    near = None
    if half is not None:
        two_away = to_layer(half, 2)
    same, other, *send = product_pieces(gate_in, values, half, layers, members)
    core = [to_member(piece, 1, 0) for piece in send]
    if half is not None:
        two_away, core = lax.optimization_barrier((two_away, core))
    mine, to_across, *to_beyond = payloads(same, other, core)
    if half is not None:
        one_and_three_away = to_layer(joined([half, two_away]), 1)
        near = joined([one_and_three_away, two_away])
    ahead = to_member(mine, 0, 1)
    beyond = [to_member(piece, 2, 1) for piece in to_beyond]
    across = to_member(to_across, 2, 0)
    taps = tap_spectra(tables, filter_taps, near, layers, members)
    partial, first = own_partials(tables, taps, mine, across)
    skip = skip_gain.reshape(layers, members, width)
    skip = lax.dynamic_index_in_dim(skip, member, 1, False).reshape(CHUNKS, 1, channels // members // CHUNKS)
    out = None
    for part in range(CHUNKS):
        mixed = mixed_pieces(
            part, tables, back_tables, skip, taps, partial, first, mine, across, ahead, beyond[part]
        )
        mixed = [mixed[0]] + [to_member(mixed[d], d, 0) for d in range(1, members)]
        out = gated_output(part, gate_out, mixed, layers, members, out)
    return out


def solution(mesh):
    in_specs = (
        P(("groups", "ctx"), None),
        P(("groups", "ctx"), None),
        P(("groups", "ctx"), None),
        P(None, "ctx"),
        P(),
    )
    out_specs = P(("groups", "ctx"), None)
    return jax.shard_map(
        on_device, mesh=mesh, in_specs=in_specs, out_specs=out_specs, check_vma=False
    )
```

time: 201 us -> 59.2 us (0.29)
  waiting for transfers between devices: 85.7 us -> 20.8 us
  matrix products: 55.8 us -> 0 us
  other arithmetic: 39 us -> 0 us
  Pallas kernels: 0 us -> 15.2 us
  starting transfers between devices: 5.73 us -> 19.4 us
  between operations: 13.6 us -> 0.14 us
  local copies, waits for them, and re-layouts: 0.93 us -> 3.46 us
    ppermute x4 -> x17, waiting for transfers between devices: 85 us -> 20.8 us  [the longest x14 13.1 us: to_member(): return lax.ppermute(value, 'ctx', pairs)]
    dot_general x11 -> x0, matrix products: 55.8 us -> none  [the longest x9 36.3 us: spectrum(): jnp.dot(table, block.astype(jnp.float32), precision=lax.Precision.HIGHEST)]
    sub x4 -> x0, other arithmetic: 32 us -> none  [complex_product(): real_part = first_real * second_real - first_imag * second_imag]
    pallas_call x0 -> x10, Pallas kernels: none -> 15.2 us  [the longest x2 6.76 us: mixed_pieces(): pl.pallas_call(functools.partial(mix_kernel, members, part), in_specs=[VM...]
    ppermute x4 -> x17, starting transfers between devices: 5.73 us -> 19.4 us  [the longest x14 12.9 us: to_member(): return lax.ppermute(value, 'ctx', pairs)]
    mul x1 -> x0, other arithmetic: 4 us -> none  [inverse_table(): -weight * jnp.sin(angle)]
  transfers between devices with their start and end apart: 5 -> 17, of which waited for: 4 -> 7; matrix products, arithmetic and copies ran while one was open for 13% -> 0% of each run, Pallas kernels for 0% -> 24%
where the time goes in v2:
time: 59.2 us; the launch traced here: 59 us
  waiting for transfers between devices  20.8 us (35%)
  starting transfers between devices  19.4 us (33%)
  Pallas kernels  15.2 us (26%)
  local copies, waits for them, and re-layouts  3.46 us (6%)
    ppermute x14, waiting for transfers between devices, to_member(): return lax.ppermute(value, 'ctx', pairs)  13.1 us
    ppermute x14, starting transfers between devices, to_member(): return lax.ppermute(value, 'ctx', pairs)  12.9 us
    pallas_call x2, Pallas kernels, mixed_pieces(): pl.pallas_call(functools.partial(mix_kernel, members, part), in_specs=[VM...  6.76 us
    ppermute x2, starting transfers between devices, to_layer(): return lax.ppermute(value, 'ctx', pairs)  4.9 us
    ppermute x2, waiting for transfers between devices, to_layer(): return lax.ppermute(value, 'ctx', pairs)  4.9 us
    pallas_call x1, Pallas kernels, own_partials(): pl.pallas_call(functools.partial(own_kernel, members), in_specs=[VMEM] *...  2.97 us
    ppermute x1, waiting for transfers between devices, tap_spectra(): far = lax.ppermute(near, 'groups', [(0, 1), (1, 0)])  2.87 us
    unnamed x18, local copies, waits for them, and re-layouts  2.48 us
  transfers between devices with their start and end apart: 17, of which 7 were waited for; matrix products, arithmetic and copies ran while one was open for 0% of the time, Pallas kernels for 24%

profile of v2, /device:TPU:0, one launch (start us, length us, event | category | flops | bytes accessed | tf_op | source)
XLA Modules:
  0.0 59.0 jit_solution(481324061892384724)
XLA Ops:
  0.0 1.0 %dynamic-slice_bitcast_fusion.half_ref.refs_0_ = bf16[1,512,128]{2,1,0:T(8,128)(2,1)S(1)} fusion(bf16[1024,128]{1,0:T(8,128)(2,1)} %own_ref.1, s32[]{:T(128)S(6)} %select_n.8), kind=kLoop, calls=%fused_computation | loop fusion | bytes 262148 | tf_op jit(solution)/shard_map/broadcast_in_dim | solution.py:194
  1.0 4.1 %collective-permute-start = (bf16[1,512,128]{2,1,0:T(8,128)(2,1)S(1)}, bf16[1,512,128]{2,1,0:T(8,128)(2,1)S(1)}, u32[]{:S(2)}, u32[]{:S(2)}) collective-permute-start(bf16[1,512,128]{2,1,0:T(8,128)(2,1)S(1)} %dynamic-slice_bitcast_fusion.half_ref.refs_0_), channel_id=1, source_target_pairs={{0,8},{1,9},{2,10},{3,11},{4,12},{5,13},{6,14},{7,15},{8,0},{9,1},... | collective-permute-start | bytes 393224 | tf_op jit(solution)/shard_map/ppermute | solution.py:430
  5.1 1.2 %copy-done.6 = bf16[256,2048]{1,0:T(8,128)(2,1)S(1)} copy-done((bf16[256,2048]{1,0:T(8,128)(2,1)S(1)}, bf16[256,2048]{1,0:T(8,128)(2,1)}, u32[]{:S(2)}) %copy-start.6) | copy-done | bytes 1048600
  6.3 1.2 %copy-done.7 = bf16[256,2048]{1,0:T(8,128)(2,1)S(1)} copy-done((bf16[256,2048]{1,0:T(8,128)(2,1)S(1)}, bf16[256,2048]{1,0:T(8,128)(2,1)}, u32[]{:S(2)}) %copy-start.7) | copy-done | bytes 1048600
  7.6 0.8 %shard_map.91 = (bf16[2,256,256]{2,1,0:T(8,128)(2,1)S(1)}, bf16[2,256,256]{2,1,0:T(8,128)(2,1)S(1)}, bf16[256,256]{1,0:T(8,128)(2,1)S(1)}, bf16[256,256]{1,0:T(8...) custom-call(bf16[256,2048]{1,0:T(8,128)(2,1)S(1)} %copy-done.6, ...), custom_call_target="tpu_custom_call" | custom-call | flops 1000 | bytes 1000 | tf_op jit(solution)/shard_map/pallas_call | solution.py:112
  8.4 0.5 collective-permute-start.2
  9.0 0.4 collective-permute-start.4
  9.4 2.0 %collective-permute-done.refs_1_ = bf16[1,512,128]{2,1,0:T(8,128)(2,1)S(1)} collective-permute-done((bf16[1,512,128]{2,1,0:T(8,128)(2,1)S(1)}, bf16[1,512,128]{2,1,0:T(8,128)(2,1)S(1)}, u32[]{:S(2)}, u32[]{:S(2)}) %collective-permute-start) | collective-permute-done | bytes 131104 | tf_op jit(solution)/shard_map/ppermute | solution.py:430
  11.5 0.8 %collective-permute-start.5 = (bf16[2,512,128]{2,1,0:T(8,128)(2,1)S(1)}, bf16[2,512,128]{2,1,0:T(8,128)(2,1)S(1)}, u32[]{:S(2)}, u32[]{:S(2)}) collective-permute-start(bf16[2,512,128]{2,1,0:T(8,128)(2,1)S(1)} %shard_map.92), channel_id=1, source_target_pairs={{0,4},{1,5},{2,6},{3,7},{4,0},{5,1},{6,2},{7,3},{8,12},{9,13},{10,... | collective-permute-start | bytes 786440 | tf_op jit(solution)/shard_map/ppermute | solution.py:430
  12.2 1.0 %shard_map.95 = (bf16[2,2,256,256]{3,2,1,0:T(8,128)(2,1)S(1)}, bf16[2,2,256,256]{3,2,1,0:T(8,128)(2,1)}, bf16[2,256,256]{2,1,0:T(8,128)(2,1)}, bf16[2,256,256]{2,1,0:T(8,128)(2,1)}) custom-call(bf16[2,256,256]{2,1,0:T(8,128)(2,1)S(1)} %get-tuple-element.35.same_ref, bf16[2,256,256]{2,1,0:T(8,128)(2,1)S(1)} %get-tuple-element.36.other_ref, ...), custom_call_target="tpu_custom_call" | custom-call | flops 1000 | bytes 1000 | tf_op jit(solution)/shard_map/pallas_call | solution.py:136
  13.3 1.5 %collective-permute-start.7 = (bf16[2,2,256,256]{3,2,1,0:T(8,128)(2,1)}, bf16[2,2,256,256]{3,2,1,0:T(8,128)(2,1)S(1)}, u32[]{:S(2)}, u32[]{:S(2)}) collective-permute-start(bf16[2,2,256,256]{3,2,1,0:T(8,128)(2,1)} %get-tuple-element.42), channel_id=1, source_target_pairs={{0,2},{1,3},{2,0},{3,1},{4,6},{5,7},{6,4},{7,5},{8,10},{9,11},{10,... | collective-permute-start | bytes 1572872 | tf_op jit(solution)/shard_map/ppermute | solution.py:426
  14.8 1.4 %collective-permute-start.8 = (bf16[2,2,256,256]{3,2,1,0:T(8,128)(2,1)S(1)}, bf16[2,2,256,256]{3,2,1,0:T(8,128)(2,1)S(1)}, u32[]{:S(2)}, u32[]{:S(2)}) collective-permute-start(bf16[2,2,256,256]{3,2,1,0:T(8,128)(2,1)S(1)} %get-tuple-element.41.mine_ref), channel_id=1, source_target_pairs={{0,4},{1,5},{2,6},{3,7},{4,8},{5,9},{6,10},{7,11},{8,12},{9,13},{1... | collective-permute-start | bytes 1572872 | tf_op jit(solution)/shard_map/ppermute | solution.py:426
  16.1 2.9 %collective-permute-done.5.refs_0_ = bf16[2,512,128]{2,1,0:T(8,128)(2,1)S(1)} collective-permute-done((bf16[2,512,128]{2,1,0:T(8,128)(2,1)S(1)}, bf16[2,512,128]{2,1,0:T(8,128)(2,1)S(1)}, u32[]{:S(2)}, u32[]{:S(2)}) %collective-permute-start.5) | collective-permute-done | bytes 262176 | tf_op jit(solution)/shard_map/ppermute | solution.py:430
  19.1 1.6 %collective-permute-start.6 = (bf16[3,512,128]{2,1,0:T(8,128)(2,1)S(1)}, bf16[3,512,128]{2,1,0:T(8,128)(2,1)S(1)}, u32[]{:S(2)}, u32[]{:S(2)}) collective-permute-start(bf16[3,512,128]{2,1,0:T(8,128)(2,1)S(1)} %shard_map.93.near_ref), channel_id=1, source_target_pairs={{0,16},{16,0},{1,17},{17,1},{2,18},{18,2},{3,19},{19,3},{4,20},{20... | collective-permute-start | bytes 1179656 | tf_op jit(solution)/shard_map/ppermute | solution.py:213
  20.7 3.3 %collective-permute-start.13 = (bf16[2,256,256]{2,1,0:T(8,128)(2,1)}, bf16[2,256,256]{2,1,0:T(8,128)(2,1)}, u32[]{:S(2)}, u32[]{:S(2)}) collective-permute-start(bf16[2,256,256]{2,1,0:T(8,128)(2,1)} %get-tuple-element.50), channel_id=1, source_target_pairs={{0,6},{1,7},{2,4},{3,5},{4,10},{5,11},{6,8},{7,9},{8,14},{9,15},{1... | collective-permute-start | bytes 786440 | tf_op jit(solution)/shard_map/ppermute | solution.py:426
  23.9 1.9 %collective-permute-start.9 = (bf16[2,256,256]{2,1,0:T(8,128)(2,1)}, bf16[2,256,256]{2,1,0:T(8,128)(2,1)S(1)}, u32[]{:S(2)}, u32[]{:S(2)}) collective-permute-start(bf16[2,256,256]{2,1,0:T(8,128)(2,1)} %get-tuple-element.45), channel_id=1, source_target_pairs={{0,6},{1,7},{2,4},{3,5},{4,10},{5,11},{6,8},{7,9},{8,14},{9,15},{1... | collective-permute-start | bytes 786440 | tf_op jit(solution)/shard_map/ppermute | solution.py:426
  25.8 2.9 %collective-permute-done.6.far_ref = bf16[3,512,128]{2,1,0:T(8,128)(2,1)S(1)} collective-permute-done((bf16[3,512,128]{2,1,0:T(8,128)(2,1)S(1)}, bf16[3,512,128]{2,1,0:T(8,128)(2,1)S(1)}, u32[]{:S(2)}, u32[]{:S(2)}) %collective-permute-start.6) | collective-permute-done | bytes 393248 | tf_op jit(solution)/shard_map/ppermute | solution.py:213
  28.7 1.5 %shard_map.94.taps_ref = f32[2,4,512,256]{3,2,1,0:T(8,128)S(1)} custom-call(bf16[512,256]{1,0:T(8,128)(2,1)S(1)} %copy-done.1, bf16[512,256]{1,0:T(8,128)(2,1)S(1)} %copy-done.2, bf16[1024,128]{1,0:T(8,128)(2,1)S(1)} %copy-done.8, bf16[3,512,128]{2,1,0:T(8,128)(2,1)S(1)} %shard_map.93.near_ref, bf16[3,512,128]{2,1,0:T(8,128)(2,1)S(1)} %collective-permute-done.6.far_ref), custom_call_target="tpu_custom_call" | custom-call | flops 1000 | bytes 1000 | tf_op jit(solution)/shard_map/pallas_call | solution.py:214
  30.2 3.0 %shard_map.96 = (f32[2,3,512,256]{3,2,1,0:T(8,128)S(1)}, f32[2,512,256]{2,1,0:T(8,128)S(1)}) custom-call(bf16[512,256]{1,0:T(8,128)(2,1)S(1)} %copy-done.1, bf16[512,256]{1,0:T(8,128)(2,1)S(1)} %copy-done.2, f32[2,4,512,256]{3,2,1,0:T(8,128)S(1)} %shard_map.94.taps_ref, bf16[2,2,256,256]{3,2,1,0:T(8,128)(2,1)S(1)} %get-tuple-element.41.mine_ref, ...), custom_call_target="tpu_custom_call" | custom-call | flops 1000 | bytes 1000 | tf_op jit(solution)/shard_map/pallas_call | solution.py:287
  33.1 6.9 %collective-permute-done.13.beyond_ref = bf16[2,256,256]{2,1,0:T(8,128)(2,1)} collective-permute-done((bf16[2,256,256]{2,1,0:T(8,128)(2,1)}, bf16[2,256,256]{2,1,0:T(8,128)(2,1)}, u32[]{:S(2)}, u32[]{:S(2)}) %collective-permute-start.13) | collective-permute-done | bytes 262176 | tf_op jit(solution)/shard_map/ppermute | solution.py:426
  40.1 3.9 %shard_map.98 = (bf16[256,256]{1,0:T(8,128)(2,1)S(1)}, bf16[256,256]{1,0:T(8,128)(2,1)S(1)}, bf16[256,256]{1,0:T(8,128)(2,1)S(1)}, bf16[256,256]{1,0:T(8,128)(2,1)S(1)}) custom-call(bf16[512,256]{1,0:T(8,128)(2,1)S(1)} %copy-done.1, bf16[512,256]{1,0:T(8,128)(2,1)S(1)} %copy-done.2, bf16[256,512]{1,0:T(8,128)(2,1)S(1)} %copy-done.4, ...), custom_call_target="tpu_custom_call" | custom-call | flops 1000 | bytes 1000 | tf_op jit(solution)/shard_map/pallas_call | solution.py:358
  44.0 0.6 collective-permute-start.15
  44.6 1.3 %collective-permute-start.16 = (bf16[256,256]{1,0:T(8,128)(2,1)S(1)}, bf16[256,256]{1,0:T(8,128)(2,1)S(1)}, u32[]{:S(2)}, u32[]{:S(2)}) collective-permute-start(bf16[256,256]{1,0:T(8,128)(2,1)S(1)} %get-tuple-element.54), channel_id=1, source_target_pairs={{0,3},{1,2},{2,1},{3,0},{4,7},{5,6},{6,5},{7,4},{8,11},{9,10},{10,... | collective-permute-start | bytes 393224 | tf_op jit(solution)/shard_map/ppermute | solution.py:426
  45.9 2.9 %shard_map.97 = (bf16[256,256]{1,0:T(8,128)(2,1)S(1)}, bf16[256,256]{1,0:T(8,128)(2,1)S(1)}, bf16[256,256]{1,0:T(8,128)(2,1)S(1)}, bf16[256,256]{1,0:T(8,128)(2,1)S(1)}) custom-call(bf16[512,256]{1,0:T(8,128)(2,1)S(1)} %copy-done.1, bf16[512,256]{1,0:T(8,128)(2,1)S(1)} %copy-done.2, bf16[256,512]{1,0:T(8,128)(2,1)S(1)} %copy-done.4, ...), custom_call_target="tpu_custom_call" | custom-call | flops 1000 | bytes 1000 | tf_op jit(solution)/shard_map/pallas_call | solution.py:358
  48.8 0.4 collective-permute-start.10
  49.2 0.5 collective-permute-start.11
  49.7 1.0 %collective-permute-start.12 = (bf16[256,256]{1,0:T(8,128)(2,1)S(1)}, bf16[256,256]{1,0:T(8,128)(2,1)S(1)}, u32[]{:S(2)}, u32[]{:S(2)}) collective-permute-start(bf16[256,256]{1,0:T(8,128)(2,1)S(1)} %get-tuple-element.49), channel_id=1, source_target_pairs={{0,3},{1,2},{2,1},{3,0},{4,7},{5,6},{6,5},{7,4},{8,11},{9,10},{10,... | collective-permute-start | bytes 393224 | tf_op jit(solution)/shard_map/ppermute | solution.py:426
  50.8 1.6 %collective-permute-done.16.refs_3_ = bf16[256,256]{1,0:T(8,128)(2,1)S(1)} collective-permute-done((bf16[256,256]{1,0:T(8,128)(2,1)S(1)}, bf16[256,256]{1,0:T(8,128)(2,1)S(1)}, u32[]{:S(2)}, u32[]{:S(2)}) %collective-permute-start.16) | collective-permute-done | bytes 131104 | tf_op jit(solution)/shard_map/ppermute | solution.py:426
  52.3 1.1 %shard_map.99.refs_4_ = bf16[256,2048]{1,0:T(8,128)(2,1)} custom-call(bf16[256,2048]{1,0:T(8,128)(2,1)S(1)} %copy-done.3, bf16[256,256]{1,0:T(8,128)(2,1)S(1)} %get-tuple-element.51.refs_0_, bf16[256,256]{1,0:T(8,128)(2,1)S(1)} %collective-permute-done.14.refs_1_, bf16[256,256]{1,0:T(8,128)(2,1)S(1)} %collective-permute-done.15.refs_2_, ...), custom_call_target="tpu_custom_call" | custom-call | flops 1000 | bytes 1000 | tf_op jit(solution)/shard_map/pallas_call | solution.py:398
  53.4 2.6 %collective-permute-done.11.refs_2_ = bf16[256,256]{1,0:T(8,128)(2,1)S(1)} collective-permute-done((bf16[256,256]{1,0:T(8,128)(2,1)S(1)}, bf16[256,256]{1,0:T(8,128)(2,1)S(1)}, u32[]{:S(2)}, u32[]{:S(2)}) %collective-permute-start.11) | collective-permute-done | bytes 131104 | tf_op jit(solution)/shard_map/ppermute | solution.py:426
  56.0 1.9 %collective-permute-done.12.refs_3_ = bf16[256,256]{1,0:T(8,128)(2,1)S(1)} collective-permute-done((bf16[256,256]{1,0:T(8,128)(2,1)S(1)}, bf16[256,256]{1,0:T(8,128)(2,1)S(1)}, u32[]{:S(2)}, u32[]{:S(2)}) %collective-permute-start.12) | collective-permute-done | bytes 131104 | tf_op jit(solution)/shard_map/ppermute | solution.py:426
  57.9 1.1 %shard_map.100 = bf16[256,2048]{1,0:T(8,128)(2,1)} custom-call(bf16[256,2048]{1,0:T(8,128)(2,1)S(1)} %copy-done.3, bf16[256,256]{1,0:T(8,128)(2,1)S(1)} %get-tuple-element.46.refs_0_, bf16[256,256]{1,0:T(8,128)(2,1)S(1)} %collective-permute-done.10.refs_1_, bf16[256,256]{1,0:T(8,128)(2,1)S(1)} %collective-permute-done.11.refs_2_, ...), custom_call_target="tpu_custom_call", output_to_operand_aliasing={{}: (5, {})} | custom-call | flops 1000 | bytes 1000 | tf_op jit(solution)/shard_map/pallas_call | solution.py:398
  (32 shorter events, 0.3 us)
Async XLA Ops:
  0.0 25.8 %copy-start = (f32[2048]{0:T(1024)S(1)}, f32[2048]{0:T(1024)}, u32[]{:S(2)}) copy-start(f32[2048]{0:T(1024)} %param.13) | copy-start | bytes 24580
  0.0 28.7 %copy-start.1 = (bf16[512,256]{1,0:T(8,128)(2,1)S(1)}, bf16[512,256]{1,0:T(8,128)(2,1)}, u32[]{:S(2)}) copy-start(bf16[512,256]{1,0:T(8,128)(2,1)} %constant.32.clone.high_ref) | copy-start | bytes 786436
  0.0 28.7 %copy-start.2 = (bf16[512,256]{1,0:T(8,128)(2,1)S(1)}, bf16[512,256]{1,0:T(8,128)(2,1)}, u32[]{:S(2)}) copy-start(bf16[512,256]{1,0:T(8,128)(2,1)} %constant.33.clone.low_ref) | copy-start | bytes 786436
  1.0 10.4 %collective-permute-start = (bf16[1,512,128]{2,1,0:T(8,128)(2,1)S(1)}, bf16[1,512,128]{2,1,0:T(8,128)(2,1)S(1)}, u32[]{:S(2)}, u32[]{:S(2)}) collective-permute-start(bf16[1,512,128]{2,1,0:T(8,128)(2,1)S(1)} %dynamic-slice_bitcast_fusion.half_ref.refs_0_), channel_id=1, source_target_pairs={{0,8},{1,9},{2,10},{3,11},{4,12},{5,13},{6,14},{7,15},{8,0},{9,1},... | collective-permute-start | bytes 393224 | tf_op jit(solution)/shard_map/ppermute | solution.py:430
  5.1 1.2 %copy-start.6 = (bf16[256,2048]{1,0:T(8,128)(2,1)S(1)}, bf16[256,2048]{1,0:T(8,128)(2,1)}, u32[]{:S(2)}) copy-start(bf16[256,2048]{1,0:T(8,128)(2,1)} %gate_hbm.1) | copy-start | bytes 3145732
  6.3 1.2 %copy-start.7 = (bf16[256,2048]{1,0:T(8,128)(2,1)S(1)}, bf16[256,2048]{1,0:T(8,128)(2,1)}, u32[]{:S(2)}) copy-start(bf16[256,2048]{1,0:T(8,128)(2,1)} %values_hbm.1) | copy-start | bytes 3145732
  7.6 21.1 %copy-start.8 = (bf16[1024,128]{1,0:T(8,128)(2,1)S(1)}, bf16[1024,128]{1,0:T(8,128)(2,1)}, u32[]{:S(2)}) copy-start(bf16[1024,128]{1,0:T(8,128)(2,1)} %own_ref.1) | copy-start | bytes 786436
  8.3 3.1 %collective-permute-start.1 = (bf16[256,256]{1,0:T(8,128)(2,1)S(1)}, bf16[256,256]{1,0:T(8,128)(2,1)S(1)}, u32[]{:S(2)}, u32[]{:S(2)}) collective-permute-start(bf16[256,256]{1,0:T(8,128)(2,1)S(1)} %get-tuple-element.30), channel_id=1, source_target_pairs={{0,1},{1,0},{2,3},{3,2},{4,5},{5,4},{6,7},{7,6},{8,9},{9,8},{10,11... | collective-permute-start | bytes 393224 | tf_op jit(solution)/shard_map/ppermute | solution.py:426
  8.4 3.0 %collective-permute-start.2 = (bf16[256,256]{1,0:T(8,128)(2,1)S(1)}, bf16[256,256]{1,0:T(8,128)(2,1)S(1)}, u32[]{:S(2)}, u32[]{:S(2)}) collective-permute-start(bf16[256,256]{1,0:T(8,128)(2,1)S(1)} %get-tuple-element.31), channel_id=1, source_target_pairs={{0,1},{1,0},{2,3},{3,2},{4,5},{5,4},{6,7},{7,6},{8,9},{9,8},{10,11... | collective-permute-start | bytes 393224 | tf_op jit(solution)/shard_map/ppermute | solution.py:426
  8.9 2.5 %collective-permute-start.3 = (bf16[256,256]{1,0:T(8,128)(2,1)S(1)}, bf16[256,256]{1,0:T(8,128)(2,1)S(1)}, u32[]{:S(2)}, u32[]{:S(2)}) collective-permute-start(bf16[256,256]{1,0:T(8,128)(2,1)S(1)} %get-tuple-element.32), channel_id=1, source_target_pairs={{0,1},{1,0},{2,3},{3,2},{4,5},{5,4},{6,7},{7,6},{8,9},{9,8},{10,11... | collective-permute-start | bytes 393224 | tf_op jit(solution)/shard_map/ppermute | solution.py:426
  9.0 2.4 %collective-permute-start.4 = (bf16[256,256]{1,0:T(8,128)(2,1)S(1)}, bf16[256,256]{1,0:T(8,128)(2,1)S(1)}, u32[]{:S(2)}, u32[]{:S(2)}) collective-permute-start(bf16[256,256]{1,0:T(8,128)(2,1)S(1)} %get-tuple-element.33), channel_id=1, source_target_pairs={{0,1},{1,0},{2,3},{3,2},{4,5},{5,4},{6,7},{7,6},{8,9},{9,8},{10,11... | collective-permute-start | bytes 393224 | tf_op jit(solution)/shard_map/ppermute | solution.py:426
  11.5 7.6 %collective-permute-start.5 = (bf16[2,512,128]{2,1,0:T(8,128)(2,1)S(1)}, bf16[2,512,128]{2,1,0:T(8,128)(2,1)S(1)}, u32[]{:S(2)}, u32[]{:S(2)}) collective-permute-start(bf16[2,512,128]{2,1,0:T(8,128)(2,1)S(1)} %shard_map.92), channel_id=1, source_target_pairs={{0,4},{1,5},{2,6},{3,7},{4,0},{5,1},{6,2},{7,3},{8,12},{9,13},{10,... | collective-permute-start | bytes 786440 | tf_op jit(solution)/shard_map/ppermute | solution.py:430
  13.3 16.9 %collective-permute-start.7 = (bf16[2,2,256,256]{3,2,1,0:T(8,128)(2,1)}, bf16[2,2,256,256]{3,2,1,0:T(8,128)(2,1)S(1)}, u32[]{:S(2)}, u32[]{:S(2)}) collective-permute-start(bf16[2,2,256,256]{3,2,1,0:T(8,128)(2,1)} %get-tuple-element.42), channel_id=1, source_target_pairs={{0,2},{1,3},{2,0},{3,1},{4,6},{5,7},{6,4},{7,5},{8,10},{9,11},{10,... | collective-permute-start | bytes 1572872 | tf_op jit(solution)/shard_map/ppermute | solution.py:426
  14.8 25.3 %collective-permute-start.8 = (bf16[2,2,256,256]{3,2,1,0:T(8,128)(2,1)S(1)}, bf16[2,2,256,256]{3,2,1,0:T(8,128)(2,1)S(1)}, u32[]{:S(2)}, u32[]{:S(2)}) collective-permute-start(bf16[2,2,256,256]{3,2,1,0:T(8,128)(2,1)S(1)} %get-tuple-element.41.mine_ref), channel_id=1, source_target_pairs={{0,4},{1,5},{2,6},{3,7},{4,8},{5,9},{6,10},{7,11},{8,12},{9,13},{1... | collective-permute-start | bytes 1572872 | tf_op jit(solution)/shard_map/ppermute | solution.py:426
  19.1 9.6 %collective-permute-start.6 = (bf16[3,512,128]{2,1,0:T(8,128)(2,1)S(1)}, bf16[3,512,128]{2,1,0:T(8,128)(2,1)S(1)}, u32[]{:S(2)}, u32[]{:S(2)}) collective-permute-start(bf16[3,512,128]{2,1,0:T(8,128)(2,1)S(1)} %shard_map.93.near_ref), channel_id=1, source_target_pairs={{0,16},{16,0},{1,17},{17,1},{2,18},{18,2},{3,19},{19,3},{4,20},{20... | collective-permute-start | bytes 1179656 | tf_op jit(solution)/shard_map/ppermute | solution.py:213
  20.7 19.4 %collective-permute-start.13 = (bf16[2,256,256]{2,1,0:T(8,128)(2,1)}, bf16[2,256,256]{2,1,0:T(8,128)(2,1)}, u32[]{:S(2)}, u32[]{:S(2)}) collective-permute-start(bf16[2,256,256]{2,1,0:T(8,128)(2,1)} %get-tuple-element.50), channel_id=1, source_target_pairs={{0,6},{1,7},{2,4},{3,5},{4,10},{5,11},{6,8},{7,9},{8,14},{9,15},{1... | collective-permute-start | bytes 786440 | tf_op jit(solution)/shard_map/ppermute | solution.py:426
  23.9 22.0 %collective-permute-start.9 = (bf16[2,256,256]{2,1,0:T(8,128)(2,1)}, bf16[2,256,256]{2,1,0:T(8,128)(2,1)S(1)}, u32[]{:S(2)}, u32[]{:S(2)}) collective-permute-start(bf16[2,256,256]{2,1,0:T(8,128)(2,1)} %get-tuple-element.45), channel_id=1, source_target_pairs={{0,6},{1,7},{2,4},{3,5},{4,10},{5,11},{6,8},{7,9},{8,14},{9,15},{1... | collective-permute-start | bytes 786440 | tf_op jit(solution)/shard_map/ppermute | solution.py:426
  30.1 9.9 %copy-start.4 = (bf16[256,512]{1,0:T(8,128)(2,1)S(1)}, bf16[256,512]{1,0:T(8,128)(2,1)}, u32[]{:S(2)}) copy-start(bf16[256,512]{1,0:T(8,128)(2,1)} %constant.34.clone.back_high_ref) | copy-start | bytes 786436
  30.2 9.9 %copy-start.5 = (bf16[256,512]{1,0:T(8,128)(2,1)S(1)}, bf16[256,512]{1,0:T(8,128)(2,1)}, u32[]{:S(2)}) copy-start(bf16[256,512]{1,0:T(8,128)(2,1)} %constant.35.clone.back_low_ref) | copy-start | bytes 786436
  44.0 5.8 %collective-permute-start.14 = (bf16[256,256]{1,0:T(8,128)(2,1)S(1)}, bf16[256,256]{1,0:T(8,128)(2,1)S(1)}, u32[]{:S(2)}, u32[]{:S(2)}) collective-permute-start(bf16[256,256]{1,0:T(8,128)(2,1)S(1)} %get-tuple-element.52), channel_id=1, source_target_pairs={{0,1},{1,0},{2,3},{3,2},{4,5},{5,4},{6,7},{7,6},{8,9},{9,8},{10,11... | collective-permute-start | bytes 393224 | tf_op jit(solution)/shard_map/ppermute | solution.py:426
  44.0 6.7 %collective-permute-start.15 = (bf16[256,256]{1,0:T(8,128)(2,1)S(1)}, bf16[256,256]{1,0:T(8,128)(2,1)S(1)}, u32[]{:S(2)}, u32[]{:S(2)}) collective-permute-start(bf16[256,256]{1,0:T(8,128)(2,1)S(1)} %get-tuple-element.53), channel_id=1, source_target_pairs={{0,2},{1,3},{2,0},{3,1},{4,6},{5,7},{6,4},{7,5},{8,10},{9,11},{10,... | collective-permute-start | bytes 393224 | tf_op jit(solution)/shard_map/ppermute | solution.py:426
  44.6 7.7 %copy-start.3 = (bf16[256,2048]{1,0:T(8,128)(2,1)S(1)}, bf16[256,2048]{1,0:T(8,128)(2,1)}, u32[]{:S(2)}) copy-start(bf16[256,2048]{1,0:T(8,128)(2,1)} %gate_ref.3) | copy-start | bytes 3145732
  44.6 7.7 %collective-permute-start.16 = (bf16[256,256]{1,0:T(8,128)(2,1)S(1)}, bf16[256,256]{1,0:T(8,128)(2,1)S(1)}, u32[]{:S(2)}, u32[]{:S(2)}) collective-permute-start(bf16[256,256]{1,0:T(8,128)(2,1)S(1)} %get-tuple-element.54), channel_id=1, source_target_pairs={{0,3},{1,2},{2,1},{3,0},{4,7},{5,6},{6,5},{7,4},{8,11},{9,10},{10,... | collective-permute-start | bytes 393224 | tf_op jit(solution)/shard_map/ppermute | solution.py:426
  48.8 4.6 %collective-permute-start.10 = (bf16[256,256]{1,0:T(8,128)(2,1)S(1)}, bf16[256,256]{1,0:T(8,128)(2,1)S(1)}, u32[]{:S(2)}, u32[]{:S(2)}) collective-permute-start(bf16[256,256]{1,0:T(8,128)(2,1)S(1)} %get-tuple-element.47), channel_id=1, source_target_pairs={{0,1},{1,0},{2,3},{3,2},{4,5},{5,4},{6,7},{7,6},{8,9},{9,8},{10,11... | collective-permute-start | bytes 393224 | tf_op jit(solution)/shard_map/ppermute | solution.py:426
  49.2 6.8 %collective-permute-start.11 = (bf16[256,256]{1,0:T(8,128)(2,1)S(1)}, bf16[256,256]{1,0:T(8,128)(2,1)S(1)}, u32[]{:S(2)}, u32[]{:S(2)}) collective-permute-start(bf16[256,256]{1,0:T(8,128)(2,1)S(1)} %get-tuple-element.48), channel_id=1, source_target_pairs={{0,2},{1,3},{2,0},{3,1},{4,6},{5,7},{6,4},{7,5},{8,10},{9,11},{10,... | collective-permute-start | bytes 393224 | tf_op jit(solution)/shard_map/ppermute | solution.py:426
  49.7 8.2 %collective-permute-start.12 = (bf16[256,256]{1,0:T(8,128)(2,1)S(1)}, bf16[256,256]{1,0:T(8,128)(2,1)S(1)}, u32[]{:S(2)}, u32[]{:S(2)}) collective-permute-start(bf16[256,256]{1,0:T(8,128)(2,1)S(1)} %get-tuple-element.49), channel_id=1, source_target_pairs={{0,3},{1,2},{2,1},{3,0},{4,7},{5,6},{6,5},{7,4},{8,11},{9,10},{10,... | collective-permute-start | bytes 393224 | tf_op jit(solution)/shard_map/ppermute | solution.py:426

commit v3 on v2

--- a/solution.py
+++ b/solution.py
@@ -118,7 +118,7 @@
         scratch_shapes=[pltpu.VMEM((rows, channels), BF16)] * 2 + [pltpu.SemaphoreType.DMA((2, count))],
         compiler_params=params(8),
         cost_estimate=SMALL,
-    )(gate_in, values, half)
+    )(*(pltpu.with_memory_space_constraint(x, pltpu.HBM) for x in (gate_in, values)), half)
 
 
 def pack_kernel(same_ref, other_ref, *refs):
@@ -180,9 +180,8 @@
     taps[:, aligned(layer, LANES)] = own_ref[...]
     for apart in range(1, layers):
         lanes = aligned(layer ^ apart, LANES)
-        at = (None, 0, 2, 1)[apart]
-        taps[near, lanes] = near_ref[at]
-        taps[far, lanes] = far_ref[at]
+        taps[near, lanes] = near_ref[apart - 1]
+        taps[far, lanes] = far_ref[apart - 1]
     put_tap_spectra(high_ref, low_ref, taps, out_ref)
 
 
@@ -256,7 +255,7 @@
 
 
 def own_kernel(
-    members, high_ref, low_ref, taps_ref, mine_ref, across_ref, part_ref, first_ref, spectra
+    members, high_ref, low_ref, taps_ref, mine_ref, ahead_ref, across_ref, part_ref, first_ref, halo_ref, spectra
 ):
     member, _ = place(members)
     rows = high_ref.shape[1]
@@ -265,6 +264,9 @@
         for apart, block in enumerate(blocks):
             spectra[member ^ apart] = matmul(high_ref[...], block) + matmul(low_ref[...], block)
         first_ref[part] = spectra[0]
+        for apart in range(2):
+            block = ahead_ref[part, apart]
+            halo_ref[part, member ^ apart] = matmul(high_ref[...], block) + matmul(low_ref[...], block)
 
         def body(at, sign):
             read = reader(spectra, rows, at, 8)
@@ -280,22 +282,23 @@
         for_bins(rows, 8, body)
 
 
-def own_partials(tables, taps, mine, across):
+def own_partials(tables, taps, *blocks):
     members = taps.shape[1]
     chunk = taps.shape[-1]
     rows = tables[0].shape[1]
     return pl.pallas_call(
         functools.partial(own_kernel, members),
-        in_specs=[VMEM] * 5,
-        out_specs=[VMEM] * 2,
+        in_specs=[VMEM] * 6,
+        out_specs=[VMEM] * 3,
         out_shape=[
             jax.ShapeDtypeStruct((CHUNKS, members - 1, 2 * rows, chunk), F32),
             jax.ShapeDtypeStruct((CHUNKS, 2 * rows, chunk), F32),
+            jax.ShapeDtypeStruct((CHUNKS, members, 2 * rows, chunk), F32),
         ],
         scratch_shapes=[pltpu.VMEM((members, 2 * rows, chunk), F32)],
         compiler_params=params(20),
         cost_estimate=SMALL,
-    )(*tables, taps, mine, across)
+    )(*tables, taps, *blocks)
 
 
 def mix_kernel(
@@ -311,15 +314,28 @@
     first_ref,
     mine_ref,
     across_ref,
-    ahead_ref,
     beyond_ref,
+    _,
     *refs,
 ):
-    out_refs, (halo, sums) = refs[:members], refs[members:]
+    out_refs, (halo_ref, sums) = refs[:members], refs[members:]
+    halo = halo_ref.at[part]
+
+    def skip_of(part):
+        chunk = out_refs[0].shape[1]
+        if skip_ref.shape[1] == chunk:
+            return skip_ref[pl.ds(part, 1), :]
+        shares = skip_ref.shape[1] // (members * LANES) // CHUNKS
+        picked = [
+            skip_ref[:, aligned((part * shares + layer) * members + member, LANES)]
+            for layer in range(shares)
+        ]
+        return jnp.concatenate(picked, axis=1)
+
     member, _ = place(members)
     rows = high_ref.shape[1]
-    halo_blocks = [ahead_ref[part, 0], ahead_ref[part, 1], beyond_ref[0], beyond_ref[1]]
-    for apart, block in enumerate(halo_blocks):
+    for apart in range(2, members):
+        block = beyond_ref[apart - 2]
         halo[member ^ apart] = matmul(high_ref[...], block) + matmul(low_ref[...], block)
 
     def body(at, sign):
@@ -341,6 +357,7 @@
 
     for_bins(rows, 8, body)
     blocks = [mine_ref[part, 0], mine_ref[part, 1], across_ref[part, 0], across_ref[part, 1]]
+    skip = skip_of(part)
     for apart, block in enumerate(blocks):
         total = sums[member ^ apart]
         high = total.astype(BF16)
@@ -348,22 +365,26 @@
         convolved = matmul(back_high_ref[...], high) + (
             matmul(back_high_ref[...], low) + matmul(back_low_ref[...], high)
         )
-        mixed = convolved + skip_ref[part] * block.astype(F32)
+        mixed = convolved + skip * block.astype(F32)
         out_refs[apart][...] = mixed.astype(BF16)
 
 
-def mixed_pieces(part, tables, back_tables, skip, taps, partial, first, *blocks):
+def mixed_pieces(part, tables, back_tables, skip, taps, partial, first, mine, across, beyond, halo):
     members, chunk = taps.shape[1], taps.shape[-1]
     rows = tables[0].shape[1]
-    return pl.pallas_call(
+    operands = [*tables, *back_tables, skip, taps, partial, first, mine, across]
+    *pieces, halo = pl.pallas_call(
         functools.partial(mix_kernel, members, part),
-        in_specs=[VMEM] * 12,
-        out_specs=[VMEM] * members,
-        out_shape=[jax.ShapeDtypeStruct((rows, chunk), BF16)] * members,
-        scratch_shapes=[pltpu.VMEM((members, 2 * rows, chunk), F32)] * 2,
+        in_specs=[VMEM] * (len(operands) + 2),
+        out_specs=[VMEM] * (members + 1),
+        out_shape=[jax.ShapeDtypeStruct((rows, chunk), BF16)] * members
+        + [jax.ShapeDtypeStruct(halo.shape, F32)],
+        input_output_aliases={len(operands) + 1: members},
+        scratch_shapes=[pltpu.VMEM((members, 2 * rows, chunk), F32)],
         compiler_params=params(20),
         cost_estimate=SMALL,
-    )(*tables, *back_tables, skip, taps, partial, first, *blocks)
+    )(*operands, beyond, halo)
+    return pieces, halo
 
 
 def gate_kernel(layers, members, part, gate_ref, *refs):
@@ -430,28 +451,30 @@
         return lax.ppermute(value, "ctx", pairs)
 
     half = near_half(filter_taps, layers, lax.axis_size("groups"))
-    near = None
+    near = one_away = None
     if half is not None:
-        two_away = to_layer(half, 2)
-    same, other, *send = product_pieces(gate_in, values, half, layers, members)
+        two_away, one_away = to_layer(half, 2), to_layer(half, 1)
+    same, other, *send = product_pieces(gate_in, values, one_away, layers, members)
     core = [to_member(piece, 1, 0) for piece in send]
     if half is not None:
         two_away, core = lax.optimization_barrier((two_away, core))
     mine, to_across, *to_beyond = payloads(same, other, core)
     if half is not None:
-        one_and_three_away = to_layer(joined([half, two_away]), 1)
-        near = joined([one_and_three_away, two_away])
+        three_away = to_layer(two_away, 1)
+        near = joined([one_away, two_away, three_away])
     ahead = to_member(mine, 0, 1)
     beyond = [to_member(piece, 2, 1) for piece in to_beyond]
     across = to_member(to_across, 2, 0)
     taps = tap_spectra(tables, filter_taps, near, layers, members)
-    partial, first = own_partials(tables, taps, mine, across)
-    skip = skip_gain.reshape(layers, members, width)
-    skip = lax.dynamic_index_in_dim(skip, member, 1, False).reshape(CHUNKS, 1, channels // members // CHUNKS)
+    partial, first, spectra = own_partials(tables, taps, mine, ahead, across)
+    skip = skip_gain.reshape(1, channels)
+    if width != LANES:
+        skip = skip_gain.reshape(layers, members, width)
+        skip = lax.dynamic_index_in_dim(skip, member, 1, False).reshape(CHUNKS, -1)
     out = None
     for part in range(CHUNKS):
-        mixed = mixed_pieces(
-            part, tables, back_tables, skip, taps, partial, first, mine, across, ahead, beyond[part]
+        mixed, spectra = mixed_pieces(
+            part, tables, back_tables, skip, taps, partial, first, mine, across, beyond[part], spectra
         )
         mixed = [mixed[0]] + [to_member(mixed[d], d, 0) for d in range(1, members)]
         out = gated_output(part, gate_out, mixed, layers, members, out)

time: 59.2 us -> 56.8 us (0.959)
  local copies, waits for them, and re-layouts: 3.46 us -> 1.02 us
  Pallas kernels: 15.2 us -> 14.1 us
  starting transfers between devices: 19.4 us -> 20.2 us
    unnamed x18 -> x14, local copies, waits for them, and re-layouts: 2.48 us -> 0.03 us
    ppermute x1, waiting for transfers between devices: 2.87 us -> 5.05 us  [tap_spectra(): far = lax.ppermute(near, 'groups', [(0, 1), (1, 0)])]
    ppermute x14, waiting for transfers between devices: 13.1 us -> 11.1 us  [to_member(): return lax.ppermute(value, 'ctx', pairs)]
    pallas_call x2, Pallas kernels: 6.76 us -> 5.15 us  [mixed_pieces(): pl.pallas_call(functools.partial(mix_kernel, members, part), in_specs=[VM...]
    ppermute x2 -> x3, starting transfers between devices: 4.9 us -> 6.06 us  [to_layer(): return lax.ppermute(value, 'ctx', pairs)]
    pallas_call x1, Pallas kernels: 1.03 us -> 0.1 us  [payloads(): pl.pallas_call(pack_kernel, in_specs=[VMEM] * (2 + len(core)), out_specs=...]
    pallas_call x1, Pallas kernels: 0.78 us -> 1.71 us  [product_pieces(): pl.pallas_call(functools.partial(product_kernel, layers, members), in_spe...]
    ppermute x14, starting transfers between devices: 12.9 us -> 12.3 us  [to_member(): return lax.ppermute(value, 'ctx', pairs)]
  transfers between devices with their start and end apart: 17 -> 18, of which waited for: 7 -> 12; matrix products, arithmetic and copies ran while one was open for 0% -> 0% of each run, Pallas kernels for 24% -> 23%
where the time goes in v3:
time: 56.8 us; the launch traced here: 56.7 us
  waiting for transfers between devices  21.2 us (37%)
  starting transfers between devices  20.2 us (36%)
  Pallas kernels  14.1 us (25%)
  local copies, waits for them, and re-layouts  1.02 us (2%)
    ppermute x14, starting transfers between devices, to_member(): return lax.ppermute(value, 'ctx', pairs)  12.3 us
    ppermute x14, waiting for transfers between devices, to_member(): return lax.ppermute(value, 'ctx', pairs)  11.1 us
    ppermute x3, starting transfers between devices, to_layer(): return lax.ppermute(value, 'ctx', pairs)  6.06 us
    pallas_call x2, Pallas kernels, mixed_pieces(): pl.pallas_call(functools.partial(mix_kernel, members, part), in_specs=[VM...  5.15 us
    ppermute x1, waiting for transfers between devices, tap_spectra(): far = lax.ppermute(near, 'groups', [(0, 1), (1, 0)])  5.05 us
    ppermute x3, waiting for transfers between devices, to_layer(): return lax.ppermute(value, 'ctx', pairs)  5 us
    pallas_call x1, Pallas kernels, own_partials(): pl.pallas_call(functools.partial(own_kernel, members), in_specs=[VMEM] *...  3.57 us
    pallas_call x2, Pallas kernels, gated_output(): pl.pallas_call(functools.partial(gate_kernel, layers // CHUNKS, members,...  2.13 us
  transfers between devices with their start and end apart: 18, of which 12 were waited for; matrix products, arithmetic and copies ran while one was open for 0% of the time, Pallas kernels for 23%

profile of v3, /device:TPU:0, one launch (start us, length us, event | category | flops | bytes accessed | tf_op | source)
XLA Modules:
  0.0 56.7 jit_solution(16189577586708509379)
XLA Ops:
  0.0 1.0 %dynamic-slice_bitcast_fusion = bf16[1,512,128]{2,1,0:T(8,128)(2,1)S(1)} fusion(bf16[1024,128]{1,0:T(8,128)(2,1)} %own_ref.1, s32[]{:T(128)S(6)} %select_n.3), kind=kLoop, calls=%fused_computation | loop fusion | bytes 262148 | tf_op jit(solution)/shard_map/broadcast_in_dim | solution.py:193
  1.0 3.1 %collective-permute-start = (bf16[1,512,128]{2,1,0:T(8,128)(2,1)S(1)}, bf16[1,512,128]{2,1,0:T(8,128)(2,1)S(1)}, u32[]{:S(2)}, u32[]{:S(2)}) collective-permute-start(bf16[1,512,128]{2,1,0:T(8,128)(2,1)S(1)} %dynamic-slice_bitcast_fusion), channel_id=1, source_target_pairs={{0,4},{1,5},{2,6},{3,7},{4,0},{5,1},{6,2},{7,3},{8,12},{9,13},{10,... | collective-permute-start | bytes 393224 | tf_op jit(solution)/shard_map/ppermute | solution.py:451
  4.1 2.6 %collective-permute-start.1 = (bf16[1,512,128]{2,1,0:T(8,128)(2,1)S(1)}, bf16[1,512,128]{2,1,0:T(8,128)(2,1)S(1)}, u32[]{:S(2)}, u32[]{:S(2)}) collective-permute-start(bf16[1,512,128]{2,1,0:T(8,128)(2,1)S(1)} %dynamic-slice_bitcast_fusion), channel_id=1, source_target_pairs={{0,8},{1,9},{2,10},{3,11},{4,12},{5,13},{6,14},{7,15},{8,0},{9,1},... | collective-permute-start | bytes 393224 | tf_op jit(solution)/shard_map/ppermute | solution.py:451
  6.7 2.8 %collective-permute-done.half_ref.refs_0_ = bf16[1,512,128]{2,1,0:T(8,128)(2,1)S(1)} collective-permute-done((bf16[1,512,128]{2,1,0:T(8,128)(2,1)S(1)}, bf16[1,512,128]{2,1,0:T(8,128)(2,1)S(1)}, u32[]{:S(2)}, u32[]{:S(2)}) %collective-permute-start) | collective-permute-done | bytes 131104 | tf_op jit(solution)/shard_map/ppermute | solution.py:451
  9.4 1.7 %shard_map.91 = (bf16[2,256,256]{2,1,0:T(8,128)(2,1)S(1)}, bf16[2,256,256]{2,1,0:T(8,128)(2,1)S(1)}, bf16[256,256]{1,0:T(8,128)(2,1)S(1)}, bf16[256,256]{1,0:T(8...) custom-call(bf16[256,2048]{1,0:T(8,128)(2,1)} %gate_hbm.1, bf16[256,2048]{1,0:T(8,128)(2,1)} %values_hbm.1, ...), custom_call_target="tpu_custom_call" | custom-call | flops 1000 | bytes 1000 | tf_op jit(solution)/shard_map/pallas_call | solution.py:112
  11.2 0.5 collective-permute-start.3
  11.8 0.4 collective-permute-start.5
  12.2 0.6 %collective-permute-done.1.refs_1_ = bf16[1,512,128]{2,1,0:T(8,128)(2,1)S(1)} collective-permute-done((bf16[1,512,128]{2,1,0:T(8,128)(2,1)S(1)}, bf16[1,512,128]{2,1,0:T(8,128)(2,1)S(1)}, u32[]{:S(2)}, u32[]{:S(2)}) %collective-permute-start.1) | collective-permute-done | bytes 131104 | tf_op jit(solution)/shard_map/ppermute | solution.py:451
  13.3 0.4 collective-permute-start.6
  13.7 1.6 %collective-permute-start.9 = (bf16[2,2,256,256]{3,2,1,0:T(8,128)(2,1)S(1)}, bf16[2,2,256,256]{3,2,1,0:T(8,128)(2,1)S(1)}, u32[]{:S(2)}, u32[]{:S(2)}) collective-permute-start(bf16[2,2,256,256]{3,2,1,0:T(8,128)(2,1)S(1)} %get-tuple-element.44), channel_id=1, source_target_pairs={{0,2},{1,3},{2,0},{3,1},{4,6},{5,7},{6,4},{7,5},{8,10},{9,11},{10,... | collective-permute-start | bytes 1572872 | tf_op jit(solution)/shard_map/ppermute | solution.py:447
  15.3 2.0 %collective-permute-start.8 = (bf16[2,2,256,256]{3,2,1,0:T(8,128)(2,1)S(1)}, bf16[2,2,256,256]{3,2,1,0:T(8,128)(2,1)S(1)}, u32[]{:S(2)}, u32[]{:S(2)}) collective-permute-start(bf16[2,2,256,256]{3,2,1,0:T(8,128)(2,1)S(1)} %get-tuple-element.43.mine_ref), channel_id=1, source_target_pairs={{0,4},{1,5},{2,6},{3,7},{4,8},{5,9},{6,10},{7,11},{8,12},{9,13},{1... | collective-permute-start | bytes 1572872 | tf_op jit(solution)/shard_map/ppermute | solution.py:447
  17.3 1.7 %collective-permute-done.6.refs_2_ = bf16[1,512,128]{2,1,0:T(8,128)(2,1)S(1)} collective-permute-done((bf16[1,512,128]{2,1,0:T(8,128)(2,1)S(1)}, bf16[1,512,128]{2,1,0:T(8,128)(2,1)S(1)}, u32[]{:S(2)}, u32[]{:S(2)}) %collective-permute-start.6) | collective-permute-done | bytes 131104 | tf_op jit(solution)/shard_map/ppermute | solution.py:451
  19.0 1.9 %collective-permute-start.7 = (bf16[3,512,128]{2,1,0:T(8,128)(2,1)S(1)}, bf16[3,512,128]{2,1,0:T(8,128)(2,1)S(1)}, u32[]{:S(2)}, u32[]{:S(2)}) collective-permute-start(bf16[3,512,128]{2,1,0:T(8,128)(2,1)S(1)} %shard_map.92.near_ref), channel_id=1, source_target_pairs={{0,16},{16,0},{1,17},{17,1},{2,18},{18,2},{3,19},{19,3},{4,20},{20... | collective-permute-start | bytes 1179656 | tf_op jit(solution)/shard_map/ppermute | solution.py:212
  20.9 1.6 %collective-permute-start.11 = (bf16[2,256,256]{2,1,0:T(8,128)(2,1)S(1)}, bf16[2,256,256]{2,1,0:T(8,128)(2,1)S(1)}, u32[]{:S(2)}, u32[]{:S(2)}) collective-permute-start(bf16[2,256,256]{2,1,0:T(8,128)(2,1)S(1)} %get-tuple-element.48), channel_id=1, source_target_pairs={{0,6},{1,7},{2,4},{3,5},{4,10},{5,11},{6,8},{7,9},{8,14},{9,15},{1... | collective-permute-start | bytes 786440 | tf_op jit(solution)/shard_map/ppermute | solution.py:447
  22.5 2.2 %collective-permute-start.10 = (bf16[2,256,256]{2,1,0:T(8,128)(2,1)S(1)}, bf16[2,256,256]{2,1,0:T(8,128)(2,1)S(1)}, u32[]{:S(2)}, u32[]{:S(2)}) collective-permute-start(bf16[2,256,256]{2,1,0:T(8,128)(2,1)S(1)} %get-tuple-element.47), channel_id=1, source_target_pairs={{0,6},{1,7},{2,4},{3,5},{4,10},{5,11},{6,8},{7,9},{8,14},{9,15},{1... | collective-permute-start | bytes 786440 | tf_op jit(solution)/shard_map/ppermute | solution.py:447
  24.7 5.0 %collective-permute-done.7.far_ref = bf16[3,512,128]{2,1,0:T(8,128)(2,1)S(1)} collective-permute-done((bf16[3,512,128]{2,1,0:T(8,128)(2,1)S(1)}, bf16[3,512,128]{2,1,0:T(8,128)(2,1)S(1)}, u32[]{:S(2)}, u32[]{:S(2)}) %collective-permute-start.7) | collective-permute-done | bytes 393248 | tf_op jit(solution)/shard_map/ppermute | solution.py:212
  29.7 1.5 %shard_map.93.taps_ref = f32[2,4,512,256]{3,2,1,0:T(8,128)S(1)} custom-call(bf16[512,256]{1,0:T(8,128)(2,1)S(1)} %copy-done.1, bf16[512,256]{1,0:T(8,128)(2,1)S(1)} %copy-done, bf16[1024,128]{1,0:T(8,128)(2,1)S(1)} %copy-done.5, bf16[3,512,128]{2,1,0:T(8,128)(2,1)S(1)} %shard_map.92.near_ref, bf16[3,512,128]{2,1,0:T(8,128)(2,1)S(1)} %collective-permute-done.7.far_ref), custom_call_target="tpu_custom_call" | custom-call | flops 1000 | bytes 1000 | tf_op jit(solution)/shard_map/pallas_call | solution.py:213
  31.2 1.0 %collective-permute-done.8.ahead_ref = bf16[2,2,256,256]{3,2,1,0:T(8,128)(2,1)S(1)} collective-permute-done((bf16[2,2,256,256]{3,2,1,0:T(8,128)(2,1)S(1)}, bf16[2,2,256,256]{3,2,1,0:T(8,128)(2,1)S(1)}, u32[]{:S(2)}, u32[]{:S(2)}) %collective-permute-start.8) | collective-permute-done | bytes 524320 | tf_op jit(solution)/shard_map/ppermute | solution.py:447
  32.3 3.6 %shard_map.95 = (f32[2,3,512,256]{3,2,1,0:T(8,128)S(1)}, f32[2,512,256]{2,1,0:T(8,128)S(1)}, f32[2,4,512,256]{3,2,1,0:T(8,128)S(1)}) custom-call(bf16[512,256]{1,0:T(8,128)(2,1)S(1)} %copy-done.1, bf16[512,256]{1,0:T(8,128)(2,1)S(1)} %copy-done, f32[2,4,512,256]{3,2,1,0:T(8,128)S(1)} %shard_map.93.taps_ref, ...), custom_call_target="tpu_custom_call" | custom-call | flops 1000 | bytes 1000 | tf_op jit(solution)/shard_map/pallas_call | solution.py:289
  35.9 3.0 %collective-permute-done.11.beyond_ref = bf16[2,256,256]{2,1,0:T(8,128)(2,1)S(1)} collective-permute-done((bf16[2,256,256]{2,1,0:T(8,128)(2,1)S(1)}, bf16[2,256,256]{2,1,0:T(8,128)(2,1)S(1)}, u32[]{:S(2)}, u32[]{:S(2)}) %collective-permute-start.11) | collective-permute-done | bytes 262176 | tf_op jit(solution)/shard_map/ppermute | solution.py:447
  38.9 2.6 %shard_map.96 = (bf16[256,256]{1,0:T(8,128)(2,1)S(1)}, bf16[256,256]{1,0:T(8,128)(2,1)S(1)}, bf16[256,256]{1,0:T(8,128)(2,1)S(1)}, bf16[256,256]{1,0:T(8,128)(2,1)S(1)}, f32[2,4,512,256]{3,2,1,0:T(8,128)S(1)}) custom-call(bf16[512,256]{1,0:T(8,128)(2,1)S(1)} %copy-done.1, bf16[512,256]{1,0:T(8,128)(2,1)S(1)} %copy-done, ...), custom_call_target="tpu_custom_call", output_to_operand_aliasing={{4}: (11, {})} | custom-call | flops 1000 | bytes 1000 | tf_op jit(solution)/shard_map/pallas_call | solution.py:376
  41.5 0.6 %collective-permute-start.16 = (bf16[256,256]{1,0:T(8,128)(2,1)S(1)}, bf16[256,256]{1,0:T(8,128)(2,1)S(1)}, u32[]{:S(2)}, u32[]{:S(2)}) collective-permute-start(bf16[256,256]{1,0:T(8,128)(2,1)S(1)} %get-tuple-element.57), channel_id=1, source_target_pairs={{0,2},{1,3},{2,0},{3,1},{4,6},{5,7},{6,4},{7,5},{8,10},{9,11},{10,... | collective-permute-start | bytes 393224 | tf_op jit(solution)/shard_map/ppermute | solution.py:447
  42.1 1.3 %collective-permute-start.17 = (bf16[256,256]{1,0:T(8,128)(2,1)S(1)}, bf16[256,256]{1,0:T(8,128)(2,1)S(1)}, u32[]{:S(2)}, u32[]{:S(2)}) collective-permute-start(bf16[256,256]{1,0:T(8,128)(2,1)S(1)} %get-tuple-element.58), channel_id=1, source_target_pairs={{0,3},{1,2},{2,1},{3,0},{4,7},{5,6},{6,5},{7,4},{8,11},{9,10},{10,... | collective-permute-start | bytes 393224 | tf_op jit(solution)/shard_map/ppermute | solution.py:447
  43.4 0.8 %collective-permute-done.10.beyond_ref = bf16[2,256,256]{2,1,0:T(8,128)(2,1)S(1)} collective-permute-done((bf16[2,256,256]{2,1,0:T(8,128)(2,1)S(1)}, bf16[2,256,256]{2,1,0:T(8,128)(2,1)S(1)}, u32[]{:S(2)}, u32[]{:S(2)}) %collective-permute-start.10) | collective-permute-done | bytes 262176 | tf_op jit(solution)/shard_map/ppermute | solution.py:447
  44.2 2.6 %shard_map.97 = (bf16[256,256]{1,0:T(8,128)(2,1)S(1)}, bf16[256,256]{1,0:T(8,128)(2,1)S(1)}, bf16[256,256]{1,0:T(8,128)(2,1)S(1)}, bf16[256,256]{1,0:T(8,128)(2,1)S(1)}, f32[2,4,512,256]{3,2,1,0:T(8,128)S(1)}) custom-call(bf16[512,256]{1,0:T(8,128)(2,1)S(1)} %copy-done.1, bf16[512,256]{1,0:T(8,128)(2,1)S(1)} %copy-done, ...), custom_call_target="tpu_custom_call", output_to_operand_aliasing={{4}: (11, {})} | custom-call | flops 1000 | bytes 1000 | tf_op jit(solution)/shard_map/pallas_call | solution.py:376
  46.8 0.6 %collective-permute-start.13 = (bf16[256,256]{1,0:T(8,128)(2,1)S(1)}, bf16[256,256]{1,0:T(8,128)(2,1)S(1)}, u32[]{:S(2)}, u32[]{:S(2)}) collective-permute-start(bf16[256,256]{1,0:T(8,128)(2,1)S(1)} %get-tuple-element.53), channel_id=1, source_target_pairs={{0,2},{1,3},{2,0},{3,1},{4,6},{5,7},{6,4},{7,5},{8,10},{9,11},{10,... | collective-permute-start | bytes 393224 | tf_op jit(solution)/shard_map/ppermute | solution.py:447
  47.4 1.3 %collective-permute-start.14 = (bf16[256,256]{1,0:T(8,128)(2,1)S(1)}, bf16[256,256]{1,0:T(8,128)(2,1)S(1)}, u32[]{:S(2)}, u32[]{:S(2)}) collective-permute-start(bf16[256,256]{1,0:T(8,128)(2,1)S(1)} %get-tuple-element.54), channel_id=1, source_target_pairs={{0,3},{1,2},{2,1},{3,0},{4,7},{5,6},{6,5},{7,4},{8,11},{9,10},{10,... | collective-permute-start | bytes 393224 | tf_op jit(solution)/shard_map/ppermute | solution.py:447
  48.7 1.1 %collective-permute-done.17.refs_3_ = bf16[256,256]{1,0:T(8,128)(2,1)S(1)} collective-permute-done((bf16[256,256]{1,0:T(8,128)(2,1)S(1)}, bf16[256,256]{1,0:T(8,128)(2,1)S(1)}, u32[]{:S(2)}, u32[]{:S(2)}) %collective-permute-start.17) | collective-permute-done | bytes 131104 | tf_op jit(solution)/shard_map/ppermute | solution.py:447
  49.8 1.1 %shard_map.98.refs_4_ = bf16[256,2048]{1,0:T(8,128)(2,1)} custom-call(bf16[256,2048]{1,0:T(8,128)(2,1)S(1)} %copy-done.2, bf16[256,256]{1,0:T(8,128)(2,1)S(1)} %get-tuple-element.55.refs_0_, bf16[256,256]{1,0:T(8,128)(2,1)S(1)} %collective-permute-done.15.refs_1_, bf16[256,256]{1,0:T(8,128)(2,1)S(1)} %collective-permute-done.16.refs_2_, ...), custom_call_target="tpu_custom_call" | custom-call | flops 1000 | bytes 1000 | tf_op jit(solution)/shard_map/pallas_call | solution.py:419
  50.9 2.4 %collective-permute-done.13.refs_2_ = bf16[256,256]{1,0:T(8,128)(2,1)S(1)} collective-permute-done((bf16[256,256]{1,0:T(8,128)(2,1)S(1)}, bf16[256,256]{1,0:T(8,128)(2,1)S(1)}, u32[]{:S(2)}, u32[]{:S(2)}) %collective-permute-start.13) | collective-permute-done | bytes 131104 | tf_op jit(solution)/shard_map/ppermute | solution.py:447
  53.3 2.3 %collective-permute-done.14.refs_3_ = bf16[256,256]{1,0:T(8,128)(2,1)S(1)} collective-permute-done((bf16[256,256]{1,0:T(8,128)(2,1)S(1)}, bf16[256,256]{1,0:T(8,128)(2,1)S(1)}, u32[]{:S(2)}, u32[]{:S(2)}) %collective-permute-start.14) | collective-permute-done | bytes 131104 | tf_op jit(solution)/shard_map/ppermute | solution.py:447
  55.6 1.1 %shard_map.99 = bf16[256,2048]{1,0:T(8,128)(2,1)} custom-call(bf16[256,2048]{1,0:T(8,128)(2,1)S(1)} %copy-done.2, bf16[256,256]{1,0:T(8,128)(2,1)S(1)} %get-tuple-element.51.refs_0_, bf16[256,256]{1,0:T(8,128)(2,1)S(1)} %collective-permute-done.12.refs_1_, bf16[256,256]{1,0:T(8,128)(2,1)S(1)} %collective-permute-done.13.refs_2_, ...), custom_call_target="tpu_custom_call", output_to_operand_aliasing={{}: (5, {})} | custom-call | flops 1000 | bytes 1000 | tf_op jit(solution)/shard_map/pallas_call | solution.py:419
  (28 shorter events, 0.9 us)
Async XLA Ops:
  0.0 29.7 %copy-start = (bf16[512,256]{1,0:T(8,128)(2,1)S(1)}, bf16[512,256]{1,0:T(8,128)(2,1)}, u32[]{:S(2)}) copy-start(bf16[512,256]{1,0:T(8,128)(2,1)} %constant.21.clone.low_ref) | copy-start | bytes 786436
  0.0 29.7 %copy-start.1 = (bf16[512,256]{1,0:T(8,128)(2,1)S(1)}, bf16[512,256]{1,0:T(8,128)(2,1)}, u32[]{:S(2)}) copy-start(bf16[512,256]{1,0:T(8,128)(2,1)} %constant.20.clone.high_ref) | copy-start | bytes 786436
  0.0 29.7 %copy-start.5 = (bf16[1024,128]{1,0:T(8,128)(2,1)S(1)}, bf16[1024,128]{1,0:T(8,128)(2,1)}, u32[]{:S(2)}) copy-start(bf16[1024,128]{1,0:T(8,128)(2,1)} %own_ref.1) | copy-start | bytes 786436
  1.0 8.4 %collective-permute-start = (bf16[1,512,128]{2,1,0:T(8,128)(2,1)S(1)}, bf16[1,512,128]{2,1,0:T(8,128)(2,1)S(1)}, u32[]{:S(2)}, u32[]{:S(2)}) collective-permute-start(bf16[1,512,128]{2,1,0:T(8,128)(2,1)S(1)} %dynamic-slice_bitcast_fusion), channel_id=1, source_target_pairs={{0,4},{1,5},{2,6},{3,7},{4,0},{5,1},{6,2},{7,3},{8,12},{9,13},{10,... | collective-permute-start | bytes 393224 | tf_op jit(solution)/shard_map/ppermute | solution.py:451
  4.1 8.7 %collective-permute-start.1 = (bf16[1,512,128]{2,1,0:T(8,128)(2,1)S(1)}, bf16[1,512,128]{2,1,0:T(8,128)(2,1)S(1)}, u32[]{:S(2)}, u32[]{:S(2)}) collective-permute-start(bf16[1,512,128]{2,1,0:T(8,128)(2,1)S(1)} %dynamic-slice_bitcast_fusion), channel_id=1, source_target_pairs={{0,8},{1,9},{2,10},{3,11},{4,12},{5,13},{6,14},{7,15},{8,0},{9,1},... | collective-permute-start | bytes 393224 | tf_op jit(solution)/shard_map/ppermute | solution.py:451
  11.2 1.7 %collective-permute-start.2 = (bf16[256,256]{1,0:T(8,128)(2,1)S(1)}, bf16[256,256]{1,0:T(8,128)(2,1)S(1)}, u32[]{:S(2)}, u32[]{:S(2)}) collective-permute-start(bf16[256,256]{1,0:T(8,128)(2,1)S(1)} %get-tuple-element.32), channel_id=1, source_target_pairs={{0,1},{1,0},{2,3},{3,2},{4,5},{5,4},{6,7},{7,6},{8,9},{9,8},{10,11... | collective-permute-start | bytes 393224 | tf_op jit(solution)/shard_map/ppermute | solution.py:447
  11.2 1.6 %collective-permute-start.3 = (bf16[256,256]{1,0:T(8,128)(2,1)S(1)}, bf16[256,256]{1,0:T(8,128)(2,1)S(1)}, u32[]{:S(2)}, u32[]{:S(2)}) collective-permute-start(bf16[256,256]{1,0:T(8,128)(2,1)S(1)} %get-tuple-element.33), channel_id=1, source_target_pairs={{0,1},{1,0},{2,3},{3,2},{4,5},{5,4},{6,7},{7,6},{8,9},{9,8},{10,11... | collective-permute-start | bytes 393224 | tf_op jit(solution)/shard_map/ppermute | solution.py:447
  11.7 1.3 %collective-permute-start.4 = (bf16[256,256]{1,0:T(8,128)(2,1)S(1)}, bf16[256,256]{1,0:T(8,128)(2,1)S(1)}, u32[]{:S(2)}, u32[]{:S(2)}) collective-permute-start(bf16[256,256]{1,0:T(8,128)(2,1)S(1)} %get-tuple-element.34), channel_id=1, source_target_pairs={{0,1},{1,0},{2,3},{3,2},{4,5},{5,4},{6,7},{7,6},{8,9},{9,8},{10,11... | collective-permute-start | bytes 393224 | tf_op jit(solution)/shard_map/ppermute | solution.py:447
  11.8 1.5 %collective-permute-start.5 = (bf16[256,256]{1,0:T(8,128)(2,1)S(1)}, bf16[256,256]{1,0:T(8,128)(2,1)S(1)}, u32[]{:S(2)}, u32[]{:S(2)}) collective-permute-start(bf16[256,256]{1,0:T(8,128)(2,1)S(1)} %get-tuple-element.35), channel_id=1, source_target_pairs={{0,1},{1,0},{2,3},{3,2},{4,5},{5,4},{6,7},{7,6},{8,9},{9,8},{10,11... | collective-permute-start | bytes 393224 | tf_op jit(solution)/shard_map/ppermute | solution.py:447
  13.3 5.7 %collective-permute-start.6 = (bf16[1,512,128]{2,1,0:T(8,128)(2,1)S(1)}, bf16[1,512,128]{2,1,0:T(8,128)(2,1)S(1)}, u32[]{:S(2)}, u32[]{:S(2)}) collective-permute-start(bf16[1,512,128]{2,1,0:T(8,128)(2,1)S(1)} %collective-permute-done.1.refs_1_), channel_id=1, source_target_pairs={{0,4},{1,5},{2,6},{3,7},{4,0},{5,1},{6,2},{7,3},{8,12},{9,13},{10,... | collective-permute-start | bytes 393224 | tf_op jit(solution)/shard_map/ppermute | solution.py:451
  13.7 17.5 %collective-permute-start.9 = (bf16[2,2,256,256]{3,2,1,0:T(8,128)(2,1)S(1)}, bf16[2,2,256,256]{3,2,1,0:T(8,128)(2,1)S(1)}, u32[]{:S(2)}, u32[]{:S(2)}) collective-permute-start(bf16[2,2,256,256]{3,2,1,0:T(8,128)(2,1)S(1)} %get-tuple-element.44), channel_id=1, source_target_pairs={{0,2},{1,3},{2,0},{3,1},{4,6},{5,7},{6,4},{7,5},{8,10},{9,11},{10,... | collective-permute-start | bytes 1572872 | tf_op jit(solution)/shard_map/ppermute | solution.py:447
  15.3 16.9 %collective-permute-start.8 = (bf16[2,2,256,256]{3,2,1,0:T(8,128)(2,1)S(1)}, bf16[2,2,256,256]{3,2,1,0:T(8,128)(2,1)S(1)}, u32[]{:S(2)}, u32[]{:S(2)}) collective-permute-start(bf16[2,2,256,256]{3,2,1,0:T(8,128)(2,1)S(1)} %get-tuple-element.43.mine_ref), channel_id=1, source_target_pairs={{0,4},{1,5},{2,6},{3,7},{4,8},{5,9},{6,10},{7,11},{8,12},{9,13},{1... | collective-permute-start | bytes 1572872 | tf_op jit(solution)/shard_map/ppermute | solution.py:447
  19.0 10.7 %collective-permute-start.7 = (bf16[3,512,128]{2,1,0:T(8,128)(2,1)S(1)}, bf16[3,512,128]{2,1,0:T(8,128)(2,1)S(1)}, u32[]{:S(2)}, u32[]{:S(2)}) collective-permute-start(bf16[3,512,128]{2,1,0:T(8,128)(2,1)S(1)} %shard_map.92.near_ref), channel_id=1, source_target_pairs={{0,16},{16,0},{1,17},{17,1},{2,18},{18,2},{3,19},{19,3},{4,20},{20... | collective-permute-start | bytes 1179656 | tf_op jit(solution)/shard_map/ppermute | solution.py:212
  20.9 17.9 %collective-permute-start.11 = (bf16[2,256,256]{2,1,0:T(8,128)(2,1)S(1)}, bf16[2,256,256]{2,1,0:T(8,128)(2,1)S(1)}, u32[]{:S(2)}, u32[]{:S(2)}) collective-permute-start(bf16[2,256,256]{2,1,0:T(8,128)(2,1)S(1)} %get-tuple-element.48), channel_id=1, source_target_pairs={{0,6},{1,7},{2,4},{3,5},{4,10},{5,11},{6,8},{7,9},{8,14},{9,15},{1... | collective-permute-start | bytes 786440 | tf_op jit(solution)/shard_map/ppermute | solution.py:447
  22.5 21.7 %collective-permute-start.10 = (bf16[2,256,256]{2,1,0:T(8,128)(2,1)S(1)}, bf16[2,256,256]{2,1,0:T(8,128)(2,1)S(1)}, u32[]{:S(2)}, u32[]{:S(2)}) collective-permute-start(bf16[2,256,256]{2,1,0:T(8,128)(2,1)S(1)} %get-tuple-element.47), channel_id=1, source_target_pairs={{0,6},{1,7},{2,4},{3,5},{4,10},{5,11},{6,8},{7,9},{8,14},{9,15},{1... | collective-permute-start | bytes 786440 | tf_op jit(solution)/shard_map/ppermute | solution.py:447
  31.2 7.7 %copy-start.3 = (bf16[256,512]{1,0:T(8,128)(2,1)S(1)}, bf16[256,512]{1,0:T(8,128)(2,1)}, u32[]{:S(2)}) copy-start(bf16[256,512]{1,0:T(8,128)(2,1)} %constant.23.clone.back_low_ref) | copy-start | bytes 786436
  31.2 7.7 %copy-start.4 = (bf16[256,512]{1,0:T(8,128)(2,1)S(1)}, bf16[256,512]{1,0:T(8,128)(2,1)}, u32[]{:S(2)}) copy-start(bf16[256,512]{1,0:T(8,128)(2,1)} %constant.22.clone.back_high_ref) | copy-start | bytes 786436
  31.2 7.7 %copy-start.6 = (f32[2048]{0:T(1024)S(1)}, f32[2048]{0:T(1024)}, u32[]{:S(2)}) copy-start(f32[2048]{0:T(1024)} %param.13) | copy-start | bytes 24580
  41.4 6.0 %collective-permute-start.15 = (bf16[256,256]{1,0:T(8,128)(2,1)S(1)}, bf16[256,256]{1,0:T(8,128)(2,1)S(1)}, u32[]{:S(2)}, u32[]{:S(2)}) collective-permute-start(bf16[256,256]{1,0:T(8,128)(2,1)S(1)} %get-tuple-element.56), channel_id=1, source_target_pairs={{0,1},{1,0},{2,3},{3,2},{4,5},{5,4},{6,7},{7,6},{8,9},{9,8},{10,11... | collective-permute-start | bytes 393224 | tf_op jit(solution)/shard_map/ppermute | solution.py:447
  41.5 7.2 %collective-permute-start.16 = (bf16[256,256]{1,0:T(8,128)(2,1)S(1)}, bf16[256,256]{1,0:T(8,128)(2,1)S(1)}, u32[]{:S(2)}, u32[]{:S(2)}) collective-permute-start(bf16[256,256]{1,0:T(8,128)(2,1)S(1)} %get-tuple-element.57), channel_id=1, source_target_pairs={{0,2},{1,3},{2,0},{3,1},{4,6},{5,7},{6,4},{7,5},{8,10},{9,11},{10,... | collective-permute-start | bytes 393224 | tf_op jit(solution)/shard_map/ppermute | solution.py:447
  42.1 7.7 %collective-permute-start.17 = (bf16[256,256]{1,0:T(8,128)(2,1)S(1)}, bf16[256,256]{1,0:T(8,128)(2,1)S(1)}, u32[]{:S(2)}, u32[]{:S(2)}) collective-permute-start(bf16[256,256]{1,0:T(8,128)(2,1)S(1)} %get-tuple-element.58), channel_id=1, source_target_pairs={{0,3},{1,2},{2,1},{3,0},{4,7},{5,6},{6,5},{7,4},{8,11},{9,10},{10,... | collective-permute-start | bytes 393224 | tf_op jit(solution)/shard_map/ppermute | solution.py:447
  44.2 5.6 %copy-start.2 = (bf16[256,2048]{1,0:T(8,128)(2,1)S(1)}, bf16[256,2048]{1,0:T(8,128)(2,1)}, u32[]{:S(2)}) copy-start(bf16[256,2048]{1,0:T(8,128)(2,1)} %gate_ref.3) | copy-start | bytes 3145732
  46.7 4.1 %collective-permute-start.12 = (bf16[256,256]{1,0:T(8,128)(2,1)S(1)}, bf16[256,256]{1,0:T(8,128)(2,1)S(1)}, u32[]{:S(2)}, u32[]{:S(2)}) collective-permute-start(bf16[256,256]{1,0:T(8,128)(2,1)S(1)} %get-tuple-element.52), channel_id=1, source_target_pairs={{0,1},{1,0},{2,3},{3,2},{4,5},{5,4},{6,7},{7,6},{8,9},{9,8},{10,11... | collective-permute-start | bytes 393224 | tf_op jit(solution)/shard_map/ppermute | solution.py:447
  46.8 6.5 %collective-permute-start.13 = (bf16[256,256]{1,0:T(8,128)(2,1)S(1)}, bf16[256,256]{1,0:T(8,128)(2,1)S(1)}, u32[]{:S(2)}, u32[]{:S(2)}) collective-permute-start(bf16[256,256]{1,0:T(8,128)(2,1)S(1)} %get-tuple-element.53), channel_id=1, source_target_pairs={{0,2},{1,3},{2,0},{3,1},{4,6},{5,7},{6,4},{7,5},{8,10},{9,11},{10,... | collective-permute-start | bytes 393224 | tf_op jit(solution)/shard_map/ppermute | solution.py:447
  47.4 8.2 %collective-permute-start.14 = (bf16[256,256]{1,0:T(8,128)(2,1)S(1)}, bf16[256,256]{1,0:T(8,128)(2,1)S(1)}, u32[]{:S(2)}, u32[]{:S(2)}) collective-permute-start(bf16[256,256]{1,0:T(8,128)(2,1)S(1)} %get-tuple-element.54), channel_id=1, source_target_pairs={{0,3},{1,2},{2,1},{3,0},{4,7},{5,6},{6,5},{7,4},{8,11},{9,10},{10,... | collective-permute-start | bytes 393224 | tf_op jit(solution)/shard_map/ppermute | solution.py:447

commit v4 on v3

--- a/solution.py
+++ b/solution.py
@@ -454,7 +454,9 @@
     near = one_away = None
     if half is not None:
         two_away, one_away = to_layer(half, 2), to_layer(half, 1)
-    same, other, *send = product_pieces(gate_in, values, one_away, layers, members)
+    same, other, *send = product_pieces(gate_in, values, half, layers, members)
+    if half is not None:
+        one_away, send = lax.optimization_barrier((one_away, send))
     core = [to_member(piece, 1, 0) for piece in send]
     if half is not None:
         two_away, core = lax.optimization_barrier((two_away, core))

time: 56.8 us -> 55.3 us (0.974)
  waiting for transfers between devices: 21.2 us -> 20.2 us
    ppermute x1, waiting for transfers between devices: 5.05 us -> 3.52 us  [tap_spectra(): far = lax.ppermute(near, 'groups', [(0, 1), (1, 0)])]
    ppermute x14, waiting for transfers between devices: 11.1 us -> 12 us  [to_member(): return lax.ppermute(value, 'ctx', pairs)]
  transfers between devices with their start and end apart: 18 -> 18, of which waited for: 12 -> 10; matrix products, arithmetic and copies ran while one was open for 0% -> 0% of each run, Pallas kernels for 23% -> 24%
where the time goes in v4:
time: 55.3 us; the launch traced here: 55.1 us
  waiting for transfers between devices  20.2 us (37%)
  starting transfers between devices  19.7 us (36%)
  Pallas kernels  14.2 us (26%)
  local copies, waits for them, and re-layouts  1.02 us (2%)
    ppermute x14, waiting for transfers between devices, to_member(): return lax.ppermute(value, 'ctx', pairs)  12 us
    ppermute x14, starting transfers between devices, to_member(): return lax.ppermute(value, 'ctx', pairs)  11.9 us
    ppermute x3, starting transfers between devices, to_layer(): return lax.ppermute(value, 'ctx', pairs)  6.2 us
    pallas_call x2, Pallas kernels, mixed_pieces(): pl.pallas_call(functools.partial(mix_kernel, members, part), in_specs=[VM...  5.15 us
    ppermute x3, waiting for transfers between devices, to_layer(): return lax.ppermute(value, 'ctx', pairs)  4.64 us
    pallas_call x1, Pallas kernels, own_partials(): pl.pallas_call(functools.partial(own_kernel, members), in_specs=[VMEM] *...  3.57 us
    ppermute x1, waiting for transfers between devices, tap_spectra(): far = lax.ppermute(near, 'groups', [(0, 1), (1, 0)])  3.52 us
    pallas_call x2, Pallas kernels, gated_output(): pl.pallas_call(functools.partial(gate_kernel, layers // CHUNKS, members,...  2.13 us
  transfers between devices with their start and end apart: 18, of which 10 were waited for; matrix products, arithmetic and copies ran while one was open for 0% of the time, Pallas kernels for 24%

profile of v4, /device:TPU:0, one launch (start us, length us, event | category | flops | bytes accessed | tf_op | source)
XLA Modules:
  0.0 55.1 jit_solution(1916264997127728964)
XLA Ops:
  0.0 1.0 %dynamic-slice_bitcast_fusion.half_ref = bf16[1,512,128]{2,1,0:T(8,128)(2,1)S(1)} fusion(bf16[1024,128]{1,0:T(8,128)(2,1)} %own_ref.1, s32[]{:T(128)S(6)} %select_n.3), kind=kLoop, calls=%fused_computation | loop fusion | bytes 262148 | tf_op jit(solution)/shard_map/broadcast_in_dim | solution.py:193
  1.0 3.1 %collective-permute-start = (bf16[1,512,128]{2,1,0:T(8,128)(2,1)S(1)}, bf16[1,512,128]{2,1,0:T(8,128)(2,1)S(1)}, u32[]{:S(2)}, u32[]{:S(2)}) collective-permute-start(bf16[1,512,128]{2,1,0:T(8,128)(2,1)S(1)} %dynamic-slice_bitcast_fusion.half_ref), channel_id=1, source_target_pairs={{0,4},{1,5},{2,6},{3,7},{4,0},{5,1},{6,2},{7,3},{8,12},{9,13},{10,... | collective-permute-start | bytes 393224 | tf_op jit(solution)/shard_map/ppermute | solution.py:451
  4.1 2.6 %collective-permute-start.1 = (bf16[1,512,128]{2,1,0:T(8,128)(2,1)S(1)}, bf16[1,512,128]{2,1,0:T(8,128)(2,1)S(1)}, u32[]{:S(2)}, u32[]{:S(2)}) collective-permute-start(bf16[1,512,128]{2,1,0:T(8,128)(2,1)S(1)} %dynamic-slice_bitcast_fusion.half_ref), channel_id=1, source_target_pairs={{0,8},{1,9},{2,10},{3,11},{4,12},{5,13},{6,14},{7,15},{8,0},{9,1},... | collective-permute-start | bytes 393224 | tf_op jit(solution)/shard_map/ppermute | solution.py:451
  6.7 1.7 %shard_map.91 = (bf16[2,256,256]{2,1,0:T(8,128)(2,1)S(1)}, bf16[2,256,256]{2,1,0:T(8,128)(2,1)S(1)}, bf16[256,256]{1,0:T(8,128)(2,1)S(1)}, bf16[256,256]{1,0:T(8...) custom-call(bf16[256,2048]{1,0:T(8,128)(2,1)} %gate_hbm.1, bf16[256,2048]{1,0:T(8,128)(2,1)} %values_hbm.1, ...), custom_call_target="tpu_custom_call" | custom-call | flops 1000 | bytes 1000 | tf_op jit(solution)/shard_map/pallas_call | solution.py:112
  8.4 1.0 %collective-permute-done.refs_0_ = bf16[1,512,128]{2,1,0:T(8,128)(2,1)S(1)} collective-permute-done((bf16[1,512,128]{2,1,0:T(8,128)(2,1)S(1)}, bf16[1,512,128]{2,1,0:T(8,128)(2,1)S(1)}, u32[]{:S(2)}, u32[]{:S(2)}) %collective-permute-start) | collective-permute-done | bytes 131104 | tf_op jit(solution)/shard_map/ppermute | solution.py:451
  9.4 0.5 collective-permute-start.3
  10.0 0.5 collective-permute-start.5
  10.5 2.4 %collective-permute-done.1.refs_1_ = bf16[1,512,128]{2,1,0:T(8,128)(2,1)S(1)} collective-permute-done((bf16[1,512,128]{2,1,0:T(8,128)(2,1)S(1)}, bf16[1,512,128]{2,1,0:T(8,128)(2,1)S(1)}, u32[]{:S(2)}, u32[]{:S(2)}) %collective-permute-start.1) | collective-permute-done | bytes 131104 | tf_op jit(solution)/shard_map/ppermute | solution.py:451
  12.8 0.5 collective-permute-start.6
  13.5 1.6 %collective-permute-start.9 = (bf16[2,2,256,256]{3,2,1,0:T(8,128)(2,1)S(1)}, bf16[2,2,256,256]{3,2,1,0:T(8,128)(2,1)S(1)}, u32[]{:S(2)}, u32[]{:S(2)}) collective-permute-start(bf16[2,2,256,256]{3,2,1,0:T(8,128)(2,1)S(1)} %get-tuple-element.54), channel_id=1, source_target_pairs={{0,2},{1,3},{2,0},{3,1},{4,6},{5,7},{6,4},{7,5},{8,10},{9,11},{10,... | collective-permute-start | bytes 1572872 | tf_op jit(solution)/shard_map/ppermute | solution.py:447
  15.0 1.6 %collective-permute-start.8 = (bf16[2,2,256,256]{3,2,1,0:T(8,128)(2,1)S(1)}, bf16[2,2,256,256]{3,2,1,0:T(8,128)(2,1)S(1)}, u32[]{:S(2)}, u32[]{:S(2)}) collective-permute-start(bf16[2,2,256,256]{3,2,1,0:T(8,128)(2,1)S(1)} %get-tuple-element.53.mine_ref), channel_id=1, source_target_pairs={{0,4},{1,5},{2,6},{3,7},{4,8},{5,9},{6,10},{7,11},{8,12},{9,13},{1... | collective-permute-start | bytes 1572872 | tf_op jit(solution)/shard_map/ppermute | solution.py:447
  16.6 1.3 %collective-permute-done.6.refs_2_ = bf16[1,512,128]{2,1,0:T(8,128)(2,1)S(1)} collective-permute-done((bf16[1,512,128]{2,1,0:T(8,128)(2,1)S(1)}, bf16[1,512,128]{2,1,0:T(8,128)(2,1)S(1)}, u32[]{:S(2)}, u32[]{:S(2)}) %collective-permute-start.6) | collective-permute-done | bytes 131104 | tf_op jit(solution)/shard_map/ppermute | solution.py:451
  17.9 1.6 %collective-permute-start.7 = (bf16[3,512,128]{2,1,0:T(8,128)(2,1)S(1)}, bf16[3,512,128]{2,1,0:T(8,128)(2,1)S(1)}, u32[]{:S(2)}, u32[]{:S(2)}) collective-permute-start(bf16[3,512,128]{2,1,0:T(8,128)(2,1)S(1)} %shard_map.92.near_ref), channel_id=1, source_target_pairs={{0,16},{16,0},{1,17},{17,1},{2,18},{18,2},{3,19},{19,3},{4,20},{20... | collective-permute-start | bytes 1179656 | tf_op jit(solution)/shard_map/ppermute | solution.py:212
  19.5 2.8 %collective-permute-start.11 = (bf16[2,256,256]{2,1,0:T(8,128)(2,1)S(1)}, bf16[2,256,256]{2,1,0:T(8,128)(2,1)S(1)}, u32[]{:S(2)}, u32[]{:S(2)}) collective-permute-start(bf16[2,256,256]{2,1,0:T(8,128)(2,1)S(1)} %get-tuple-element.58), channel_id=1, source_target_pairs={{0,6},{1,7},{2,4},{3,5},{4,10},{5,11},{6,8},{7,9},{8,14},{9,15},{1... | collective-permute-start | bytes 786440 | tf_op jit(solution)/shard_map/ppermute | solution.py:447
  22.3 1.0 %collective-permute-start.10 = (bf16[2,256,256]{2,1,0:T(8,128)(2,1)S(1)}, bf16[2,256,256]{2,1,0:T(8,128)(2,1)S(1)}, u32[]{:S(2)}, u32[]{:S(2)}) collective-permute-start(bf16[2,256,256]{2,1,0:T(8,128)(2,1)S(1)} %get-tuple-element.57), channel_id=1, source_target_pairs={{0,6},{1,7},{2,4},{3,5},{4,10},{5,11},{6,8},{7,9},{8,14},{9,15},{1... | collective-permute-start | bytes 786440 | tf_op jit(solution)/shard_map/ppermute | solution.py:447
  23.3 3.5 %collective-permute-done.7.far_ref = bf16[3,512,128]{2,1,0:T(8,128)(2,1)S(1)} collective-permute-done((bf16[3,512,128]{2,1,0:T(8,128)(2,1)S(1)}, bf16[3,512,128]{2,1,0:T(8,128)(2,1)S(1)}, u32[]{:S(2)}, u32[]{:S(2)}) %collective-permute-start.7) | collective-permute-done | bytes 393248 | tf_op jit(solution)/shard_map/ppermute | solution.py:212
  26.8 1.5 %shard_map.93.taps_ref = f32[2,4,512,256]{3,2,1,0:T(8,128)S(1)} custom-call(bf16[512,256]{1,0:T(8,128)(2,1)S(1)} %copy-done.1, bf16[512,256]{1,0:T(8,128)(2,1)S(1)} %copy-done, bf16[1024,128]{1,0:T(8,128)(2,1)S(1)} %copy-done.5, bf16[3,512,128]{2,1,0:T(8,128)(2,1)S(1)} %shard_map.92.near_ref, bf16[3,512,128]{2,1,0:T(8,128)(2,1)S(1)} %collective-permute-done.7.far_ref), custom_call_target="tpu_custom_call" | custom-call | flops 1000 | bytes 1000 | tf_op jit(solution)/shard_map/pallas_call | solution.py:213
  28.3 3.3 %collective-permute-done.8.ahead_ref = bf16[2,2,256,256]{3,2,1,0:T(8,128)(2,1)S(1)} collective-permute-done((bf16[2,2,256,256]{3,2,1,0:T(8,128)(2,1)S(1)}, bf16[2,2,256,256]{3,2,1,0:T(8,128)(2,1)S(1)}, u32[]{:S(2)}, u32[]{:S(2)}) %collective-permute-start.8) | collective-permute-done | bytes 524320 | tf_op jit(solution)/shard_map/ppermute | solution.py:447
  31.7 3.6 %shard_map.95 = (f32[2,3,512,256]{3,2,1,0:T(8,128)S(1)}, f32[2,512,256]{2,1,0:T(8,128)S(1)}, f32[2,4,512,256]{3,2,1,0:T(8,128)S(1)}) custom-call(bf16[512,256]{1,0:T(8,128)(2,1)S(1)} %copy-done.1, bf16[512,256]{1,0:T(8,128)(2,1)S(1)} %copy-done, f32[2,4,512,256]{3,2,1,0:T(8,128)S(1)} %shard_map.93.taps_ref, ...), custom_call_target="tpu_custom_call" | custom-call | flops 1000 | bytes 1000 | tf_op jit(solution)/shard_map/pallas_call | solution.py:289
  35.3 2.2 %collective-permute-done.11.beyond_ref = bf16[2,256,256]{2,1,0:T(8,128)(2,1)S(1)} collective-permute-done((bf16[2,256,256]{2,1,0:T(8,128)(2,1)S(1)}, bf16[2,256,256]{2,1,0:T(8,128)(2,1)S(1)}, u32[]{:S(2)}, u32[]{:S(2)}) %collective-permute-start.11) | collective-permute-done | bytes 262176 | tf_op jit(solution)/shard_map/ppermute | solution.py:447
  37.5 2.6 %shard_map.96 = (bf16[256,256]{1,0:T(8,128)(2,1)S(1)}, bf16[256,256]{1,0:T(8,128)(2,1)S(1)}, bf16[256,256]{1,0:T(8,128)(2,1)S(1)}, bf16[256,256]{1,0:T(8,128)(2,1)S(1)}, f32[2,4,512,256]{3,2,1,0:T(8,128)S(1)}) custom-call(bf16[512,256]{1,0:T(8,128)(2,1)S(1)} %copy-done.1, bf16[512,256]{1,0:T(8,128)(2,1)S(1)} %copy-done, ...), custom_call_target="tpu_custom_call", output_to_operand_aliasing={{4}: (11, {})} | custom-call | flops 1000 | bytes 1000 | tf_op jit(solution)/shard_map/pallas_call | solution.py:376
  40.2 1.3 %collective-permute-start.16 = (bf16[256,256]{1,0:T(8,128)(2,1)S(1)}, bf16[256,256]{1,0:T(8,128)(2,1)S(1)}, u32[]{:S(2)}, u32[]{:S(2)}) collective-permute-start(bf16[256,256]{1,0:T(8,128)(2,1)S(1)} %get-tuple-element.67), channel_id=1, source_target_pairs={{0,2},{1,3},{2,0},{3,1},{4,6},{5,7},{6,4},{7,5},{8,10},{9,11},{10,... | collective-permute-start | bytes 393224 | tf_op jit(solution)/shard_map/ppermute | solution.py:447
  41.5 0.5 collective-permute-start.17
  42.0 0.4 collective-permute-done.10.beyond_ref
  42.4 2.6 %shard_map.97 = (bf16[256,256]{1,0:T(8,128)(2,1)S(1)}, bf16[256,256]{1,0:T(8,128)(2,1)S(1)}, bf16[256,256]{1,0:T(8,128)(2,1)S(1)}, bf16[256,256]{1,0:T(8,128)(2,1)S(1)}, f32[2,4,512,256]{3,2,1,0:T(8,128)S(1)}) custom-call(bf16[512,256]{1,0:T(8,128)(2,1)S(1)} %copy-done.1, bf16[512,256]{1,0:T(8,128)(2,1)S(1)} %copy-done, ...), custom_call_target="tpu_custom_call", output_to_operand_aliasing={{4}: (11, {})} | custom-call | flops 1000 | bytes 1000 | tf_op jit(solution)/shard_map/pallas_call | solution.py:376
  45.0 1.3 %collective-permute-start.13 = (bf16[256,256]{1,0:T(8,128)(2,1)S(1)}, bf16[256,256]{1,0:T(8,128)(2,1)S(1)}, u32[]{:S(2)}, u32[]{:S(2)}) collective-permute-start(bf16[256,256]{1,0:T(8,128)(2,1)S(1)} %get-tuple-element.63), channel_id=1, source_target_pairs={{0,2},{1,3},{2,0},{3,1},{4,6},{5,7},{6,4},{7,5},{8,10},{9,11},{10,... | collective-permute-start | bytes 393224 | tf_op jit(solution)/shard_map/ppermute | solution.py:447
  46.3 0.6 %collective-permute-start.14 = (bf16[256,256]{1,0:T(8,128)(2,1)S(1)}, bf16[256,256]{1,0:T(8,128)(2,1)S(1)}, u32[]{:S(2)}, u32[]{:S(2)}) collective-permute-start(bf16[256,256]{1,0:T(8,128)(2,1)S(1)} %get-tuple-element.64), channel_id=1, source_target_pairs={{0,3},{1,2},{2,1},{3,0},{4,7},{5,6},{6,5},{7,4},{8,11},{9,10},{10,... | collective-permute-start | bytes 393224 | tf_op jit(solution)/shard_map/ppermute | solution.py:447
  46.9 1.5 %collective-permute-done.17.refs_3_ = bf16[256,256]{1,0:T(8,128)(2,1)S(1)} collective-permute-done((bf16[256,256]{1,0:T(8,128)(2,1)S(1)}, bf16[256,256]{1,0:T(8,128)(2,1)S(1)}, u32[]{:S(2)}, u32[]{:S(2)}) %collective-permute-start.17) | collective-permute-done | bytes 131104 | tf_op jit(solution)/shard_map/ppermute | solution.py:447
  48.4 1.1 %shard_map.98.refs_4_ = bf16[256,2048]{1,0:T(8,128)(2,1)} custom-call(bf16[256,2048]{1,0:T(8,128)(2,1)S(1)} %copy-done.2, bf16[256,256]{1,0:T(8,128)(2,1)S(1)} %get-tuple-element.65.refs_0_, bf16[256,256]{1,0:T(8,128)(2,1)S(1)} %collective-permute-done.15.refs_1_, bf16[256,256]{1,0:T(8,128)(2,1)S(1)} %collective-permute-done.16.refs_2_, ...), custom_call_target="tpu_custom_call" | custom-call | flops 1000 | bytes 1000 | tf_op jit(solution)/shard_map/pallas_call | solution.py:419
  49.5 2.6 %collective-permute-done.13.refs_2_ = bf16[256,256]{1,0:T(8,128)(2,1)S(1)} collective-permute-done((bf16[256,256]{1,0:T(8,128)(2,1)S(1)}, bf16[256,256]{1,0:T(8,128)(2,1)S(1)}, u32[]{:S(2)}, u32[]{:S(2)}) %collective-permute-start.13) | collective-permute-done | bytes 131104 | tf_op jit(solution)/shard_map/ppermute | solution.py:447
  52.2 1.9 %collective-permute-done.14.refs_3_ = bf16[256,256]{1,0:T(8,128)(2,1)S(1)} collective-permute-done((bf16[256,256]{1,0:T(8,128)(2,1)S(1)}, bf16[256,256]{1,0:T(8,128)(2,1)S(1)}, u32[]{:S(2)}, u32[]{:S(2)}) %collective-permute-start.14) | collective-permute-done | bytes 131104 | tf_op jit(solution)/shard_map/ppermute | solution.py:447
  54.1 1.1 %shard_map.99 = bf16[256,2048]{1,0:T(8,128)(2,1)} custom-call(bf16[256,2048]{1,0:T(8,128)(2,1)S(1)} %copy-done.2, bf16[256,256]{1,0:T(8,128)(2,1)S(1)} %get-tuple-element.61.refs_0_, bf16[256,256]{1,0:T(8,128)(2,1)S(1)} %collective-permute-done.12.refs_1_, bf16[256,256]{1,0:T(8,128)(2,1)S(1)} %collective-permute-done.13.refs_2_, ...), custom_call_target="tpu_custom_call", output_to_operand_aliasing={{}: (5, {})} | custom-call | flops 1000 | bytes 1000 | tf_op jit(solution)/shard_map/pallas_call | solution.py:419
  (28 shorter events, 0.3 us)
Async XLA Ops:
  0.0 26.8 %copy-start = (bf16[512,256]{1,0:T(8,128)(2,1)S(1)}, bf16[512,256]{1,0:T(8,128)(2,1)}, u32[]{:S(2)}) copy-start(bf16[512,256]{1,0:T(8,128)(2,1)} %constant.21.clone.low_ref) | copy-start | bytes 786436
  0.0 26.8 %copy-start.1 = (bf16[512,256]{1,0:T(8,128)(2,1)S(1)}, bf16[512,256]{1,0:T(8,128)(2,1)}, u32[]{:S(2)}) copy-start(bf16[512,256]{1,0:T(8,128)(2,1)} %constant.20.clone.high_ref) | copy-start | bytes 786436
  0.0 26.8 %copy-start.5 = (bf16[1024,128]{1,0:T(8,128)(2,1)S(1)}, bf16[1024,128]{1,0:T(8,128)(2,1)}, u32[]{:S(2)}) copy-start(bf16[1024,128]{1,0:T(8,128)(2,1)} %own_ref.1) | copy-start | bytes 786436
  1.0 8.4 %collective-permute-start = (bf16[1,512,128]{2,1,0:T(8,128)(2,1)S(1)}, bf16[1,512,128]{2,1,0:T(8,128)(2,1)S(1)}, u32[]{:S(2)}, u32[]{:S(2)}) collective-permute-start(bf16[1,512,128]{2,1,0:T(8,128)(2,1)S(1)} %dynamic-slice_bitcast_fusion.half_ref), channel_id=1, source_target_pairs={{0,4},{1,5},{2,6},{3,7},{4,0},{5,1},{6,2},{7,3},{8,12},{9,13},{10,... | collective-permute-start | bytes 393224 | tf_op jit(solution)/shard_map/ppermute | solution.py:451
  4.1 8.7 %collective-permute-start.1 = (bf16[1,512,128]{2,1,0:T(8,128)(2,1)S(1)}, bf16[1,512,128]{2,1,0:T(8,128)(2,1)S(1)}, u32[]{:S(2)}, u32[]{:S(2)}) collective-permute-start(bf16[1,512,128]{2,1,0:T(8,128)(2,1)S(1)} %dynamic-slice_bitcast_fusion.half_ref), channel_id=1, source_target_pairs={{0,8},{1,9},{2,10},{3,11},{4,12},{5,13},{6,14},{7,15},{8,0},{9,1},... | collective-permute-start | bytes 393224 | tf_op jit(solution)/shard_map/ppermute | solution.py:451
  9.4 3.4 %collective-permute-start.2 = (bf16[256,256]{1,0:T(8,128)(2,1)S(1)}, bf16[256,256]{1,0:T(8,128)(2,1)S(1)}, u32[]{:S(2)}, u32[]{:S(2)}) collective-permute-start(bf16[256,256]{1,0:T(8,128)(2,1)S(1)} %get-tuple-element.42), channel_id=1, source_target_pairs={{0,1},{1,0},{2,3},{3,2},{4,5},{5,4},{6,7},{7,6},{8,9},{9,8},{10,11... | collective-permute-start | bytes 393224 | tf_op jit(solution)/shard_map/ppermute | solution.py:447
  9.4 3.4 %collective-permute-start.3 = (bf16[256,256]{1,0:T(8,128)(2,1)S(1)}, bf16[256,256]{1,0:T(8,128)(2,1)S(1)}, u32[]{:S(2)}, u32[]{:S(2)}) collective-permute-start(bf16[256,256]{1,0:T(8,128)(2,1)S(1)} %get-tuple-element.43), channel_id=1, source_target_pairs={{0,1},{1,0},{2,3},{3,2},{4,5},{5,4},{6,7},{7,6},{8,9},{9,8},{10,11... | collective-permute-start | bytes 393224 | tf_op jit(solution)/shard_map/ppermute | solution.py:447
  9.9 2.9 %collective-permute-start.4 = (bf16[256,256]{1,0:T(8,128)(2,1)S(1)}, bf16[256,256]{1,0:T(8,128)(2,1)S(1)}, u32[]{:S(2)}, u32[]{:S(2)}) collective-permute-start(bf16[256,256]{1,0:T(8,128)(2,1)S(1)} %get-tuple-element.44), channel_id=1, source_target_pairs={{0,1},{1,0},{2,3},{3,2},{4,5},{5,4},{6,7},{7,6},{8,9},{9,8},{10,11... | collective-permute-start | bytes 393224 | tf_op jit(solution)/shard_map/ppermute | solution.py:447
  10.0 2.9 %collective-permute-start.5 = (bf16[256,256]{1,0:T(8,128)(2,1)S(1)}, bf16[256,256]{1,0:T(8,128)(2,1)S(1)}, u32[]{:S(2)}, u32[]{:S(2)}) collective-permute-start(bf16[256,256]{1,0:T(8,128)(2,1)S(1)} %get-tuple-element.45), channel_id=1, source_target_pairs={{0,1},{1,0},{2,3},{3,2},{4,5},{5,4},{6,7},{7,6},{8,9},{9,8},{10,11... | collective-permute-start | bytes 393224 | tf_op jit(solution)/shard_map/ppermute | solution.py:447
  12.8 5.0 %collective-permute-start.6 = (bf16[1,512,128]{2,1,0:T(8,128)(2,1)S(1)}, bf16[1,512,128]{2,1,0:T(8,128)(2,1)S(1)}, u32[]{:S(2)}, u32[]{:S(2)}) collective-permute-start(bf16[1,512,128]{2,1,0:T(8,128)(2,1)S(1)} %collective-permute-done.1.refs_1_), channel_id=1, source_target_pairs={{0,4},{1,5},{2,6},{3,7},{4,0},{5,1},{6,2},{7,3},{8,12},{9,13},{10,... | collective-permute-start | bytes 393224 | tf_op jit(solution)/shard_map/ppermute | solution.py:451
  13.5 14.9 %collective-permute-start.9 = (bf16[2,2,256,256]{3,2,1,0:T(8,128)(2,1)S(1)}, bf16[2,2,256,256]{3,2,1,0:T(8,128)(2,1)S(1)}, u32[]{:S(2)}, u32[]{:S(2)}) collective-permute-start(bf16[2,2,256,256]{3,2,1,0:T(8,128)(2,1)S(1)} %get-tuple-element.54), channel_id=1, source_target_pairs={{0,2},{1,3},{2,0},{3,1},{4,6},{5,7},{6,4},{7,5},{8,10},{9,11},{10,... | collective-permute-start | bytes 1572872 | tf_op jit(solution)/shard_map/ppermute | solution.py:447
  15.0 16.7 %collective-permute-start.8 = (bf16[2,2,256,256]{3,2,1,0:T(8,128)(2,1)S(1)}, bf16[2,2,256,256]{3,2,1,0:T(8,128)(2,1)S(1)}, u32[]{:S(2)}, u32[]{:S(2)}) collective-permute-start(bf16[2,2,256,256]{3,2,1,0:T(8,128)(2,1)S(1)} %get-tuple-element.53.mine_ref), channel_id=1, source_target_pairs={{0,4},{1,5},{2,6},{3,7},{4,8},{5,9},{6,10},{7,11},{8,12},{9,13},{1... | collective-permute-start | bytes 1572872 | tf_op jit(solution)/shard_map/ppermute | solution.py:447
  17.9 8.9 %collective-permute-start.7 = (bf16[3,512,128]{2,1,0:T(8,128)(2,1)S(1)}, bf16[3,512,128]{2,1,0:T(8,128)(2,1)S(1)}, u32[]{:S(2)}, u32[]{:S(2)}) collective-permute-start(bf16[3,512,128]{2,1,0:T(8,128)(2,1)S(1)} %shard_map.92.near_ref), channel_id=1, source_target_pairs={{0,16},{16,0},{1,17},{17,1},{2,18},{18,2},{3,19},{19,3},{4,20},{20... | collective-permute-start | bytes 1179656 | tf_op jit(solution)/shard_map/ppermute | solution.py:212
  19.5 18.0 %collective-permute-start.11 = (bf16[2,256,256]{2,1,0:T(8,128)(2,1)S(1)}, bf16[2,256,256]{2,1,0:T(8,128)(2,1)S(1)}, u32[]{:S(2)}, u32[]{:S(2)}) collective-permute-start(bf16[2,256,256]{2,1,0:T(8,128)(2,1)S(1)} %get-tuple-element.58), channel_id=1, source_target_pairs={{0,6},{1,7},{2,4},{3,5},{4,10},{5,11},{6,8},{7,9},{8,14},{9,15},{1... | collective-permute-start | bytes 786440 | tf_op jit(solution)/shard_map/ppermute | solution.py:447
  22.3 20.1 %collective-permute-start.10 = (bf16[2,256,256]{2,1,0:T(8,128)(2,1)S(1)}, bf16[2,256,256]{2,1,0:T(8,128)(2,1)S(1)}, u32[]{:S(2)}, u32[]{:S(2)}) collective-permute-start(bf16[2,256,256]{2,1,0:T(8,128)(2,1)S(1)} %get-tuple-element.57), channel_id=1, source_target_pairs={{0,6},{1,7},{2,4},{3,5},{4,10},{5,11},{6,8},{7,9},{8,14},{9,15},{1... | collective-permute-start | bytes 786440 | tf_op jit(solution)/shard_map/ppermute | solution.py:447
  28.3 9.2 %copy-start.3 = (bf16[256,512]{1,0:T(8,128)(2,1)S(1)}, bf16[256,512]{1,0:T(8,128)(2,1)}, u32[]{:S(2)}) copy-start(bf16[256,512]{1,0:T(8,128)(2,1)} %constant.23.clone.back_low_ref) | copy-start | bytes 786436
  28.3 9.2 %copy-start.4 = (bf16[256,512]{1,0:T(8,128)(2,1)S(1)}, bf16[256,512]{1,0:T(8,128)(2,1)}, u32[]{:S(2)}) copy-start(bf16[256,512]{1,0:T(8,128)(2,1)} %constant.22.clone.back_high_ref) | copy-start | bytes 786436
  28.3 9.2 %copy-start.6 = (f32[2048]{0:T(1024)S(1)}, f32[2048]{0:T(1024)}, u32[]{:S(2)}) copy-start(f32[2048]{0:T(1024)} %param.13) | copy-start | bytes 24580
  40.1 6.2 %collective-permute-start.15 = (bf16[256,256]{1,0:T(8,128)(2,1)S(1)}, bf16[256,256]{1,0:T(8,128)(2,1)S(1)}, u32[]{:S(2)}, u32[]{:S(2)}) collective-permute-start(bf16[256,256]{1,0:T(8,128)(2,1)S(1)} %get-tuple-element.66), channel_id=1, source_target_pairs={{0,1},{1,0},{2,3},{3,2},{4,5},{5,4},{6,7},{7,6},{8,9},{9,8},{10,11... | collective-permute-start | bytes 393224 | tf_op jit(solution)/shard_map/ppermute | solution.py:447
  40.2 6.7 %collective-permute-start.16 = (bf16[256,256]{1,0:T(8,128)(2,1)S(1)}, bf16[256,256]{1,0:T(8,128)(2,1)S(1)}, u32[]{:S(2)}, u32[]{:S(2)}) collective-permute-start(bf16[256,256]{1,0:T(8,128)(2,1)S(1)} %get-tuple-element.67), channel_id=1, source_target_pairs={{0,2},{1,3},{2,0},{3,1},{4,6},{5,7},{6,4},{7,5},{8,10},{9,11},{10,... | collective-permute-start | bytes 393224 | tf_op jit(solution)/shard_map/ppermute | solution.py:447
  41.5 6.9 %collective-permute-start.17 = (bf16[256,256]{1,0:T(8,128)(2,1)S(1)}, bf16[256,256]{1,0:T(8,128)(2,1)S(1)}, u32[]{:S(2)}, u32[]{:S(2)}) collective-permute-start(bf16[256,256]{1,0:T(8,128)(2,1)S(1)} %get-tuple-element.68), channel_id=1, source_target_pairs={{0,3},{1,2},{2,1},{3,0},{4,7},{5,6},{6,5},{7,4},{8,11},{9,10},{10,... | collective-permute-start | bytes 393224 | tf_op jit(solution)/shard_map/ppermute | solution.py:447
  42.4 6.1 %copy-start.2 = (bf16[256,2048]{1,0:T(8,128)(2,1)S(1)}, bf16[256,2048]{1,0:T(8,128)(2,1)}, u32[]{:S(2)}) copy-start(bf16[256,2048]{1,0:T(8,128)(2,1)} %gate_ref.3) | copy-start | bytes 3145732
  45.0 4.5 %collective-permute-start.12 = (bf16[256,256]{1,0:T(8,128)(2,1)S(1)}, bf16[256,256]{1,0:T(8,128)(2,1)S(1)}, u32[]{:S(2)}, u32[]{:S(2)}) collective-permute-start(bf16[256,256]{1,0:T(8,128)(2,1)S(1)} %get-tuple-element.62), channel_id=1, source_target_pairs={{0,1},{1,0},{2,3},{3,2},{4,5},{5,4},{6,7},{7,6},{8,9},{9,8},{10,11... | collective-permute-start | bytes 393224 | tf_op jit(solution)/shard_map/ppermute | solution.py:447
  45.0 7.1 %collective-permute-start.13 = (bf16[256,256]{1,0:T(8,128)(2,1)S(1)}, bf16[256,256]{1,0:T(8,128)(2,1)S(1)}, u32[]{:S(2)}, u32[]{:S(2)}) collective-permute-start(bf16[256,256]{1,0:T(8,128)(2,1)S(1)} %get-tuple-element.63), channel_id=1, source_target_pairs={{0,2},{1,3},{2,0},{3,1},{4,6},{5,7},{6,4},{7,5},{8,10},{9,11},{10,... | collective-permute-start | bytes 393224 | tf_op jit(solution)/shard_map/ppermute | solution.py:447
  46.3 7.7 %collective-permute-start.14 = (bf16[256,256]{1,0:T(8,128)(2,1)S(1)}, bf16[256,256]{1,0:T(8,128)(2,1)S(1)}, u32[]{:S(2)}, u32[]{:S(2)}) collective-permute-start(bf16[256,256]{1,0:T(8,128)(2,1)S(1)} %get-tuple-element.64), channel_id=1, source_target_pairs={{0,3},{1,2},{2,1},{3,0},{4,7},{5,6},{6,5},{7,4},{8,11},{9,10},{10,... | collective-permute-start | bytes 393224 | tf_op jit(solution)/shard_map/ppermute | solution.py:447

commit v5 on v4

--- a/solution.py
+++ b/solution.py
@@ -14,6 +14,7 @@
 BF16 = jnp.bfloat16
 F32 = jnp.float32
 VMEM = pl.BlockSpec(memory_space=pltpu.VMEM)
+GATE_ORDER = (0, 2, 3, 1)
 SMALL = pl.CostEstimate(flops=1000, bytes_accessed=1000, transcendentals=0)
 
 
@@ -185,12 +186,27 @@
     put_tap_spectra(high_ref, low_ref, taps, out_ref)
 
 
+def half_kernel(taps_hbm, half_ref, sem):
+    half = half_ref.shape[1]
+    rows = aligned(lax.axis_index("groups"), half)
+    copy = pltpu.make_async_copy(taps_hbm.at[rows], half_ref.at[0], sem)
+    copy.start()
+    copy.wait()
+
+
 def near_half(filter_taps, layers, groups):
     count, width = filter_taps.shape
     if width != LANES or groups != 2 or layers != 4:
         return None
-    start = lax.axis_index("groups") * (count // 2)
-    return lax.dynamic_slice_in_dim(filter_taps, start, count // 2, 0)[None]
+    return pl.pallas_call(
+        half_kernel,
+        in_specs=[pl.BlockSpec(memory_space=pltpu.HBM)],
+        out_specs=VMEM,
+        out_shape=jax.ShapeDtypeStruct((1, count // 2, width), BF16),
+        scratch_shapes=[pltpu.SemaphoreType.DMA],
+        compiler_params=params(8),
+        cost_estimate=SMALL,
+    )(pltpu.with_memory_space_constraint(filter_taps, pltpu.HBM))
 
 
 def tap_spectra(tables, filter_taps, near, layers, members):
@@ -388,14 +404,25 @@
 
 
 def gate_kernel(layers, members, part, gate_ref, *refs):
-    piece_refs, out_ref = refs[:members], refs[-1]
+    piece_refs, (out_hbm, out, sems) = refs[:members], refs[-3:]
     member, _ = place(members)
-    for apart in range(members):
-        held = member ^ apart
-        for layer in range(layers):
-            lanes = aligned(layer * members + held, LANES)
-            mixed = piece_refs[apart][:, layer * LANES : (layer + 1) * LANES].astype(F32)
-            out_ref[:, lanes] = (gate_ref[:, lanes].astype(F32) * mixed).astype(BF16)
+    count = sems.shape[0]
+    step, wide = out.shape[0] // count, out.shape[1]
+    here = slice(part * wide, (part + 1) * wide)
+    copies = []
+    for index in range(count):
+        rows = slice(index * step, (index + 1) * step)
+        for which, apart in enumerate(GATE_ORDER):
+            held = member ^ apart
+            for layer in range(layers):
+                lanes = aligned(layer * members + held, LANES)
+                source = aligned((part * layers + layer) * members + held, LANES)
+                mixed = piece_refs[which][rows, layer * LANES : (layer + 1) * LANES].astype(F32)
+                out[rows, lanes] = (gate_ref[rows, source].astype(F32) * mixed).astype(BF16)
+        copies.append(pltpu.make_async_copy(out.at[rows], out_hbm.at[rows, here], sems.at[index]))
+        copies[-1].start()
+    for copy in copies:
+        copy.wait()
 
 
 def gated_output(part, gate_out, pieces, layers, members, out):
@@ -413,21 +440,18 @@
         gate = gate_out[:, part * wide : (part + 1) * wide].astype(F32)
         gated = (gate * mixed.reshape(rows, wide).astype(F32)).astype(BF16)
         return gated if out is None else jnp.concatenate([out, gated], axis=1)
-    step = rows // 2
-    there = pl.BlockSpec((step, wide), lambda r: (r, part))
     more = [] if out is None else [out]
+    count = 2
     return pl.pallas_call(
         functools.partial(gate_kernel, layers // CHUNKS, members, part),
-        grid=(2,),
-        in_specs=[there]
-        + [pl.BlockSpec((step, chunk), lambda r: (r, 0))] * members
-        + [pl.BlockSpec(memory_space=pl.ANY)] * len(more),
-        out_specs=there,
+        in_specs=[VMEM] * (1 + members) + [pl.BlockSpec(memory_space=pl.ANY)] * len(more),
+        out_specs=pl.BlockSpec(memory_space=pl.ANY),
         out_shape=jax.ShapeDtypeStruct((rows, channels), BF16),
+        scratch_shapes=[pltpu.VMEM((rows, wide), BF16), pltpu.SemaphoreType.DMA((count,))],
         input_output_aliases={members + 1: 0} if more else {},
-        compiler_params=params(16),
-        cost_estimate=SMALL,
-    )(gate_out, *pieces, *more)
+        compiler_params=params(8),
+        cost_estimate=SMALL,
+    )(gate_out, *(pieces[apart] for apart in GATE_ORDER), *more)
 
 
 def on_device(gate_out, gate_in, values, filter_taps, skip_gain):

time: 55.3 us -> 54.1 us (0.978)
  waiting for transfers between devices: 20.2 us -> 18.6 us
  local copies, waits for them, and re-layouts: 1.02 us -> 0.03 us
  Pallas kernels: 14.2 us -> 14.8 us
    ppermute x14, waiting for transfers between devices: 12 us -> 10.5 us  [to_member(): return lax.ppermute(value, 'ctx', pairs)]
    broadcast_in_dim x1 -> x0, local copies, waits for them, and re-layouts: 0.99 us -> none  [near_half(): return lax.dynamic_slice_in_dim(filter_taps, start, count // 2, 0)[None]]
    pallas_call x0 -> x1, Pallas kernels: none -> 0.98 us  [near_half(): pl.pallas_call(half_kernel, in_specs=[pl.BlockSpec(memory_space=pltpu.HBM...]
  transfers between devices with their start and end apart: 18 -> 18, of which waited for: 10 -> 9; matrix products, arithmetic and copies ran while one was open for 0% -> 0% of each run, Pallas kernels for 24% -> 24%
where the time goes in v5:
time: 54.1 us; the launch traced here: 53.8 us
  starting transfers between devices  20.2 us (37%)
  waiting for transfers between devices  18.6 us (34%)
  Pallas kernels  14.8 us (27%)
    ppermute x14, starting transfers between devices, to_member(): return lax.ppermute(value, 'ctx', pairs)  12.4 us
    ppermute x14, waiting for transfers between devices, to_member(): return lax.ppermute(value, 'ctx', pairs)  10.5 us
    ppermute x3, starting transfers between devices, to_layer(): return lax.ppermute(value, 'ctx', pairs)  6.2 us
    pallas_call x2, Pallas kernels, mixed_pieces(): pl.pallas_call(functools.partial(mix_kernel, members, part), in_specs=[VM...  5.15 us
    ppermute x3, waiting for transfers between devices, to_layer(): return lax.ppermute(value, 'ctx', pairs)  4.64 us
    pallas_call x1, Pallas kernels, own_partials(): pl.pallas_call(functools.partial(own_kernel, members), in_specs=[VMEM] *...  3.56 us
    ppermute x1, waiting for transfers between devices, tap_spectra(): far = lax.ppermute(near, 'groups', [(0, 1), (1, 0)])  3.52 us
    pallas_call x2, Pallas kernels, gated_output(): pl.pallas_call(functools.partial(gate_kernel, layers // CHUNKS, members,...  1.81 us
  transfers between devices with their start and end apart: 18, of which 9 were waited for; matrix products, arithmetic and copies ran while one was open for 0% of the time, Pallas kernels for 24%

profile of v5, /device:TPU:0, one launch (start us, length us, event | category | flops | bytes accessed | tf_op | source)
XLA Modules:
  0.0 53.8 jit_solution(15075003809437383826)
XLA Ops:
  0.0 1.0 %shard_map.91.half_ref = bf16[1,512,128]{2,1,0:T(8,128)(2,1)S(1)} custom-call(bf16[1024,128]{1,0:T(8,128)(2,1)} %own_ref.1), custom_call_target="tpu_custom_call" | custom-call | flops 1000 | bytes 1000 | tf_op jit(solution)/shard_map/pallas_call | solution.py:201
  1.0 3.1 %collective-permute-start = (bf16[1,512,128]{2,1,0:T(8,128)(2,1)S(1)}, bf16[1,512,128]{2,1,0:T(8,128)(2,1)S(1)}, u32[]{:S(2)}, u32[]{:S(2)}) collective-permute-start(bf16[1,512,128]{2,1,0:T(8,128)(2,1)S(1)} %shard_map.91.half_ref), channel_id=1, source_target_pairs={{0,4},{1,5},{2,6},{3,7},{4,0},{5,1},{6,2},{7,3},{8,12},{9,13},{10,... | collective-permute-start | bytes 393224 | tf_op jit(solution)/shard_map/ppermute | solution.py:475
  4.1 2.6 %collective-permute-start.1 = (bf16[1,512,128]{2,1,0:T(8,128)(2,1)S(1)}, bf16[1,512,128]{2,1,0:T(8,128)(2,1)S(1)}, u32[]{:S(2)}, u32[]{:S(2)}) collective-permute-start(bf16[1,512,128]{2,1,0:T(8,128)(2,1)S(1)} %shard_map.91.half_ref), channel_id=1, source_target_pairs={{0,8},{1,9},{2,10},{3,11},{4,12},{5,13},{6,14},{7,15},{8,0},{9,1},... | collective-permute-start | bytes 393224 | tf_op jit(solution)/shard_map/ppermute | solution.py:475
  6.7 1.7 %shard_map.92 = (bf16[2,256,256]{2,1,0:T(8,128)(2,1)S(1)}, bf16[2,256,256]{2,1,0:T(8,128)(2,1)S(1)}, bf16[256,256]{1,0:T(8,128)(2,1)S(1)}, bf16[256,256]{1,0:T(8...) custom-call(bf16[256,2048]{1,0:T(8,128)(2,1)} %gate_hbm.1, bf16[256,2048]{1,0:T(8,128)(2,1)} %values_hbm.1, ...), custom_call_target="tpu_custom_call" | custom-call | flops 1000 | bytes 1000 | tf_op jit(solution)/shard_map/pallas_call | solution.py:113
  8.4 1.0 %collective-permute-done.refs_0_ = bf16[1,512,128]{2,1,0:T(8,128)(2,1)S(1)} collective-permute-done((bf16[1,512,128]{2,1,0:T(8,128)(2,1)S(1)}, bf16[1,512,128]{2,1,0:T(8,128)(2,1)S(1)}, u32[]{:S(2)}, u32[]{:S(2)}) %collective-permute-start) | collective-permute-done | bytes 131104 | tf_op jit(solution)/shard_map/ppermute | solution.py:475
  9.4 0.5 collective-permute-start.3
  10.0 0.5 collective-permute-start.5
  10.5 2.4 %collective-permute-done.1.refs_1_ = bf16[1,512,128]{2,1,0:T(8,128)(2,1)S(1)} collective-permute-done((bf16[1,512,128]{2,1,0:T(8,128)(2,1)S(1)}, bf16[1,512,128]{2,1,0:T(8,128)(2,1)S(1)}, u32[]{:S(2)}, u32[]{:S(2)}) %collective-permute-start.1) | collective-permute-done | bytes 131104 | tf_op jit(solution)/shard_map/ppermute | solution.py:475
  12.8 0.5 collective-permute-start.6
  13.4 0.1 shard_map.95
  13.5 1.6 %collective-permute-start.9 = (bf16[2,2,256,256]{3,2,1,0:T(8,128)(2,1)S(1)}, bf16[2,2,256,256]{3,2,1,0:T(8,128)(2,1)S(1)}, u32[]{:S(2)}, u32[]{:S(2)}) collective-permute-start(bf16[2,2,256,256]{3,2,1,0:T(8,128)(2,1)S(1)} %get-tuple-element.54), channel_id=1, source_target_pairs={{0,2},{1,3},{2,0},{3,1},{4,6},{5,7},{6,4},{7,5},{8,10},{9,11},{10,... | collective-permute-start | bytes 1572872 | tf_op jit(solution)/shard_map/ppermute | solution.py:471
  15.0 1.6 %collective-permute-start.8 = (bf16[2,2,256,256]{3,2,1,0:T(8,128)(2,1)S(1)}, bf16[2,2,256,256]{3,2,1,0:T(8,128)(2,1)S(1)}, u32[]{:S(2)}, u32[]{:S(2)}) collective-permute-start(bf16[2,2,256,256]{3,2,1,0:T(8,128)(2,1)S(1)} %get-tuple-element.53.mine_ref), channel_id=1, source_target_pairs={{0,4},{1,5},{2,6},{3,7},{4,8},{5,9},{6,10},{7,11},{8,12},{9,13},{1... | collective-permute-start | bytes 1572872 | tf_op jit(solution)/shard_map/ppermute | solution.py:471
  16.6 1.3 %collective-permute-done.6.refs_2_ = bf16[1,512,128]{2,1,0:T(8,128)(2,1)S(1)} collective-permute-done((bf16[1,512,128]{2,1,0:T(8,128)(2,1)S(1)}, bf16[1,512,128]{2,1,0:T(8,128)(2,1)S(1)}, u32[]{:S(2)}, u32[]{:S(2)}) %collective-permute-start.6) | collective-permute-done | bytes 131104 | tf_op jit(solution)/shard_map/ppermute | solution.py:475
  17.9 1.6 %collective-permute-start.7 = (bf16[3,512,128]{2,1,0:T(8,128)(2,1)S(1)}, bf16[3,512,128]{2,1,0:T(8,128)(2,1)S(1)}, u32[]{:S(2)}, u32[]{:S(2)}) collective-permute-start(bf16[3,512,128]{2,1,0:T(8,128)(2,1)S(1)} %shard_map.93.near_ref), channel_id=1, source_target_pairs={{0,16},{16,0},{1,17},{17,1},{2,18},{18,2},{3,19},{19,3},{4,20},{20... | collective-permute-start | bytes 1179656 | tf_op jit(solution)/shard_map/ppermute | solution.py:228
  19.5 2.8 %collective-permute-start.11 = (bf16[2,256,256]{2,1,0:T(8,128)(2,1)S(1)}, bf16[2,256,256]{2,1,0:T(8,128)(2,1)S(1)}, u32[]{:S(2)}, u32[]{:S(2)}) collective-permute-start(bf16[2,256,256]{2,1,0:T(8,128)(2,1)S(1)} %get-tuple-element.58), channel_id=1, source_target_pairs={{0,6},{1,7},{2,4},{3,5},{4,10},{5,11},{6,8},{7,9},{8,14},{9,15},{1... | collective-permute-start | bytes 786440 | tf_op jit(solution)/shard_map/ppermute | solution.py:471
  22.3 1.0 %collective-permute-start.10 = (bf16[2,256,256]{2,1,0:T(8,128)(2,1)S(1)}, bf16[2,256,256]{2,1,0:T(8,128)(2,1)S(1)}, u32[]{:S(2)}, u32[]{:S(2)}) collective-permute-start(bf16[2,256,256]{2,1,0:T(8,128)(2,1)S(1)} %get-tuple-element.57), channel_id=1, source_target_pairs={{0,6},{1,7},{2,4},{3,5},{4,10},{5,11},{6,8},{7,9},{8,14},{9,15},{1... | collective-permute-start | bytes 786440 | tf_op jit(solution)/shard_map/ppermute | solution.py:471
  23.3 3.5 %collective-permute-done.7.far_ref = bf16[3,512,128]{2,1,0:T(8,128)(2,1)S(1)} collective-permute-done((bf16[3,512,128]{2,1,0:T(8,128)(2,1)S(1)}, bf16[3,512,128]{2,1,0:T(8,128)(2,1)S(1)}, u32[]{:S(2)}, u32[]{:S(2)}) %collective-permute-start.7) | collective-permute-done | bytes 393248 | tf_op jit(solution)/shard_map/ppermute | solution.py:228
  26.8 1.5 %shard_map.94.taps_ref = f32[2,4,512,256]{3,2,1,0:T(8,128)S(1)} custom-call(bf16[512,256]{1,0:T(8,128)(2,1)S(1)} %copy-done.1, bf16[512,256]{1,0:T(8,128)(2,1)S(1)} %copy-done, bf16[1024,128]{1,0:T(8,128)(2,1)S(1)} %copy-done.5, bf16[3,512,128]{2,1,0:T(8,128)(2,1)S(1)} %shard_map.93.near_ref, bf16[3,512,128]{2,1,0:T(8,128)(2,1)S(1)} %collective-permute-done.7.far_ref), custom_call_target="tpu_custom_call" | custom-call | flops 1000 | bytes 1000 | tf_op jit(solution)/shard_map/pallas_call | solution.py:229
  28.4 3.4 %collective-permute-done.8.ahead_ref = bf16[2,2,256,256]{3,2,1,0:T(8,128)(2,1)S(1)} collective-permute-done((bf16[2,2,256,256]{3,2,1,0:T(8,128)(2,1)S(1)}, bf16[2,2,256,256]{3,2,1,0:T(8,128)(2,1)S(1)}, u32[]{:S(2)}, u32[]{:S(2)}) %collective-permute-start.8) | collective-permute-done | bytes 524320 | tf_op jit(solution)/shard_map/ppermute | solution.py:471
  31.7 3.6 %shard_map.96 = (f32[2,3,512,256]{3,2,1,0:T(8,128)S(1)}, f32[2,512,256]{2,1,0:T(8,128)S(1)}, f32[2,4,512,256]{3,2,1,0:T(8,128)S(1)}) custom-call(bf16[512,256]{1,0:T(8,128)(2,1)S(1)} %copy-done.1, bf16[512,256]{1,0:T(8,128)(2,1)S(1)} %copy-done, f32[2,4,512,256]{3,2,1,0:T(8,128)S(1)} %shard_map.94.taps_ref, ...), custom_call_target="tpu_custom_call" | custom-call | flops 1000 | bytes 1000 | tf_op jit(solution)/shard_map/pallas_call | solution.py:305
  35.3 2.2 %collective-permute-done.11.beyond_ref = bf16[2,256,256]{2,1,0:T(8,128)(2,1)S(1)} collective-permute-done((bf16[2,256,256]{2,1,0:T(8,128)(2,1)S(1)}, bf16[2,256,256]{2,1,0:T(8,128)(2,1)S(1)}, u32[]{:S(2)}, u32[]{:S(2)}) %collective-permute-start.11) | collective-permute-done | bytes 262176 | tf_op jit(solution)/shard_map/ppermute | solution.py:471
  37.5 2.6 %shard_map.97 = (bf16[256,256]{1,0:T(8,128)(2,1)S(1)}, bf16[256,256]{1,0:T(8,128)(2,1)S(1)}, bf16[256,256]{1,0:T(8,128)(2,1)S(1)}, bf16[256,256]{1,0:T(8,128)(2,1)S(1)}, f32[2,4,512,256]{3,2,1,0:T(8,128)S(1)}) custom-call(bf16[512,256]{1,0:T(8,128)(2,1)S(1)} %copy-done.1, bf16[512,256]{1,0:T(8,128)(2,1)S(1)} %copy-done, ...), custom_call_target="tpu_custom_call", output_to_operand_aliasing={{4}: (11, {})} | custom-call | flops 1000 | bytes 1000 | tf_op jit(solution)/shard_map/pallas_call | solution.py:392
  40.1 1.3 %collective-permute-start.15 = (bf16[256,256]{1,0:T(8,128)(2,1)S(1)}, bf16[256,256]{1,0:T(8,128)(2,1)S(1)}, u32[]{:S(2)}, u32[]{:S(2)}) collective-permute-start(bf16[256,256]{1,0:T(8,128)(2,1)S(1)} %get-tuple-element.66), channel_id=1, source_target_pairs={{0,2},{1,3},{2,0},{3,1},{4,6},{5,7},{6,4},{7,5},{8,10},{9,11},{10,... | collective-permute-start | bytes 393224 | tf_op jit(solution)/shard_map/ppermute | solution.py:471
  41.4 0.9 %collective-permute-start.17 = (bf16[256,256]{1,0:T(8,128)(2,1)S(1)}, bf16[256,256]{1,0:T(8,128)(2,1)S(1)}, u32[]{:S(2)}, u32[]{:S(2)}) collective-permute-start(bf16[256,256]{1,0:T(8,128)(2,1)S(1)} %get-tuple-element.68), channel_id=1, source_target_pairs={{0,1},{1,0},{2,3},{3,2},{4,5},{5,4},{6,7},{7,6},{8,9},{9,8},{10,11... | collective-permute-start | bytes 393224 | tf_op jit(solution)/shard_map/ppermute | solution.py:471
  42.3 0.2 collective-permute-done.10.beyond_ref
  42.5 2.6 %shard_map.98 = (bf16[256,256]{1,0:T(8,128)(2,1)S(1)}, bf16[256,256]{1,0:T(8,128)(2,1)S(1)}, bf16[256,256]{1,0:T(8,128)(2,1)S(1)}, bf16[256,256]{1,0:T(8,128)(2,1)S(1)}, f32[2,4,512,256]{3,2,1,0:T(8,128)S(1)}) custom-call(bf16[512,256]{1,0:T(8,128)(2,1)S(1)} %copy-done.1, bf16[512,256]{1,0:T(8,128)(2,1)S(1)} %copy-done, ...), custom_call_target="tpu_custom_call", output_to_operand_aliasing={{4}: (11, {})} | custom-call | flops 1000 | bytes 1000 | tf_op jit(solution)/shard_map/pallas_call | solution.py:392
  45.1 1.2 %collective-permute-start.12 = (bf16[256,256]{1,0:T(8,128)(2,1)S(1)}, bf16[256,256]{1,0:T(8,128)(2,1)S(1)}, u32[]{:S(2)}, u32[]{:S(2)}) collective-permute-start(bf16[256,256]{1,0:T(8,128)(2,1)S(1)} %get-tuple-element.62), channel_id=1, source_target_pairs={{0,2},{1,3},{2,0},{3,1},{4,6},{5,7},{6,4},{7,5},{8,10},{9,11},{10,... | collective-permute-start | bytes 393224 | tf_op jit(solution)/shard_map/ppermute | solution.py:471
  46.3 1.0 %collective-permute-start.14 = (bf16[256,256]{1,0:T(8,128)(2,1)S(1)}, bf16[256,256]{1,0:T(8,128)(2,1)S(1)}, u32[]{:S(2)}, u32[]{:S(2)}) collective-permute-start(bf16[256,256]{1,0:T(8,128)(2,1)S(1)} %get-tuple-element.64), channel_id=1, source_target_pairs={{0,1},{1,0},{2,3},{3,2},{4,5},{5,4},{6,7},{7,6},{8,9},{9,8},{10,11... | collective-permute-start | bytes 393224 | tf_op jit(solution)/shard_map/ppermute | solution.py:471
  47.3 0.9 %shard_map.99.refs_4_ = bf16[256,2048]{1,0:T(8,128)(2,1)} custom-call(bf16[256,2048]{1,0:T(8,128)(2,1)S(1)} %copy-done.2, bf16[256,256]{1,0:T(8,128)(2,1)S(1)} %get-tuple-element.65.refs_0_, bf16[256,256]{1,0:T(8,128)(2,1)S(1)} %collective-permute-done.15.refs_1_, bf16[256,256]{1,0:T(8,128)(2,1)S(1)} %collective-permute-done.16.refs_2_, ...), custom_call_target="tpu_custom_call" | custom-call | flops 1000 | bytes 1000 | tf_op jit(solution)/shard_map/pallas_call | solution.py:445
  48.2 3.3 %collective-permute-done.12.refs_1_ = bf16[256,256]{1,0:T(8,128)(2,1)S(1)} collective-permute-done((bf16[256,256]{1,0:T(8,128)(2,1)S(1)}, bf16[256,256]{1,0:T(8,128)(2,1)S(1)}, u32[]{:S(2)}, u32[]{:S(2)}) %collective-permute-start.12) | collective-permute-done | bytes 131104 | tf_op jit(solution)/shard_map/ppermute | solution.py:471
  51.5 1.4 %collective-permute-done.13.refs_2_ = bf16[256,256]{1,0:T(8,128)(2,1)S(1)} collective-permute-done((bf16[256,256]{1,0:T(8,128)(2,1)S(1)}, bf16[256,256]{1,0:T(8,128)(2,1)S(1)}, u32[]{:S(2)}, u32[]{:S(2)}) %collective-permute-start.13) | collective-permute-done | bytes 131104 | tf_op jit(solution)/shard_map/ppermute | solution.py:471
  52.9 0.9 %shard_map.100 = bf16[256,2048]{1,0:T(8,128)(2,1)} custom-call(bf16[256,2048]{1,0:T(8,128)(2,1)S(1)} %copy-done.2, bf16[256,256]{1,0:T(8,128)(2,1)S(1)} %get-tuple-element.61.refs_0_, bf16[256,256]{1,0:T(8,128)(2,1)S(1)} %collective-permute-done.12.refs_1_, bf16[256,256]{1,0:T(8,128)(2,1)S(1)} %collective-permute-done.13.refs_2_, ...), custom_call_target="tpu_custom_call", output_to_operand_aliasing={{}: (5, {})} | custom-call | flops 1000 | bytes 1000 | tf_op jit(solution)/shard_map/pallas_call | solution.py:445
  (28 shorter events, 0.2 us)
Async XLA Ops:
  0.0 26.8 %copy-start = (bf16[512,256]{1,0:T(8,128)(2,1)S(1)}, bf16[512,256]{1,0:T(8,128)(2,1)}, u32[]{:S(2)}) copy-start(bf16[512,256]{1,0:T(8,128)(2,1)} %constant.9.clone.low_ref) | copy-start | bytes 786436
  0.0 26.8 %copy-start.1 = (bf16[512,256]{1,0:T(8,128)(2,1)S(1)}, bf16[512,256]{1,0:T(8,128)(2,1)}, u32[]{:S(2)}) copy-start(bf16[512,256]{1,0:T(8,128)(2,1)} %constant.8.clone.high_ref) | copy-start | bytes 786436
  0.0 26.8 %copy-start.5 = (bf16[1024,128]{1,0:T(8,128)(2,1)S(1)}, bf16[1024,128]{1,0:T(8,128)(2,1)}, u32[]{:S(2)}) copy-start(bf16[1024,128]{1,0:T(8,128)(2,1)} %own_ref.1) | copy-start | bytes 786436
  1.0 8.4 %collective-permute-start = (bf16[1,512,128]{2,1,0:T(8,128)(2,1)S(1)}, bf16[1,512,128]{2,1,0:T(8,128)(2,1)S(1)}, u32[]{:S(2)}, u32[]{:S(2)}) collective-permute-start(bf16[1,512,128]{2,1,0:T(8,128)(2,1)S(1)} %shard_map.91.half_ref), channel_id=1, source_target_pairs={{0,4},{1,5},{2,6},{3,7},{4,0},{5,1},{6,2},{7,3},{8,12},{9,13},{10,... | collective-permute-start | bytes 393224 | tf_op jit(solution)/shard_map/ppermute | solution.py:475
  4.1 8.7 %collective-permute-start.1 = (bf16[1,512,128]{2,1,0:T(8,128)(2,1)S(1)}, bf16[1,512,128]{2,1,0:T(8,128)(2,1)S(1)}, u32[]{:S(2)}, u32[]{:S(2)}) collective-permute-start(bf16[1,512,128]{2,1,0:T(8,128)(2,1)S(1)} %shard_map.91.half_ref), channel_id=1, source_target_pairs={{0,8},{1,9},{2,10},{3,11},{4,12},{5,13},{6,14},{7,15},{8,0},{9,1},... | collective-permute-start | bytes 393224 | tf_op jit(solution)/shard_map/ppermute | solution.py:475
  9.4 3.4 %collective-permute-start.2 = (bf16[256,256]{1,0:T(8,128)(2,1)S(1)}, bf16[256,256]{1,0:T(8,128)(2,1)S(1)}, u32[]{:S(2)}, u32[]{:S(2)}) collective-permute-start(bf16[256,256]{1,0:T(8,128)(2,1)S(1)} %get-tuple-element.42), channel_id=1, source_target_pairs={{0,1},{1,0},{2,3},{3,2},{4,5},{5,4},{6,7},{7,6},{8,9},{9,8},{10,11... | collective-permute-start | bytes 393224 | tf_op jit(solution)/shard_map/ppermute | solution.py:471
  9.4 3.4 %collective-permute-start.3 = (bf16[256,256]{1,0:T(8,128)(2,1)S(1)}, bf16[256,256]{1,0:T(8,128)(2,1)S(1)}, u32[]{:S(2)}, u32[]{:S(2)}) collective-permute-start(bf16[256,256]{1,0:T(8,128)(2,1)S(1)} %get-tuple-element.43), channel_id=1, source_target_pairs={{0,1},{1,0},{2,3},{3,2},{4,5},{5,4},{6,7},{7,6},{8,9},{9,8},{10,11... | collective-permute-start | bytes 393224 | tf_op jit(solution)/shard_map/ppermute | solution.py:471
  10.0 2.9 %collective-permute-start.4 = (bf16[256,256]{1,0:T(8,128)(2,1)S(1)}, bf16[256,256]{1,0:T(8,128)(2,1)S(1)}, u32[]{:S(2)}, u32[]{:S(2)}) collective-permute-start(bf16[256,256]{1,0:T(8,128)(2,1)S(1)} %get-tuple-element.44), channel_id=1, source_target_pairs={{0,1},{1,0},{2,3},{3,2},{4,5},{5,4},{6,7},{7,6},{8,9},{9,8},{10,11... | collective-permute-start | bytes 393224 | tf_op jit(solution)/shard_map/ppermute | solution.py:471
  10.0 2.9 %collective-permute-start.5 = (bf16[256,256]{1,0:T(8,128)(2,1)S(1)}, bf16[256,256]{1,0:T(8,128)(2,1)S(1)}, u32[]{:S(2)}, u32[]{:S(2)}) collective-permute-start(bf16[256,256]{1,0:T(8,128)(2,1)S(1)} %get-tuple-element.45), channel_id=1, source_target_pairs={{0,1},{1,0},{2,3},{3,2},{4,5},{5,4},{6,7},{7,6},{8,9},{9,8},{10,11... | collective-permute-start | bytes 393224 | tf_op jit(solution)/shard_map/ppermute | solution.py:471
  12.8 5.0 %collective-permute-start.6 = (bf16[1,512,128]{2,1,0:T(8,128)(2,1)S(1)}, bf16[1,512,128]{2,1,0:T(8,128)(2,1)S(1)}, u32[]{:S(2)}, u32[]{:S(2)}) collective-permute-start(bf16[1,512,128]{2,1,0:T(8,128)(2,1)S(1)} %collective-permute-done.1.refs_1_), channel_id=1, source_target_pairs={{0,4},{1,5},{2,6},{3,7},{4,0},{5,1},{6,2},{7,3},{8,12},{9,13},{10,... | collective-permute-start | bytes 393224 | tf_op jit(solution)/shard_map/ppermute | solution.py:475
  13.5 14.9 %collective-permute-start.9 = (bf16[2,2,256,256]{3,2,1,0:T(8,128)(2,1)S(1)}, bf16[2,2,256,256]{3,2,1,0:T(8,128)(2,1)S(1)}, u32[]{:S(2)}, u32[]{:S(2)}) collective-permute-start(bf16[2,2,256,256]{3,2,1,0:T(8,128)(2,1)S(1)} %get-tuple-element.54), channel_id=1, source_target_pairs={{0,2},{1,3},{2,0},{3,1},{4,6},{5,7},{6,4},{7,5},{8,10},{9,11},{10,... | collective-permute-start | bytes 1572872 | tf_op jit(solution)/shard_map/ppermute | solution.py:471
  15.0 16.7 %collective-permute-start.8 = (bf16[2,2,256,256]{3,2,1,0:T(8,128)(2,1)S(1)}, bf16[2,2,256,256]{3,2,1,0:T(8,128)(2,1)S(1)}, u32[]{:S(2)}, u32[]{:S(2)}) collective-permute-start(bf16[2,2,256,256]{3,2,1,0:T(8,128)(2,1)S(1)} %get-tuple-element.53.mine_ref), channel_id=1, source_target_pairs={{0,4},{1,5},{2,6},{3,7},{4,8},{5,9},{6,10},{7,11},{8,12},{9,13},{1... | collective-permute-start | bytes 1572872 | tf_op jit(solution)/shard_map/ppermute | solution.py:471
  17.9 8.9 %collective-permute-start.7 = (bf16[3,512,128]{2,1,0:T(8,128)(2,1)S(1)}, bf16[3,512,128]{2,1,0:T(8,128)(2,1)S(1)}, u32[]{:S(2)}, u32[]{:S(2)}) collective-permute-start(bf16[3,512,128]{2,1,0:T(8,128)(2,1)S(1)} %shard_map.93.near_ref), channel_id=1, source_target_pairs={{0,16},{16,0},{1,17},{17,1},{2,18},{18,2},{3,19},{19,3},{4,20},{20... | collective-permute-start | bytes 1179656 | tf_op jit(solution)/shard_map/ppermute | solution.py:228
  19.5 18.0 %collective-permute-start.11 = (bf16[2,256,256]{2,1,0:T(8,128)(2,1)S(1)}, bf16[2,256,256]{2,1,0:T(8,128)(2,1)S(1)}, u32[]{:S(2)}, u32[]{:S(2)}) collective-permute-start(bf16[2,256,256]{2,1,0:T(8,128)(2,1)S(1)} %get-tuple-element.58), channel_id=1, source_target_pairs={{0,6},{1,7},{2,4},{3,5},{4,10},{5,11},{6,8},{7,9},{8,14},{9,15},{1... | collective-permute-start | bytes 786440 | tf_op jit(solution)/shard_map/ppermute | solution.py:471
  22.3 20.2 %collective-permute-start.10 = (bf16[2,256,256]{2,1,0:T(8,128)(2,1)S(1)}, bf16[2,256,256]{2,1,0:T(8,128)(2,1)S(1)}, u32[]{:S(2)}, u32[]{:S(2)}) collective-permute-start(bf16[2,256,256]{2,1,0:T(8,128)(2,1)S(1)} %get-tuple-element.57), channel_id=1, source_target_pairs={{0,6},{1,7},{2,4},{3,5},{4,10},{5,11},{6,8},{7,9},{8,14},{9,15},{1... | collective-permute-start | bytes 786440 | tf_op jit(solution)/shard_map/ppermute | solution.py:471
  28.3 9.2 %copy-start.3 = (bf16[256,512]{1,0:T(8,128)(2,1)S(1)}, bf16[256,512]{1,0:T(8,128)(2,1)}, u32[]{:S(2)}) copy-start(bf16[256,512]{1,0:T(8,128)(2,1)} %constant.11.clone.back_low_ref) | copy-start | bytes 786436
  28.3 9.2 %copy-start.4 = (bf16[256,512]{1,0:T(8,128)(2,1)S(1)}, bf16[256,512]{1,0:T(8,128)(2,1)}, u32[]{:S(2)}) copy-start(bf16[256,512]{1,0:T(8,128)(2,1)} %constant.10.clone.back_high_ref) | copy-start | bytes 786436
  28.3 9.2 %copy-start.6 = (f32[2048]{0:T(1024)S(1)}, f32[2048]{0:T(1024)}, u32[]{:S(2)}) copy-start(f32[2048]{0:T(1024)} %param.13) | copy-start | bytes 24580
  40.1 6.2 %collective-permute-start.15 = (bf16[256,256]{1,0:T(8,128)(2,1)S(1)}, bf16[256,256]{1,0:T(8,128)(2,1)S(1)}, u32[]{:S(2)}, u32[]{:S(2)}) collective-permute-start(bf16[256,256]{1,0:T(8,128)(2,1)S(1)} %get-tuple-element.66), channel_id=1, source_target_pairs={{0,2},{1,3},{2,0},{3,1},{4,6},{5,7},{6,4},{7,5},{8,10},{9,11},{10,... | collective-permute-start | bytes 393224 | tf_op jit(solution)/shard_map/ppermute | solution.py:471
  41.4 5.9 %collective-permute-start.16 = (bf16[256,256]{1,0:T(8,128)(2,1)S(1)}, bf16[256,256]{1,0:T(8,128)(2,1)S(1)}, u32[]{:S(2)}, u32[]{:S(2)}) collective-permute-start(bf16[256,256]{1,0:T(8,128)(2,1)S(1)} %get-tuple-element.67), channel_id=1, source_target_pairs={{0,3},{1,2},{2,1},{3,0},{4,7},{5,6},{6,5},{7,4},{8,11},{9,10},{10,... | collective-permute-start | bytes 393224 | tf_op jit(solution)/shard_map/ppermute | solution.py:471
  41.4 5.9 %collective-permute-start.17 = (bf16[256,256]{1,0:T(8,128)(2,1)S(1)}, bf16[256,256]{1,0:T(8,128)(2,1)S(1)}, u32[]{:S(2)}, u32[]{:S(2)}) collective-permute-start(bf16[256,256]{1,0:T(8,128)(2,1)S(1)} %get-tuple-element.68), channel_id=1, source_target_pairs={{0,1},{1,0},{2,3},{3,2},{4,5},{5,4},{6,7},{7,6},{8,9},{9,8},{10,11... | collective-permute-start | bytes 393224 | tf_op jit(solution)/shard_map/ppermute | solution.py:471
  42.5 4.8 %copy-start.2 = (bf16[256,2048]{1,0:T(8,128)(2,1)S(1)}, bf16[256,2048]{1,0:T(8,128)(2,1)}, u32[]{:S(2)}) copy-start(bf16[256,2048]{1,0:T(8,128)(2,1)} %gate_ref.3) | copy-start | bytes 3145732
  45.1 6.5 %collective-permute-start.12 = (bf16[256,256]{1,0:T(8,128)(2,1)S(1)}, bf16[256,256]{1,0:T(8,128)(2,1)S(1)}, u32[]{:S(2)}, u32[]{:S(2)}) collective-permute-start(bf16[256,256]{1,0:T(8,128)(2,1)S(1)} %get-tuple-element.62), channel_id=1, source_target_pairs={{0,2},{1,3},{2,0},{3,1},{4,6},{5,7},{6,4},{7,5},{8,10},{9,11},{10,... | collective-permute-start | bytes 393224 | tf_op jit(solution)/shard_map/ppermute | solution.py:471
  46.2 6.7 %collective-permute-start.13 = (bf16[256,256]{1,0:T(8,128)(2,1)S(1)}, bf16[256,256]{1,0:T(8,128)(2,1)S(1)}, u32[]{:S(2)}, u32[]{:S(2)}) collective-permute-start(bf16[256,256]{1,0:T(8,128)(2,1)S(1)} %get-tuple-element.63), channel_id=1, source_target_pairs={{0,3},{1,2},{2,1},{3,0},{4,7},{5,6},{6,5},{7,4},{8,11},{9,10},{10,... | collective-permute-start | bytes 393224 | tf_op jit(solution)/shard_map/ppermute | solution.py:471
  46.3 6.6 %collective-permute-start.14 = (bf16[256,256]{1,0:T(8,128)(2,1)S(1)}, bf16[256,256]{1,0:T(8,128)(2,1)S(1)}, u32[]{:S(2)}, u32[]{:S(2)}) collective-permute-start(bf16[256,256]{1,0:T(8,128)(2,1)S(1)} %get-tuple-element.64), channel_id=1, source_target_pairs={{0,1},{1,0},{2,3},{3,2},{4,5},{5,4},{6,7},{7,6},{8,9},{9,8},{10,11... | collective-permute-start | bytes 393224 | tf_op jit(solution)/shard_map/ppermute | solution.py:471

commit v6 on v5

--- a/solution.py
+++ b/solution.py
@@ -282,7 +282,7 @@
         first_ref[part] = spectra[0]
         for apart in range(2):
             block = ahead_ref[part, apart]
-            halo_ref[part, member ^ apart] = matmul(high_ref[...], block) + matmul(low_ref[...], block)
+            halo_ref[part, (member ^ apart) % 2] = matmul(high_ref[...], block) + matmul(low_ref[...], block)
 
         def body(at, sign):
             read = reader(spectra, rows, at, 8)
@@ -309,7 +309,7 @@
         out_shape=[
             jax.ShapeDtypeStruct((CHUNKS, members - 1, 2 * rows, chunk), F32),
             jax.ShapeDtypeStruct((CHUNKS, 2 * rows, chunk), F32),
-            jax.ShapeDtypeStruct((CHUNKS, members, 2 * rows, chunk), F32),
+            jax.ShapeDtypeStruct((CHUNKS, members // 2, 2 * rows, chunk), F32),
         ],
         scratch_shapes=[pltpu.VMEM((members, 2 * rows, chunk), F32)],
         compiler_params=params(20),
@@ -331,11 +331,11 @@
     mine_ref,
     across_ref,
     beyond_ref,
+    ahead_ref,
     _,
     *refs,
 ):
-    out_refs, (halo_ref, sums) = refs[:members], refs[members:]
-    halo = halo_ref.at[part]
+    out_refs, (beyond, sums) = refs[:members], refs[members:]
 
     def skip_of(part):
         chunk = out_refs[0].shape[1]
@@ -352,13 +352,14 @@
     rows = high_ref.shape[1]
     for apart in range(2, members):
         block = beyond_ref[apart - 2]
-        halo[member ^ apart] = matmul(high_ref[...], block) + matmul(low_ref[...], block)
-
-    def body(at, sign):
-        read = reader(halo, rows, at, 8)
+        beyond[(member ^ apart) % 2] = matmul(high_ref[...], block) + matmul(low_ref[...], block)
+
+    def body(pair, at, sign):
+        halves = [reader(beyond, rows, at, 8)] * (members // 2)
+        halves[pair] = functools.partial(reader(ahead_ref, rows, at, 8), part)
         taps_read = reader(taps_ref, rows, at, 8)
         taps = [taps_read(part, lag) for lag in range(members)]
-        blocks = [read(position) for position in range(members)]
+        blocks = [halves[position // 2](position % 2) for position in range(members)]
         blocks.append(reader(first_ref, rows, at, 8)(part))
         windows = [window(a, b, sign) for a, b in zip(blocks, blocks[1:])]
         for output in range(members):
@@ -371,7 +372,10 @@
             sums[output, pl.ds(at, 8), :] = total[0]
             sums[output, pl.ds(at + rows, 8), :] = total[1]
 
-    for_bins(rows, 8, body)
+    for pair in range(members // 2):
+        pl.when(member // 2 == pair)(
+            functools.partial(for_bins, rows, 8, functools.partial(body, pair))
+        )
     blocks = [mine_ref[part, 0], mine_ref[part, 1], across_ref[part, 0], across_ref[part, 1]]
     skip = skip_of(part)
     for apart, block in enumerate(blocks):
@@ -385,22 +389,21 @@
         out_refs[apart][...] = mixed.astype(BF16)
 
 
-def mixed_pieces(part, tables, back_tables, skip, taps, partial, first, mine, across, beyond, halo):
+def mixed_pieces(part, tables, back_tables, skip, taps, partial, first, mine, across, beyond, ahead, after):
     members, chunk = taps.shape[1], taps.shape[-1]
     rows = tables[0].shape[1]
-    operands = [*tables, *back_tables, skip, taps, partial, first, mine, across]
-    *pieces, halo = pl.pallas_call(
+    return pl.pallas_call(
         functools.partial(mix_kernel, members, part),
-        in_specs=[VMEM] * (len(operands) + 2),
-        out_specs=[VMEM] * (members + 1),
-        out_shape=[jax.ShapeDtypeStruct((rows, chunk), BF16)] * members
-        + [jax.ShapeDtypeStruct(halo.shape, F32)],
-        input_output_aliases={len(operands) + 1: members},
-        scratch_shapes=[pltpu.VMEM((members, 2 * rows, chunk), F32)],
+        in_specs=[VMEM] * 12 + [pl.BlockSpec(memory_space=pl.ANY)],
+        out_specs=[VMEM] * members,
+        out_shape=[jax.ShapeDtypeStruct((rows, chunk), BF16)] * members,
+        scratch_shapes=[
+            pltpu.VMEM((members // 2, 2 * rows, chunk), F32),
+            pltpu.VMEM((members, 2 * rows, chunk), F32),
+        ],
         compiler_params=params(20),
         cost_estimate=SMALL,
-    )(*operands, beyond, halo)
-    return pieces, halo
+    )(*tables, *back_tables, skip, taps, partial, first, mine, across, beyond, ahead, after)
 
 
 def gate_kernel(layers, members, part, gate_ref, *refs):
@@ -497,11 +500,12 @@
     if width != LANES:
         skip = skip_gain.reshape(layers, members, width)
         skip = lax.dynamic_index_in_dim(skip, member, 1, False).reshape(CHUNKS, -1)
-    out = None
+    out, after = None, first
     for part in range(CHUNKS):
-        mixed, spectra = mixed_pieces(
-            part, tables, back_tables, skip, taps, partial, first, mine, across, beyond[part], spectra
+        mixed = mixed_pieces(
+            part, tables, back_tables, skip, taps, partial, first, mine, across, beyond[part], spectra, after
         )
+        after = mixed[0]
         mixed = [mixed[0]] + [to_member(mixed[d], d, 0) for d in range(1, members)]
         out = gated_output(part, gate_out, mixed, layers, members, out)
     return out

time: 54.1 us -> 54.1 us (level)
  no operation moved by 1% of the time
where the time goes in v6:
time: 54.1 us; the launch traced here: 53.8 us
  starting transfers between devices  20.2 us (37%)
  waiting for transfers between devices  18.8 us (35%)
  Pallas kernels  14.7 us (27%)
    ppermute x14, starting transfers between devices, to_member(): return lax.ppermute(value, 'ctx', pairs)  12.4 us
    ppermute x14, waiting for transfers between devices, to_member(): return lax.ppermute(value, 'ctx', pairs)  10.6 us
    ppermute x3, starting transfers between devices, to_layer(): return lax.ppermute(value, 'ctx', pairs)  6.2 us
    pallas_call x2, Pallas kernels, mixed_pieces(): pl.pallas_call(functools.partial(mix_kernel, members, part), in_specs=[VM...  5.1 us
    ppermute x3, waiting for transfers between devices, to_layer(): return lax.ppermute(value, 'ctx', pairs)  4.64 us
    ppermute x1, waiting for transfers between devices, tap_spectra(): far = lax.ppermute(near, 'groups', [(0, 1), (1, 0)])  3.52 us
    pallas_call x1, Pallas kernels, own_partials(): pl.pallas_call(functools.partial(own_kernel, members), in_specs=[VMEM] *...  3.5 us
    pallas_call x2, Pallas kernels, gated_output(): pl.pallas_call(functools.partial(gate_kernel, layers // CHUNKS, members,...  1.81 us
  transfers between devices with their start and end apart: 18, of which 9 were waited for; matrix products, arithmetic and copies ran while one was open for 0% of the time, Pallas kernels for 24%

profile of v6, /device:TPU:0, one launch (start us, length us, event | category | flops | bytes accessed | tf_op | source)
XLA Modules:
  0.0 53.8 jit_solution(3758412597645792280)
XLA Ops:
  0.0 1.0 %shard_map.91.half_ref = bf16[1,512,128]{2,1,0:T(8,128)(2,1)S(1)} custom-call(bf16[1024,128]{1,0:T(8,128)(2,1)} %own_ref.1), custom_call_target="tpu_custom_call" | custom-call | flops 1000 | bytes 1000 | tf_op jit(solution)/shard_map/pallas_call | solution.py:201
  1.0 3.1 %collective-permute-start = (bf16[1,512,128]{2,1,0:T(8,128)(2,1)S(1)}, bf16[1,512,128]{2,1,0:T(8,128)(2,1)S(1)}, u32[]{:S(2)}, u32[]{:S(2)}) collective-permute-start(bf16[1,512,128]{2,1,0:T(8,128)(2,1)S(1)} %shard_map.91.half_ref), channel_id=1, source_target_pairs={{0,4},{1,5},{2,6},{3,7},{4,0},{5,1},{6,2},{7,3},{8,12},{9,13},{10,... | collective-permute-start | bytes 393224 | tf_op jit(solution)/shard_map/ppermute | solution.py:478
  4.1 2.6 %collective-permute-start.1 = (bf16[1,512,128]{2,1,0:T(8,128)(2,1)S(1)}, bf16[1,512,128]{2,1,0:T(8,128)(2,1)S(1)}, u32[]{:S(2)}, u32[]{:S(2)}) collective-permute-start(bf16[1,512,128]{2,1,0:T(8,128)(2,1)S(1)} %shard_map.91.half_ref), channel_id=1, source_target_pairs={{0,8},{1,9},{2,10},{3,11},{4,12},{5,13},{6,14},{7,15},{8,0},{9,1},... | collective-permute-start | bytes 393224 | tf_op jit(solution)/shard_map/ppermute | solution.py:478
  6.7 1.7 %shard_map.92 = (bf16[2,256,256]{2,1,0:T(8,128)(2,1)S(1)}, bf16[2,256,256]{2,1,0:T(8,128)(2,1)S(1)}, bf16[256,256]{1,0:T(8,128)(2,1)S(1)}, bf16[256,256]{1,0:T(8...) custom-call(bf16[256,2048]{1,0:T(8,128)(2,1)} %gate_hbm.1, bf16[256,2048]{1,0:T(8,128)(2,1)} %values_hbm.1, ...), custom_call_target="tpu_custom_call" | custom-call | flops 1000 | bytes 1000 | tf_op jit(solution)/shard_map/pallas_call | solution.py:113
  8.4 1.0 %collective-permute-done.refs_0_ = bf16[1,512,128]{2,1,0:T(8,128)(2,1)S(1)} collective-permute-done((bf16[1,512,128]{2,1,0:T(8,128)(2,1)S(1)}, bf16[1,512,128]{2,1,0:T(8,128)(2,1)S(1)}, u32[]{:S(2)}, u32[]{:S(2)}) %collective-permute-start) | collective-permute-done | bytes 131104 | tf_op jit(solution)/shard_map/ppermute | solution.py:478
  9.4 0.5 collective-permute-start.3
  10.0 0.5 collective-permute-start.5
  10.5 2.4 %collective-permute-done.1.refs_1_ = bf16[1,512,128]{2,1,0:T(8,128)(2,1)S(1)} collective-permute-done((bf16[1,512,128]{2,1,0:T(8,128)(2,1)S(1)}, bf16[1,512,128]{2,1,0:T(8,128)(2,1)S(1)}, u32[]{:S(2)}, u32[]{:S(2)}) %collective-permute-start.1) | collective-permute-done | bytes 131104 | tf_op jit(solution)/shard_map/ppermute | solution.py:478
  12.8 0.5 collective-permute-start.6
  13.4 0.1 shard_map.95
  13.5 1.6 %collective-permute-start.9 = (bf16[2,2,256,256]{3,2,1,0:T(8,128)(2,1)S(1)}, bf16[2,2,256,256]{3,2,1,0:T(8,128)(2,1)S(1)}, u32[]{:S(2)}, u32[]{:S(2)}) collective-permute-start(bf16[2,2,256,256]{3,2,1,0:T(8,128)(2,1)S(1)} %get-tuple-element.53), channel_id=1, source_target_pairs={{0,2},{1,3},{2,0},{3,1},{4,6},{5,7},{6,4},{7,5},{8,10},{9,11},{10,... | collective-permute-start | bytes 1572872 | tf_op jit(solution)/shard_map/ppermute | solution.py:474
  15.0 1.6 %collective-permute-start.8 = (bf16[2,2,256,256]{3,2,1,0:T(8,128)(2,1)S(1)}, bf16[2,2,256,256]{3,2,1,0:T(8,128)(2,1)S(1)}, u32[]{:S(2)}, u32[]{:S(2)}) collective-permute-start(bf16[2,2,256,256]{3,2,1,0:T(8,128)(2,1)S(1)} %get-tuple-element.52.mine_ref), channel_id=1, source_target_pairs={{0,4},{1,5},{2,6},{3,7},{4,8},{5,9},{6,10},{7,11},{8,12},{9,13},{1... | collective-permute-start | bytes 1572872 | tf_op jit(solution)/shard_map/ppermute | solution.py:474
  16.6 1.3 %collective-permute-done.6.refs_2_ = bf16[1,512,128]{2,1,0:T(8,128)(2,1)S(1)} collective-permute-done((bf16[1,512,128]{2,1,0:T(8,128)(2,1)S(1)}, bf16[1,512,128]{2,1,0:T(8,128)(2,1)S(1)}, u32[]{:S(2)}, u32[]{:S(2)}) %collective-permute-start.6) | collective-permute-done | bytes 131104 | tf_op jit(solution)/shard_map/ppermute | solution.py:478
  17.9 1.6 %collective-permute-start.7 = (bf16[3,512,128]{2,1,0:T(8,128)(2,1)S(1)}, bf16[3,512,128]{2,1,0:T(8,128)(2,1)S(1)}, u32[]{:S(2)}, u32[]{:S(2)}) collective-permute-start(bf16[3,512,128]{2,1,0:T(8,128)(2,1)S(1)} %shard_map.93.near_ref), channel_id=1, source_target_pairs={{0,16},{16,0},{1,17},{17,1},{2,18},{18,2},{3,19},{19,3},{4,20},{20... | collective-permute-start | bytes 1179656 | tf_op jit(solution)/shard_map/ppermute | solution.py:228
  19.5 2.8 %collective-permute-start.11 = (bf16[2,256,256]{2,1,0:T(8,128)(2,1)S(1)}, bf16[2,256,256]{2,1,0:T(8,128)(2,1)S(1)}, u32[]{:S(2)}, u32[]{:S(2)}) collective-permute-start(bf16[2,256,256]{2,1,0:T(8,128)(2,1)S(1)} %get-tuple-element.58), channel_id=1, source_target_pairs={{0,6},{1,7},{2,4},{3,5},{4,10},{5,11},{6,8},{7,9},{8,14},{9,15},{1... | collective-permute-start | bytes 786440 | tf_op jit(solution)/shard_map/ppermute | solution.py:474
  22.3 1.0 %collective-permute-start.10 = (bf16[2,256,256]{2,1,0:T(8,128)(2,1)S(1)}, bf16[2,256,256]{2,1,0:T(8,128)(2,1)S(1)}, u32[]{:S(2)}, u32[]{:S(2)}) collective-permute-start(bf16[2,256,256]{2,1,0:T(8,128)(2,1)S(1)} %get-tuple-element.56), channel_id=1, source_target_pairs={{0,6},{1,7},{2,4},{3,5},{4,10},{5,11},{6,8},{7,9},{8,14},{9,15},{1... | collective-permute-start | bytes 786440 | tf_op jit(solution)/shard_map/ppermute | solution.py:474
  23.3 3.5 %collective-permute-done.7.far_ref = bf16[3,512,128]{2,1,0:T(8,128)(2,1)S(1)} collective-permute-done((bf16[3,512,128]{2,1,0:T(8,128)(2,1)S(1)}, bf16[3,512,128]{2,1,0:T(8,128)(2,1)S(1)}, u32[]{:S(2)}, u32[]{:S(2)}) %collective-permute-start.7) | collective-permute-done | bytes 393248 | tf_op jit(solution)/shard_map/ppermute | solution.py:228
  26.8 1.5 %shard_map.94.taps_ref = f32[2,4,512,256]{3,2,1,0:T(8,128)S(1)} custom-call(bf16[512,256]{1,0:T(8,128)(2,1)S(1)} %copy-done.1, bf16[512,256]{1,0:T(8,128)(2,1)S(1)} %copy-done, bf16[1024,128]{1,0:T(8,128)(2,1)S(1)} %copy-done.5, bf16[3,512,128]{2,1,0:T(8,128)(2,1)S(1)} %shard_map.93.near_ref, bf16[3,512,128]{2,1,0:T(8,128)(2,1)S(1)} %collective-permute-done.7.far_ref), custom_call_target="tpu_custom_call" | custom-call | flops 1000 | bytes 1000 | tf_op jit(solution)/shard_map/pallas_call | solution.py:229
  28.4 3.4 %collective-permute-done.8.ahead_ref = bf16[2,2,256,256]{3,2,1,0:T(8,128)(2,1)S(1)} collective-permute-done((bf16[2,2,256,256]{3,2,1,0:T(8,128)(2,1)S(1)}, bf16[2,2,256,256]{3,2,1,0:T(8,128)(2,1)S(1)}, u32[]{:S(2)}, u32[]{:S(2)}) %collective-permute-start.8) | collective-permute-done | bytes 524320 | tf_op jit(solution)/shard_map/ppermute | solution.py:474
  31.7 3.5 %shard_map.96 = (f32[2,3,512,256]{3,2,1,0:T(8,128)S(1)}, f32[2,512,256]{2,1,0:T(8,128)S(1)}, f32[2,2,512,256]{3,2,1,0:T(8,128)S(1)}) custom-call(bf16[512,256]{1,0:T(8,128)(2,1)S(1)} %copy-done.1, bf16[512,256]{1,0:T(8,128)(2,1)S(1)} %copy-done, f32[2,4,512,256]{3,2,1,0:T(8,128)S(1)} %shard_map.94.taps_ref, ...), custom_call_target="tpu_custom_call" | custom-call | flops 1000 | bytes 1000 | tf_op jit(solution)/shard_map/pallas_call | solution.py:305
  35.2 2.3 %collective-permute-done.11.beyond_ref = bf16[2,256,256]{2,1,0:T(8,128)(2,1)S(1)} collective-permute-done((bf16[2,256,256]{2,1,0:T(8,128)(2,1)S(1)}, bf16[2,256,256]{2,1,0:T(8,128)(2,1)S(1)}, u32[]{:S(2)}, u32[]{:S(2)}) %collective-permute-start.11) | collective-permute-done | bytes 262176 | tf_op jit(solution)/shard_map/ppermute | solution.py:474
  37.5 2.6 %shard_map.97 = (bf16[256,256]{1,0:T(8,128)(2,1)S(1)}, bf16[256,256]{1,0:T(8,128)(2,1)S(1)}, bf16[256,256]{1,0:T(8,128)(2,1)S(1)}, bf16[256,256]{1,0:T(8,128)(2,1)S(1)}) custom-call(bf16[512,256]{1,0:T(8,128)(2,1)S(1)} %copy-done.1, bf16[512,256]{1,0:T(8,128)(2,1)S(1)} %copy-done, bf16[256,512]{1,0:T(8,128)(2,1)S(1)} %copy-done.4, ...), custom_call_target="tpu_custom_call" | custom-call | flops 1000 | bytes 1000 | tf_op jit(solution)/shard_map/pallas_call | solution.py:395
  40.1 1.3 %collective-permute-start.15 = (bf16[256,256]{1,0:T(8,128)(2,1)S(1)}, bf16[256,256]{1,0:T(8,128)(2,1)S(1)}, u32[]{:S(2)}, u32[]{:S(2)}) collective-permute-start(bf16[256,256]{1,0:T(8,128)(2,1)S(1)} %get-tuple-element.64), channel_id=1, source_target_pairs={{0,2},{1,3},{2,0},{3,1},{4,6},{5,7},{6,4},{7,5},{8,10},{9,11},{10,... | collective-permute-start | bytes 393224 | tf_op jit(solution)/shard_map/ppermute | solution.py:474
  41.4 0.9 %collective-permute-start.17 = (bf16[256,256]{1,0:T(8,128)(2,1)S(1)}, bf16[256,256]{1,0:T(8,128)(2,1)S(1)}, u32[]{:S(2)}, u32[]{:S(2)}) collective-permute-start(bf16[256,256]{1,0:T(8,128)(2,1)S(1)} %get-tuple-element.66), channel_id=1, source_target_pairs={{0,1},{1,0},{2,3},{3,2},{4,5},{5,4},{6,7},{7,6},{8,9},{9,8},{10,11... | collective-permute-start | bytes 393224 | tf_op jit(solution)/shard_map/ppermute | solution.py:474
  42.3 0.2 collective-permute-done.10.beyond_ref
  42.5 2.5 %shard_map.98 = (bf16[256,256]{1,0:T(8,128)(2,1)S(1)}, bf16[256,256]{1,0:T(8,128)(2,1)S(1)}, bf16[256,256]{1,0:T(8,128)(2,1)S(1)}, bf16[256,256]{1,0:T(8,128)(2,1)S(1)}) custom-call(bf16[512,256]{1,0:T(8,128)(2,1)S(1)} %copy-done.1, bf16[512,256]{1,0:T(8,128)(2,1)S(1)} %copy-done, bf16[256,512]{1,0:T(8,128)(2,1)S(1)} %copy-done.4, ...), custom_call_target="tpu_custom_call" | custom-call | flops 1000 | bytes 1000 | tf_op jit(solution)/shard_map/pallas_call | solution.py:395
  45.1 1.1 %collective-permute-start.12 = (bf16[256,256]{1,0:T(8,128)(2,1)S(1)}, bf16[256,256]{1,0:T(8,128)(2,1)S(1)}, u32[]{:S(2)}, u32[]{:S(2)}) collective-permute-start(bf16[256,256]{1,0:T(8,128)(2,1)S(1)} %get-tuple-element.61), channel_id=1, source_target_pairs={{0,2},{1,3},{2,0},{3,1},{4,6},{5,7},{6,4},{7,5},{8,10},{9,11},{10,... | collective-permute-start | bytes 393224 | tf_op jit(solution)/shard_map/ppermute | solution.py:474
  46.3 1.0 %collective-permute-start.14 = (bf16[256,256]{1,0:T(8,128)(2,1)S(1)}, bf16[256,256]{1,0:T(8,128)(2,1)S(1)}, u32[]{:S(2)}, u32[]{:S(2)}) collective-permute-start(bf16[256,256]{1,0:T(8,128)(2,1)S(1)} %get-tuple-element.63), channel_id=1, source_target_pairs={{0,1},{1,0},{2,3},{3,2},{4,5},{5,4},{6,7},{7,6},{8,9},{9,8},{10,11... | collective-permute-start | bytes 393224 | tf_op jit(solution)/shard_map/ppermute | solution.py:474
  47.3 0.9 %shard_map.99.refs_4_ = bf16[256,2048]{1,0:T(8,128)(2,1)} custom-call(bf16[256,2048]{1,0:T(8,128)(2,1)S(1)} %copy-done.2, bf16[256,256]{1,0:T(8,128)(2,1)S(1)} %get-tuple-element.59._.refs_0_, bf16[256,256]{1,0:T(8,128)(2,1)S(1)} %collective-permute-done.15.refs_1_, bf16[256,256]{1,0:T(8,128)(2,1)S(1)} %collective-permute-done.16.refs_2_, ...), custom_call_target="tpu_custom_call" | custom-call | flops 1000 | bytes 1000 | tf_op jit(solution)/shard_map/pallas_call | solution.py:448
  48.2 3.3 %collective-permute-done.12.refs_1_ = bf16[256,256]{1,0:T(8,128)(2,1)S(1)} collective-permute-done((bf16[256,256]{1,0:T(8,128)(2,1)S(1)}, bf16[256,256]{1,0:T(8,128)(2,1)S(1)}, u32[]{:S(2)}, u32[]{:S(2)}) %collective-permute-start.12) | collective-permute-done | bytes 131104 | tf_op jit(solution)/shard_map/ppermute | solution.py:474
  51.5 1.4 %collective-permute-done.13.refs_2_ = bf16[256,256]{1,0:T(8,128)(2,1)S(1)} collective-permute-done((bf16[256,256]{1,0:T(8,128)(2,1)S(1)}, bf16[256,256]{1,0:T(8,128)(2,1)S(1)}, u32[]{:S(2)}, u32[]{:S(2)}) %collective-permute-start.13) | collective-permute-done | bytes 131104 | tf_op jit(solution)/shard_map/ppermute | solution.py:474
  52.9 0.9 %shard_map.100 = bf16[256,2048]{1,0:T(8,128)(2,1)} custom-call(bf16[256,2048]{1,0:T(8,128)(2,1)S(1)} %copy-done.2, bf16[256,256]{1,0:T(8,128)(2,1)S(1)} %get-tuple-element.60.refs_0_, bf16[256,256]{1,0:T(8,128)(2,1)S(1)} %collective-permute-done.12.refs_1_, bf16[256,256]{1,0:T(8,128)(2,1)S(1)} %collective-permute-done.13.refs_2_, ...), custom_call_target="tpu_custom_call", output_to_operand_aliasing={{}: (5, {})} | custom-call | flops 1000 | bytes 1000 | tf_op jit(solution)/shard_map/pallas_call | solution.py:448
  (28 shorter events, 0.2 us)
Async XLA Ops:
  0.0 26.8 %copy-start = (bf16[512,256]{1,0:T(8,128)(2,1)S(1)}, bf16[512,256]{1,0:T(8,128)(2,1)}, u32[]{:S(2)}) copy-start(bf16[512,256]{1,0:T(8,128)(2,1)} %constant.9.clone.low_ref) | copy-start | bytes 786436
  0.0 26.8 %copy-start.1 = (bf16[512,256]{1,0:T(8,128)(2,1)S(1)}, bf16[512,256]{1,0:T(8,128)(2,1)}, u32[]{:S(2)}) copy-start(bf16[512,256]{1,0:T(8,128)(2,1)} %constant.8.clone.high_ref) | copy-start | bytes 786436
  0.0 26.8 %copy-start.5 = (bf16[1024,128]{1,0:T(8,128)(2,1)S(1)}, bf16[1024,128]{1,0:T(8,128)(2,1)}, u32[]{:S(2)}) copy-start(bf16[1024,128]{1,0:T(8,128)(2,1)} %own_ref.1) | copy-start | bytes 786436
  1.0 8.4 %collective-permute-start = (bf16[1,512,128]{2,1,0:T(8,128)(2,1)S(1)}, bf16[1,512,128]{2,1,0:T(8,128)(2,1)S(1)}, u32[]{:S(2)}, u32[]{:S(2)}) collective-permute-start(bf16[1,512,128]{2,1,0:T(8,128)(2,1)S(1)} %shard_map.91.half_ref), channel_id=1, source_target_pairs={{0,4},{1,5},{2,6},{3,7},{4,0},{5,1},{6,2},{7,3},{8,12},{9,13},{10,... | collective-permute-start | bytes 393224 | tf_op jit(solution)/shard_map/ppermute | solution.py:478
  4.1 8.7 %collective-permute-start.1 = (bf16[1,512,128]{2,1,0:T(8,128)(2,1)S(1)}, bf16[1,512,128]{2,1,0:T(8,128)(2,1)S(1)}, u32[]{:S(2)}, u32[]{:S(2)}) collective-permute-start(bf16[1,512,128]{2,1,0:T(8,128)(2,1)S(1)} %shard_map.91.half_ref), channel_id=1, source_target_pairs={{0,8},{1,9},{2,10},{3,11},{4,12},{5,13},{6,14},{7,15},{8,0},{9,1},... | collective-permute-start | bytes 393224 | tf_op jit(solution)/shard_map/ppermute | solution.py:478
  9.4 3.4 %collective-permute-start.2 = (bf16[256,256]{1,0:T(8,128)(2,1)S(1)}, bf16[256,256]{1,0:T(8,128)(2,1)S(1)}, u32[]{:S(2)}, u32[]{:S(2)}) collective-permute-start(bf16[256,256]{1,0:T(8,128)(2,1)S(1)} %get-tuple-element.41), channel_id=1, source_target_pairs={{0,1},{1,0},{2,3},{3,2},{4,5},{5,4},{6,7},{7,6},{8,9},{9,8},{10,11... | collective-permute-start | bytes 393224 | tf_op jit(solution)/shard_map/ppermute | solution.py:474
  9.4 3.4 %collective-permute-start.3 = (bf16[256,256]{1,0:T(8,128)(2,1)S(1)}, bf16[256,256]{1,0:T(8,128)(2,1)S(1)}, u32[]{:S(2)}, u32[]{:S(2)}) collective-permute-start(bf16[256,256]{1,0:T(8,128)(2,1)S(1)} %get-tuple-element.42), channel_id=1, source_target_pairs={{0,1},{1,0},{2,3},{3,2},{4,5},{5,4},{6,7},{7,6},{8,9},{9,8},{10,11... | collective-permute-start | bytes 393224 | tf_op jit(solution)/shard_map/ppermute | solution.py:474
  10.0 2.9 %collective-permute-start.4 = (bf16[256,256]{1,0:T(8,128)(2,1)S(1)}, bf16[256,256]{1,0:T(8,128)(2,1)S(1)}, u32[]{:S(2)}, u32[]{:S(2)}) collective-permute-start(bf16[256,256]{1,0:T(8,128)(2,1)S(1)} %get-tuple-element.43), channel_id=1, source_target_pairs={{0,1},{1,0},{2,3},{3,2},{4,5},{5,4},{6,7},{7,6},{8,9},{9,8},{10,11... | collective-permute-start | bytes 393224 | tf_op jit(solution)/shard_map/ppermute | solution.py:474
  10.0 2.9 %collective-permute-start.5 = (bf16[256,256]{1,0:T(8,128)(2,1)S(1)}, bf16[256,256]{1,0:T(8,128)(2,1)S(1)}, u32[]{:S(2)}, u32[]{:S(2)}) collective-permute-start(bf16[256,256]{1,0:T(8,128)(2,1)S(1)} %get-tuple-element.44), channel_id=1, source_target_pairs={{0,1},{1,0},{2,3},{3,2},{4,5},{5,4},{6,7},{7,6},{8,9},{9,8},{10,11... | collective-permute-start | bytes 393224 | tf_op jit(solution)/shard_map/ppermute | solution.py:474
  12.8 5.0 %collective-permute-start.6 = (bf16[1,512,128]{2,1,0:T(8,128)(2,1)S(1)}, bf16[1,512,128]{2,1,0:T(8,128)(2,1)S(1)}, u32[]{:S(2)}, u32[]{:S(2)}) collective-permute-start(bf16[1,512,128]{2,1,0:T(8,128)(2,1)S(1)} %collective-permute-done.1.refs_1_), channel_id=1, source_target_pairs={{0,4},{1,5},{2,6},{3,7},{4,0},{5,1},{6,2},{7,3},{8,12},{9,13},{10,... | collective-permute-start | bytes 393224 | tf_op jit(solution)/shard_map/ppermute | solution.py:478
  13.5 14.9 %collective-permute-start.9 = (bf16[2,2,256,256]{3,2,1,0:T(8,128)(2,1)S(1)}, bf16[2,2,256,256]{3,2,1,0:T(8,128)(2,1)S(1)}, u32[]{:S(2)}, u32[]{:S(2)}) collective-permute-start(bf16[2,2,256,256]{3,2,1,0:T(8,128)(2,1)S(1)} %get-tuple-element.53), channel_id=1, source_target_pairs={{0,2},{1,3},{2,0},{3,1},{4,6},{5,7},{6,4},{7,5},{8,10},{9,11},{10,... | collective-permute-start | bytes 1572872 | tf_op jit(solution)/shard_map/ppermute | solution.py:474
  15.0 16.7 %collective-permute-start.8 = (bf16[2,2,256,256]{3,2,1,0:T(8,128)(2,1)S(1)}, bf16[2,2,256,256]{3,2,1,0:T(8,128)(2,1)S(1)}, u32[]{:S(2)}, u32[]{:S(2)}) collective-permute-start(bf16[2,2,256,256]{3,2,1,0:T(8,128)(2,1)S(1)} %get-tuple-element.52.mine_ref), channel_id=1, source_target_pairs={{0,4},{1,5},{2,6},{3,7},{4,8},{5,9},{6,10},{7,11},{8,12},{9,13},{1... | collective-permute-start | bytes 1572872 | tf_op jit(solution)/shard_map/ppermute | solution.py:474
  17.9 8.9 %collective-permute-start.7 = (bf16[3,512,128]{2,1,0:T(8,128)(2,1)S(1)}, bf16[3,512,128]{2,1,0:T(8,128)(2,1)S(1)}, u32[]{:S(2)}, u32[]{:S(2)}) collective-permute-start(bf16[3,512,128]{2,1,0:T(8,128)(2,1)S(1)} %shard_map.93.near_ref), channel_id=1, source_target_pairs={{0,16},{16,0},{1,17},{17,1},{2,18},{18,2},{3,19},{19,3},{4,20},{20... | collective-permute-start | bytes 1179656 | tf_op jit(solution)/shard_map/ppermute | solution.py:228
  19.5 18.0 %collective-permute-start.11 = (bf16[2,256,256]{2,1,0:T(8,128)(2,1)S(1)}, bf16[2,256,256]{2,1,0:T(8,128)(2,1)S(1)}, u32[]{:S(2)}, u32[]{:S(2)}) collective-permute-start(bf16[2,256,256]{2,1,0:T(8,128)(2,1)S(1)} %get-tuple-element.58), channel_id=1, source_target_pairs={{0,6},{1,7},{2,4},{3,5},{4,10},{5,11},{6,8},{7,9},{8,14},{9,15},{1... | collective-permute-start | bytes 786440 | tf_op jit(solution)/shard_map/ppermute | solution.py:474
  22.3 20.2 %collective-permute-start.10 = (bf16[2,256,256]{2,1,0:T(8,128)(2,1)S(1)}, bf16[2,256,256]{2,1,0:T(8,128)(2,1)S(1)}, u32[]{:S(2)}, u32[]{:S(2)}) collective-permute-start(bf16[2,256,256]{2,1,0:T(8,128)(2,1)S(1)} %get-tuple-element.56), channel_id=1, source_target_pairs={{0,6},{1,7},{2,4},{3,5},{4,10},{5,11},{6,8},{7,9},{8,14},{9,15},{1... | collective-permute-start | bytes 786440 | tf_op jit(solution)/shard_map/ppermute | solution.py:474
  28.3 9.2 %copy-start.3 = (bf16[256,512]{1,0:T(8,128)(2,1)S(1)}, bf16[256,512]{1,0:T(8,128)(2,1)}, u32[]{:S(2)}) copy-start(bf16[256,512]{1,0:T(8,128)(2,1)} %constant.11.clone.back_low_ref) | copy-start | bytes 786436
  28.3 9.2 %copy-start.4 = (bf16[256,512]{1,0:T(8,128)(2,1)S(1)}, bf16[256,512]{1,0:T(8,128)(2,1)}, u32[]{:S(2)}) copy-start(bf16[256,512]{1,0:T(8,128)(2,1)} %constant.10.clone.back_high_ref) | copy-start | bytes 786436
  28.3 9.2 %copy-start.6 = (f32[2048]{0:T(1024)S(1)}, f32[2048]{0:T(1024)}, u32[]{:S(2)}) copy-start(f32[2048]{0:T(1024)} %param.13) | copy-start | bytes 24580
  40.1 6.2 %collective-permute-start.15 = (bf16[256,256]{1,0:T(8,128)(2,1)S(1)}, bf16[256,256]{1,0:T(8,128)(2,1)S(1)}, u32[]{:S(2)}, u32[]{:S(2)}) collective-permute-start(bf16[256,256]{1,0:T(8,128)(2,1)S(1)} %get-tuple-element.64), channel_id=1, source_target_pairs={{0,2},{1,3},{2,0},{3,1},{4,6},{5,7},{6,4},{7,5},{8,10},{9,11},{10,... | collective-permute-start | bytes 393224 | tf_op jit(solution)/shard_map/ppermute | solution.py:474
  41.4 5.9 %collective-permute-start.16 = (bf16[256,256]{1,0:T(8,128)(2,1)S(1)}, bf16[256,256]{1,0:T(8,128)(2,1)S(1)}, u32[]{:S(2)}, u32[]{:S(2)}) collective-permute-start(bf16[256,256]{1,0:T(8,128)(2,1)S(1)} %get-tuple-element.65), channel_id=1, source_target_pairs={{0,3},{1,2},{2,1},{3,0},{4,7},{5,6},{6,5},{7,4},{8,11},{9,10},{10,... | collective-permute-start | bytes 393224 | tf_op jit(solution)/shard_map/ppermute | solution.py:474
  41.4 5.9 %collective-permute-start.17 = (bf16[256,256]{1,0:T(8,128)(2,1)S(1)}, bf16[256,256]{1,0:T(8,128)(2,1)S(1)}, u32[]{:S(2)}, u32[]{:S(2)}) collective-permute-start(bf16[256,256]{1,0:T(8,128)(2,1)S(1)} %get-tuple-element.66), channel_id=1, source_target_pairs={{0,1},{1,0},{2,3},{3,2},{4,5},{5,4},{6,7},{7,6},{8,9},{9,8},{10,11... | collective-permute-start | bytes 393224 | tf_op jit(solution)/shard_map/ppermute | solution.py:474
  42.5 4.8 %copy-start.2 = (bf16[256,2048]{1,0:T(8,128)(2,1)S(1)}, bf16[256,2048]{1,0:T(8,128)(2,1)}, u32[]{:S(2)}) copy-start(bf16[256,2048]{1,0:T(8,128)(2,1)} %gate_ref.3) | copy-start | bytes 3145732
  45.1 6.5 %collective-permute-start.12 = (bf16[256,256]{1,0:T(8,128)(2,1)S(1)}, bf16[256,256]{1,0:T(8,128)(2,1)S(1)}, u32[]{:S(2)}, u32[]{:S(2)}) collective-permute-start(bf16[256,256]{1,0:T(8,128)(2,1)S(1)} %get-tuple-element.61), channel_id=1, source_target_pairs={{0,2},{1,3},{2,0},{3,1},{4,6},{5,7},{6,4},{7,5},{8,10},{9,11},{10,... | collective-permute-start | bytes 393224 | tf_op jit(solution)/shard_map/ppermute | solution.py:474
  46.2 6.7 %collective-permute-start.13 = (bf16[256,256]{1,0:T(8,128)(2,1)S(1)}, bf16[256,256]{1,0:T(8,128)(2,1)S(1)}, u32[]{:S(2)}, u32[]{:S(2)}) collective-permute-start(bf16[256,256]{1,0:T(8,128)(2,1)S(1)} %get-tuple-element.62), channel_id=1, source_target_pairs={{0,3},{1,2},{2,1},{3,0},{4,7},{5,6},{6,5},{7,4},{8,11},{9,10},{10,... | collective-permute-start | bytes 393224 | tf_op jit(solution)/shard_map/ppermute | solution.py:474
  46.3 6.7 %collective-permute-start.14 = (bf16[256,256]{1,0:T(8,128)(2,1)S(1)}, bf16[256,256]{1,0:T(8,128)(2,1)S(1)}, u32[]{:S(2)}, u32[]{:S(2)}) collective-permute-start(bf16[256,256]{1,0:T(8,128)(2,1)S(1)} %get-tuple-element.63), channel_id=1, source_target_pairs={{0,1},{1,0},{2,3},{3,2},{4,5},{5,4},{6,7},{7,6},{8,9},{9,8},{10,11... | collective-permute-start | bytes 393224 | tf_op jit(solution)/shard_map/ppermute | solution.py:474

commit v7 on v6

--- a/solution.py
+++ b/solution.py
@@ -355,26 +355,26 @@
         beyond[(member ^ apart) % 2] = matmul(high_ref[...], block) + matmul(low_ref[...], block)
 
     def body(pair, at, sign):
-        halves = [reader(beyond, rows, at, 8)] * (members // 2)
-        halves[pair] = functools.partial(reader(ahead_ref, rows, at, 8), part)
-        taps_read = reader(taps_ref, rows, at, 8)
+        halves = [reader(beyond, rows, at, 16)] * (members // 2)
+        halves[pair] = functools.partial(reader(ahead_ref, rows, at, 16), part)
+        taps_read = reader(taps_ref, rows, at, 16)
         taps = [taps_read(part, lag) for lag in range(members)]
         blocks = [halves[position // 2](position % 2) for position in range(members)]
-        blocks.append(reader(first_ref, rows, at, 8)(part))
+        blocks.append(reader(first_ref, rows, at, 16)(part))
         windows = [window(a, b, sign) for a, b in zip(blocks, blocks[1:])]
         for output in range(members):
             total = sum_products(
                 [(taps[lag], windows[members - 1 + output - lag]) for lag in range(output, members)]
             )
             if output:
-                before = reader(part_ref, rows, at, 8)(part, output - 1)
+                before = reader(part_ref, rows, at, 16)(part, output - 1)
                 total = total[0] + before[0], total[1] + before[1]
-            sums[output, pl.ds(at, 8), :] = total[0]
-            sums[output, pl.ds(at + rows, 8), :] = total[1]
+            sums[output, pl.ds(at, 16), :] = total[0]
+            sums[output, pl.ds(at + rows, 16), :] = total[1]
 
     for pair in range(members // 2):
         pl.when(member // 2 == pair)(
-            functools.partial(for_bins, rows, 8, functools.partial(body, pair))
+            functools.partial(for_bins, rows, 16, functools.partial(body, pair))
         )
     blocks = [mine_ref[part, 0], mine_ref[part, 1], across_ref[part, 0], across_ref[part, 1]]
     skip = skip_of(part)

time: 54.1 us -> 54.1 us (level)
  transfers between devices with their start and end apart: 18 -> 18, of which waited for: 9 -> 10; matrix products, arithmetic and copies ran while one was open for 0% -> 0% of each run, Pallas kernels for 24% -> 23%
where the time goes in v7:
time: 54.1 us; the launch traced here: 53.9 us
  starting transfers between devices  20.1 us (37%)
  waiting for transfers between devices  19.2 us (35%)
  Pallas kernels  14.4 us (27%)
    ppermute x14, starting transfers between devices, to_member(): return lax.ppermute(value, 'ctx', pairs)  12.3 us
    ppermute x14, waiting for transfers between devices, to_member(): return lax.ppermute(value, 'ctx', pairs)  11 us
    ppermute x3, starting transfers between devices, to_layer(): return lax.ppermute(value, 'ctx', pairs)  6.2 us
    pallas_call x2, Pallas kernels, mixed_pieces(): pl.pallas_call(functools.partial(mix_kernel, members, part), in_specs=[VM...  4.85 us
    ppermute x3, waiting for transfers between devices, to_layer(): return lax.ppermute(value, 'ctx', pairs)  4.64 us
    ppermute x1, waiting for transfers between devices, tap_spectra(): far = lax.ppermute(near, 'groups', [(0, 1), (1, 0)])  3.52 us
    pallas_call x1, Pallas kernels, own_partials(): pl.pallas_call(functools.partial(own_kernel, members), in_specs=[VMEM] *...  3.5 us
    pallas_call x2, Pallas kernels, gated_output(): pl.pallas_call(functools.partial(gate_kernel, layers // CHUNKS, members,...  1.81 us
  transfers between devices with their start and end apart: 18, of which 10 were waited for; matrix products, arithmetic and copies ran while one was open for 0% of the time, Pallas kernels for 23%

profile of v7, /device:TPU:0, one launch (start us, length us, event | category | flops | bytes accessed | tf_op | source)
XLA Modules:
  0.0 53.9 jit_solution(13987300021256591829)
XLA Ops:
  0.0 1.0 %shard_map.91.half_ref = bf16[1,512,128]{2,1,0:T(8,128)(2,1)S(1)} custom-call(bf16[1024,128]{1,0:T(8,128)(2,1)} %own_ref.1), custom_call_target="tpu_custom_call" | custom-call | flops 1000 | bytes 1000 | tf_op jit(solution)/shard_map/pallas_call | solution.py:201
  1.0 3.1 %collective-permute-start = (bf16[1,512,128]{2,1,0:T(8,128)(2,1)S(1)}, bf16[1,512,128]{2,1,0:T(8,128)(2,1)S(1)}, u32[]{:S(2)}, u32[]{:S(2)}) collective-permute-start(bf16[1,512,128]{2,1,0:T(8,128)(2,1)S(1)} %shard_map.91.half_ref), channel_id=1, source_target_pairs={{0,4},{1,5},{2,6},{3,7},{4,0},{5,1},{6,2},{7,3},{8,12},{9,13},{10,... | collective-permute-start | bytes 393224 | tf_op jit(solution)/shard_map/ppermute | solution.py:478
  4.1 2.6 %collective-permute-start.1 = (bf16[1,512,128]{2,1,0:T(8,128)(2,1)S(1)}, bf16[1,512,128]{2,1,0:T(8,128)(2,1)S(1)}, u32[]{:S(2)}, u32[]{:S(2)}) collective-permute-start(bf16[1,512,128]{2,1,0:T(8,128)(2,1)S(1)} %shard_map.91.half_ref), channel_id=1, source_target_pairs={{0,8},{1,9},{2,10},{3,11},{4,12},{5,13},{6,14},{7,15},{8,0},{9,1},... | collective-permute-start | bytes 393224 | tf_op jit(solution)/shard_map/ppermute | solution.py:478
  6.7 1.7 %shard_map.92 = (bf16[2,256,256]{2,1,0:T(8,128)(2,1)S(1)}, bf16[2,256,256]{2,1,0:T(8,128)(2,1)S(1)}, bf16[256,256]{1,0:T(8,128)(2,1)S(1)}, bf16[256,256]{1,0:T(8...) custom-call(bf16[256,2048]{1,0:T(8,128)(2,1)} %gate_hbm.1, bf16[256,2048]{1,0:T(8,128)(2,1)} %values_hbm.1, ...), custom_call_target="tpu_custom_call" | custom-call | flops 1000 | bytes 1000 | tf_op jit(solution)/shard_map/pallas_call | solution.py:113
  8.4 1.0 %collective-permute-done.refs_0_ = bf16[1,512,128]{2,1,0:T(8,128)(2,1)S(1)} collective-permute-done((bf16[1,512,128]{2,1,0:T(8,128)(2,1)S(1)}, bf16[1,512,128]{2,1,0:T(8,128)(2,1)S(1)}, u32[]{:S(2)}, u32[]{:S(2)}) %collective-permute-start) | collective-permute-done | bytes 131104 | tf_op jit(solution)/shard_map/ppermute | solution.py:478
  9.4 0.5 collective-permute-start.3
  10.0 0.5 collective-permute-start.5
  10.5 2.4 %collective-permute-done.1.refs_1_ = bf16[1,512,128]{2,1,0:T(8,128)(2,1)S(1)} collective-permute-done((bf16[1,512,128]{2,1,0:T(8,128)(2,1)S(1)}, bf16[1,512,128]{2,1,0:T(8,128)(2,1)S(1)}, u32[]{:S(2)}, u32[]{:S(2)}) %collective-permute-start.1) | collective-permute-done | bytes 131104 | tf_op jit(solution)/shard_map/ppermute | solution.py:478
  12.8 0.5 collective-permute-start.6
  13.5 1.6 %collective-permute-start.9 = (bf16[2,2,256,256]{3,2,1,0:T(8,128)(2,1)S(1)}, bf16[2,2,256,256]{3,2,1,0:T(8,128)(2,1)S(1)}, u32[]{:S(2)}, u32[]{:S(2)}) collective-permute-start(bf16[2,2,256,256]{3,2,1,0:T(8,128)(2,1)S(1)} %get-tuple-element.53), channel_id=1, source_target_pairs={{0,2},{1,3},{2,0},{3,1},{4,6},{5,7},{6,4},{7,5},{8,10},{9,11},{10,... | collective-permute-start | bytes 1572872 | tf_op jit(solution)/shard_map/ppermute | solution.py:474
  15.0 1.6 %collective-permute-start.8 = (bf16[2,2,256,256]{3,2,1,0:T(8,128)(2,1)S(1)}, bf16[2,2,256,256]{3,2,1,0:T(8,128)(2,1)S(1)}, u32[]{:S(2)}, u32[]{:S(2)}) collective-permute-start(bf16[2,2,256,256]{3,2,1,0:T(8,128)(2,1)S(1)} %get-tuple-element.52.mine_ref), channel_id=1, source_target_pairs={{0,4},{1,5},{2,6},{3,7},{4,8},{5,9},{6,10},{7,11},{8,12},{9,13},{1... | collective-permute-start | bytes 1572872 | tf_op jit(solution)/shard_map/ppermute | solution.py:474
  16.6 1.3 %collective-permute-done.6.refs_2_ = bf16[1,512,128]{2,1,0:T(8,128)(2,1)S(1)} collective-permute-done((bf16[1,512,128]{2,1,0:T(8,128)(2,1)S(1)}, bf16[1,512,128]{2,1,0:T(8,128)(2,1)S(1)}, u32[]{:S(2)}, u32[]{:S(2)}) %collective-permute-start.6) | collective-permute-done | bytes 131104 | tf_op jit(solution)/shard_map/ppermute | solution.py:478
  17.9 1.6 %collective-permute-start.7 = (bf16[3,512,128]{2,1,0:T(8,128)(2,1)S(1)}, bf16[3,512,128]{2,1,0:T(8,128)(2,1)S(1)}, u32[]{:S(2)}, u32[]{:S(2)}) collective-permute-start(bf16[3,512,128]{2,1,0:T(8,128)(2,1)S(1)} %shard_map.93.near_ref), channel_id=1, source_target_pairs={{0,16},{16,0},{1,17},{17,1},{2,18},{18,2},{3,19},{19,3},{4,20},{20... | collective-permute-start | bytes 1179656 | tf_op jit(solution)/shard_map/ppermute | solution.py:228
  19.5 2.8 %collective-permute-start.11 = (bf16[2,256,256]{2,1,0:T(8,128)(2,1)S(1)}, bf16[2,256,256]{2,1,0:T(8,128)(2,1)S(1)}, u32[]{:S(2)}, u32[]{:S(2)}) collective-permute-start(bf16[2,256,256]{2,1,0:T(8,128)(2,1)S(1)} %get-tuple-element.58), channel_id=1, source_target_pairs={{0,6},{1,7},{2,4},{3,5},{4,10},{5,11},{6,8},{7,9},{8,14},{9,15},{1... | collective-permute-start | bytes 786440 | tf_op jit(solution)/shard_map/ppermute | solution.py:474
  22.3 1.0 %collective-permute-start.10 = (bf16[2,256,256]{2,1,0:T(8,128)(2,1)S(1)}, bf16[2,256,256]{2,1,0:T(8,128)(2,1)S(1)}, u32[]{:S(2)}, u32[]{:S(2)}) collective-permute-start(bf16[2,256,256]{2,1,0:T(8,128)(2,1)S(1)} %get-tuple-element.56), channel_id=1, source_target_pairs={{0,6},{1,7},{2,4},{3,5},{4,10},{5,11},{6,8},{7,9},{8,14},{9,15},{1... | collective-permute-start | bytes 786440 | tf_op jit(solution)/shard_map/ppermute | solution.py:474
  23.3 3.5 %collective-permute-done.7.far_ref = bf16[3,512,128]{2,1,0:T(8,128)(2,1)S(1)} collective-permute-done((bf16[3,512,128]{2,1,0:T(8,128)(2,1)S(1)}, bf16[3,512,128]{2,1,0:T(8,128)(2,1)S(1)}, u32[]{:S(2)}, u32[]{:S(2)}) %collective-permute-start.7) | collective-permute-done | bytes 393248 | tf_op jit(solution)/shard_map/ppermute | solution.py:228
  26.8 1.5 %shard_map.94.taps_ref = f32[2,4,512,256]{3,2,1,0:T(8,128)S(1)} custom-call(bf16[512,256]{1,0:T(8,128)(2,1)S(1)} %copy-done.1, bf16[512,256]{1,0:T(8,128)(2,1)S(1)} %copy-done, bf16[1024,128]{1,0:T(8,128)(2,1)S(1)} %copy-done.5, bf16[3,512,128]{2,1,0:T(8,128)(2,1)S(1)} %shard_map.93.near_ref, bf16[3,512,128]{2,1,0:T(8,128)(2,1)S(1)} %collective-permute-done.7.far_ref), custom_call_target="tpu_custom_call" | custom-call | flops 1000 | bytes 1000 | tf_op jit(solution)/shard_map/pallas_call | solution.py:229
  28.4 3.4 %collective-permute-done.8.ahead_ref = bf16[2,2,256,256]{3,2,1,0:T(8,128)(2,1)S(1)} collective-permute-done((bf16[2,2,256,256]{3,2,1,0:T(8,128)(2,1)S(1)}, bf16[2,2,256,256]{3,2,1,0:T(8,128)(2,1)S(1)}, u32[]{:S(2)}, u32[]{:S(2)}) %collective-permute-start.8) | collective-permute-done | bytes 524320 | tf_op jit(solution)/shard_map/ppermute | solution.py:474
  31.7 3.5 %shard_map.96 = (f32[2,3,512,256]{3,2,1,0:T(8,128)S(1)}, f32[2,512,256]{2,1,0:T(8,128)S(1)}, f32[2,2,512,256]{3,2,1,0:T(8,128)S(1)}) custom-call(bf16[512,256]{1,0:T(8,128)(2,1)S(1)} %copy-done.1, bf16[512,256]{1,0:T(8,128)(2,1)S(1)} %copy-done, f32[2,4,512,256]{3,2,1,0:T(8,128)S(1)} %shard_map.94.taps_ref, ...), custom_call_target="tpu_custom_call" | custom-call | flops 1000 | bytes 1000 | tf_op jit(solution)/shard_map/pallas_call | solution.py:305
  35.2 2.3 %collective-permute-done.11.beyond_ref = bf16[2,256,256]{2,1,0:T(8,128)(2,1)S(1)} collective-permute-done((bf16[2,256,256]{2,1,0:T(8,128)(2,1)S(1)}, bf16[2,256,256]{2,1,0:T(8,128)(2,1)S(1)}, u32[]{:S(2)}, u32[]{:S(2)}) %collective-permute-start.11) | collective-permute-done | bytes 262176 | tf_op jit(solution)/shard_map/ppermute | solution.py:474
  37.5 2.4 %shard_map.97 = (bf16[256,256]{1,0:T(8,128)(2,1)S(1)}, bf16[256,256]{1,0:T(8,128)(2,1)S(1)}, bf16[256,256]{1,0:T(8,128)(2,1)S(1)}, bf16[256,256]{1,0:T(8,128)(2,1)S(1)}) custom-call(bf16[512,256]{1,0:T(8,128)(2,1)S(1)} %copy-done.1, bf16[512,256]{1,0:T(8,128)(2,1)S(1)} %copy-done, bf16[256,512]{1,0:T(8,128)(2,1)S(1)} %copy-done.4, ...), custom_call_target="tpu_custom_call" | custom-call | flops 1000 | bytes 1000 | tf_op jit(solution)/shard_map/pallas_call | solution.py:395
  39.9 1.3 %collective-permute-start.15 = (bf16[256,256]{1,0:T(8,128)(2,1)S(1)}, bf16[256,256]{1,0:T(8,128)(2,1)S(1)}, u32[]{:S(2)}, u32[]{:S(2)}) collective-permute-start(bf16[256,256]{1,0:T(8,128)(2,1)S(1)} %get-tuple-element.64), channel_id=1, source_target_pairs={{0,2},{1,3},{2,0},{3,1},{4,6},{5,7},{6,4},{7,5},{8,10},{9,11},{10,... | collective-permute-start | bytes 393224 | tf_op jit(solution)/shard_map/ppermute | solution.py:474
  41.3 0.9 %collective-permute-start.17 = (bf16[256,256]{1,0:T(8,128)(2,1)S(1)}, bf16[256,256]{1,0:T(8,128)(2,1)S(1)}, u32[]{:S(2)}, u32[]{:S(2)}) collective-permute-start(bf16[256,256]{1,0:T(8,128)(2,1)S(1)} %get-tuple-element.66), channel_id=1, source_target_pairs={{0,1},{1,0},{2,3},{3,2},{4,5},{5,4},{6,7},{7,6},{8,9},{9,8},{10,11... | collective-permute-start | bytes 393224 | tf_op jit(solution)/shard_map/ppermute | solution.py:474
  42.2 0.3 collective-permute-done.10.beyond_ref
  42.5 2.4 %shard_map.98 = (bf16[256,256]{1,0:T(8,128)(2,1)S(1)}, bf16[256,256]{1,0:T(8,128)(2,1)S(1)}, bf16[256,256]{1,0:T(8,128)(2,1)S(1)}, bf16[256,256]{1,0:T(8,128)(2,1)S(1)}) custom-call(bf16[512,256]{1,0:T(8,128)(2,1)S(1)} %copy-done.1, bf16[512,256]{1,0:T(8,128)(2,1)S(1)} %copy-done, bf16[256,512]{1,0:T(8,128)(2,1)S(1)} %copy-done.4, ...), custom_call_target="tpu_custom_call" | custom-call | flops 1000 | bytes 1000 | tf_op jit(solution)/shard_map/pallas_call | solution.py:395
  44.9 1.0 %collective-permute-start.12 = (bf16[256,256]{1,0:T(8,128)(2,1)S(1)}, bf16[256,256]{1,0:T(8,128)(2,1)S(1)}, u32[]{:S(2)}, u32[]{:S(2)}) collective-permute-start(bf16[256,256]{1,0:T(8,128)(2,1)S(1)} %get-tuple-element.61), channel_id=1, source_target_pairs={{0,2},{1,3},{2,0},{3,1},{4,6},{5,7},{6,4},{7,5},{8,10},{9,11},{10,... | collective-permute-start | bytes 393224 | tf_op jit(solution)/shard_map/ppermute | solution.py:474
  46.0 0.1 collective-permute-done.15.refs_1_
  46.2 1.0 %collective-permute-start.14 = (bf16[256,256]{1,0:T(8,128)(2,1)S(1)}, bf16[256,256]{1,0:T(8,128)(2,1)S(1)}, u32[]{:S(2)}, u32[]{:S(2)}) collective-permute-start(bf16[256,256]{1,0:T(8,128)(2,1)S(1)} %get-tuple-element.63), channel_id=1, source_target_pairs={{0,1},{1,0},{2,3},{3,2},{4,5},{5,4},{6,7},{7,6},{8,9},{9,8},{10,11... | collective-permute-start | bytes 393224 | tf_op jit(solution)/shard_map/ppermute | solution.py:474
  47.2 0.9 %shard_map.99.refs_4_ = bf16[256,2048]{1,0:T(8,128)(2,1)} custom-call(bf16[256,2048]{1,0:T(8,128)(2,1)S(1)} %copy-done.2, bf16[256,256]{1,0:T(8,128)(2,1)S(1)} %get-tuple-element.59._.refs_0_, bf16[256,256]{1,0:T(8,128)(2,1)S(1)} %collective-permute-done.15.refs_1_, bf16[256,256]{1,0:T(8,128)(2,1)S(1)} %collective-permute-done.16.refs_2_, ...), custom_call_target="tpu_custom_call" | custom-call | flops 1000 | bytes 1000 | tf_op jit(solution)/shard_map/pallas_call | solution.py:448
  48.1 3.4 %collective-permute-done.12.refs_1_ = bf16[256,256]{1,0:T(8,128)(2,1)S(1)} collective-permute-done((bf16[256,256]{1,0:T(8,128)(2,1)S(1)}, bf16[256,256]{1,0:T(8,128)(2,1)S(1)}, u32[]{:S(2)}, u32[]{:S(2)}) %collective-permute-start.12) | collective-permute-done | bytes 131104 | tf_op jit(solution)/shard_map/ppermute | solution.py:474
  51.5 1.5 %collective-permute-done.13.refs_2_ = bf16[256,256]{1,0:T(8,128)(2,1)S(1)} collective-permute-done((bf16[256,256]{1,0:T(8,128)(2,1)S(1)}, bf16[256,256]{1,0:T(8,128)(2,1)S(1)}, u32[]{:S(2)}, u32[]{:S(2)}) %collective-permute-start.13) | collective-permute-done | bytes 131104 | tf_op jit(solution)/shard_map/ppermute | solution.py:474
  52.9 0.9 %shard_map.100 = bf16[256,2048]{1,0:T(8,128)(2,1)} custom-call(bf16[256,2048]{1,0:T(8,128)(2,1)S(1)} %copy-done.2, bf16[256,256]{1,0:T(8,128)(2,1)S(1)} %get-tuple-element.60.refs_0_, bf16[256,256]{1,0:T(8,128)(2,1)S(1)} %collective-permute-done.12.refs_1_, bf16[256,256]{1,0:T(8,128)(2,1)S(1)} %collective-permute-done.13.refs_2_, ...), custom_call_target="tpu_custom_call", output_to_operand_aliasing={{}: (5, {})} | custom-call | flops 1000 | bytes 1000 | tf_op jit(solution)/shard_map/pallas_call | solution.py:448
  (28 shorter events, 0.3 us)
Async XLA Ops:
  0.0 26.8 %copy-start = (bf16[512,256]{1,0:T(8,128)(2,1)S(1)}, bf16[512,256]{1,0:T(8,128)(2,1)}, u32[]{:S(2)}) copy-start(bf16[512,256]{1,0:T(8,128)(2,1)} %constant.9.clone.low_ref) | copy-start | bytes 786436
  0.0 26.8 %copy-start.1 = (bf16[512,256]{1,0:T(8,128)(2,1)S(1)}, bf16[512,256]{1,0:T(8,128)(2,1)}, u32[]{:S(2)}) copy-start(bf16[512,256]{1,0:T(8,128)(2,1)} %constant.8.clone.high_ref) | copy-start | bytes 786436
  0.0 26.8 %copy-start.5 = (bf16[1024,128]{1,0:T(8,128)(2,1)S(1)}, bf16[1024,128]{1,0:T(8,128)(2,1)}, u32[]{:S(2)}) copy-start(bf16[1024,128]{1,0:T(8,128)(2,1)} %own_ref.1) | copy-start | bytes 786436
  1.0 8.4 %collective-permute-start = (bf16[1,512,128]{2,1,0:T(8,128)(2,1)S(1)}, bf16[1,512,128]{2,1,0:T(8,128)(2,1)S(1)}, u32[]{:S(2)}, u32[]{:S(2)}) collective-permute-start(bf16[1,512,128]{2,1,0:T(8,128)(2,1)S(1)} %shard_map.91.half_ref), channel_id=1, source_target_pairs={{0,4},{1,5},{2,6},{3,7},{4,0},{5,1},{6,2},{7,3},{8,12},{9,13},{10,... | collective-permute-start | bytes 393224 | tf_op jit(solution)/shard_map/ppermute | solution.py:478
  4.1 8.7 %collective-permute-start.1 = (bf16[1,512,128]{2,1,0:T(8,128)(2,1)S(1)}, bf16[1,512,128]{2,1,0:T(8,128)(2,1)S(1)}, u32[]{:S(2)}, u32[]{:S(2)}) collective-permute-start(bf16[1,512,128]{2,1,0:T(8,128)(2,1)S(1)} %shard_map.91.half_ref), channel_id=1, source_target_pairs={{0,8},{1,9},{2,10},{3,11},{4,12},{5,13},{6,14},{7,15},{8,0},{9,1},... | collective-permute-start | bytes 393224 | tf_op jit(solution)/shard_map/ppermute | solution.py:478
  9.4 3.4 %collective-permute-start.2 = (bf16[256,256]{1,0:T(8,128)(2,1)S(1)}, bf16[256,256]{1,0:T(8,128)(2,1)S(1)}, u32[]{:S(2)}, u32[]{:S(2)}) collective-permute-start(bf16[256,256]{1,0:T(8,128)(2,1)S(1)} %get-tuple-element.41), channel_id=1, source_target_pairs={{0,1},{1,0},{2,3},{3,2},{4,5},{5,4},{6,7},{7,6},{8,9},{9,8},{10,11... | collective-permute-start | bytes 393224 | tf_op jit(solution)/shard_map/ppermute | solution.py:474
  9.4 3.4 %collective-permute-start.3 = (bf16[256,256]{1,0:T(8,128)(2,1)S(1)}, bf16[256,256]{1,0:T(8,128)(2,1)S(1)}, u32[]{:S(2)}, u32[]{:S(2)}) collective-permute-start(bf16[256,256]{1,0:T(8,128)(2,1)S(1)} %get-tuple-element.42), channel_id=1, source_target_pairs={{0,1},{1,0},{2,3},{3,2},{4,5},{5,4},{6,7},{7,6},{8,9},{9,8},{10,11... | collective-permute-start | bytes 393224 | tf_op jit(solution)/shard_map/ppermute | solution.py:474
  10.0 2.9 %collective-permute-start.4 = (bf16[256,256]{1,0:T(8,128)(2,1)S(1)}, bf16[256,256]{1,0:T(8,128)(2,1)S(1)}, u32[]{:S(2)}, u32[]{:S(2)}) collective-permute-start(bf16[256,256]{1,0:T(8,128)(2,1)S(1)} %get-tuple-element.43), channel_id=1, source_target_pairs={{0,1},{1,0},{2,3},{3,2},{4,5},{5,4},{6,7},{7,6},{8,9},{9,8},{10,11... | collective-permute-start | bytes 393224 | tf_op jit(solution)/shard_map/ppermute | solution.py:474
  10.0 2.9 %collective-permute-start.5 = (bf16[256,256]{1,0:T(8,128)(2,1)S(1)}, bf16[256,256]{1,0:T(8,128)(2,1)S(1)}, u32[]{:S(2)}, u32[]{:S(2)}) collective-permute-start(bf16[256,256]{1,0:T(8,128)(2,1)S(1)} %get-tuple-element.44), channel_id=1, source_target_pairs={{0,1},{1,0},{2,3},{3,2},{4,5},{5,4},{6,7},{7,6},{8,9},{9,8},{10,11... | collective-permute-start | bytes 393224 | tf_op jit(solution)/shard_map/ppermute | solution.py:474
  12.8 5.0 %collective-permute-start.6 = (bf16[1,512,128]{2,1,0:T(8,128)(2,1)S(1)}, bf16[1,512,128]{2,1,0:T(8,128)(2,1)S(1)}, u32[]{:S(2)}, u32[]{:S(2)}) collective-permute-start(bf16[1,512,128]{2,1,0:T(8,128)(2,1)S(1)} %collective-permute-done.1.refs_1_), channel_id=1, source_target_pairs={{0,4},{1,5},{2,6},{3,7},{4,0},{5,1},{6,2},{7,3},{8,12},{9,13},{10,... | collective-permute-start | bytes 393224 | tf_op jit(solution)/shard_map/ppermute | solution.py:478
  13.5 14.9 %collective-permute-start.9 = (bf16[2,2,256,256]{3,2,1,0:T(8,128)(2,1)S(1)}, bf16[2,2,256,256]{3,2,1,0:T(8,128)(2,1)S(1)}, u32[]{:S(2)}, u32[]{:S(2)}) collective-permute-start(bf16[2,2,256,256]{3,2,1,0:T(8,128)(2,1)S(1)} %get-tuple-element.53), channel_id=1, source_target_pairs={{0,2},{1,3},{2,0},{3,1},{4,6},{5,7},{6,4},{7,5},{8,10},{9,11},{10,... | collective-permute-start | bytes 1572872 | tf_op jit(solution)/shard_map/ppermute | solution.py:474
  15.0 16.7 %collective-permute-start.8 = (bf16[2,2,256,256]{3,2,1,0:T(8,128)(2,1)S(1)}, bf16[2,2,256,256]{3,2,1,0:T(8,128)(2,1)S(1)}, u32[]{:S(2)}, u32[]{:S(2)}) collective-permute-start(bf16[2,2,256,256]{3,2,1,0:T(8,128)(2,1)S(1)} %get-tuple-element.52.mine_ref), channel_id=1, source_target_pairs={{0,4},{1,5},{2,6},{3,7},{4,8},{5,9},{6,10},{7,11},{8,12},{9,13},{1... | collective-permute-start | bytes 1572872 | tf_op jit(solution)/shard_map/ppermute | solution.py:474
  17.9 8.9 %collective-permute-start.7 = (bf16[3,512,128]{2,1,0:T(8,128)(2,1)S(1)}, bf16[3,512,128]{2,1,0:T(8,128)(2,1)S(1)}, u32[]{:S(2)}, u32[]{:S(2)}) collective-permute-start(bf16[3,512,128]{2,1,0:T(8,128)(2,1)S(1)} %shard_map.93.near_ref), channel_id=1, source_target_pairs={{0,16},{16,0},{1,17},{17,1},{2,18},{18,2},{3,19},{19,3},{4,20},{20... | collective-permute-start | bytes 1179656 | tf_op jit(solution)/shard_map/ppermute | solution.py:228
  19.5 18.0 %collective-permute-start.11 = (bf16[2,256,256]{2,1,0:T(8,128)(2,1)S(1)}, bf16[2,256,256]{2,1,0:T(8,128)(2,1)S(1)}, u32[]{:S(2)}, u32[]{:S(2)}) collective-permute-start(bf16[2,256,256]{2,1,0:T(8,128)(2,1)S(1)} %get-tuple-element.58), channel_id=1, source_target_pairs={{0,6},{1,7},{2,4},{3,5},{4,10},{5,11},{6,8},{7,9},{8,14},{9,15},{1... | collective-permute-start | bytes 786440 | tf_op jit(solution)/shard_map/ppermute | solution.py:474
  22.3 20.2 %collective-permute-start.10 = (bf16[2,256,256]{2,1,0:T(8,128)(2,1)S(1)}, bf16[2,256,256]{2,1,0:T(8,128)(2,1)S(1)}, u32[]{:S(2)}, u32[]{:S(2)}) collective-permute-start(bf16[2,256,256]{2,1,0:T(8,128)(2,1)S(1)} %get-tuple-element.56), channel_id=1, source_target_pairs={{0,6},{1,7},{2,4},{3,5},{4,10},{5,11},{6,8},{7,9},{8,14},{9,15},{1... | collective-permute-start | bytes 786440 | tf_op jit(solution)/shard_map/ppermute | solution.py:474
  28.3 9.2 %copy-start.3 = (bf16[256,512]{1,0:T(8,128)(2,1)S(1)}, bf16[256,512]{1,0:T(8,128)(2,1)}, u32[]{:S(2)}) copy-start(bf16[256,512]{1,0:T(8,128)(2,1)} %constant.11.clone.back_low_ref) | copy-start | bytes 786436
  28.3 9.2 %copy-start.4 = (bf16[256,512]{1,0:T(8,128)(2,1)S(1)}, bf16[256,512]{1,0:T(8,128)(2,1)}, u32[]{:S(2)}) copy-start(bf16[256,512]{1,0:T(8,128)(2,1)} %constant.10.clone.back_high_ref) | copy-start | bytes 786436
  28.3 9.2 %copy-start.6 = (f32[2048]{0:T(1024)S(1)}, f32[2048]{0:T(1024)}, u32[]{:S(2)}) copy-start(f32[2048]{0:T(1024)} %param.13) | copy-start | bytes 24580
  39.9 6.2 %collective-permute-start.15 = (bf16[256,256]{1,0:T(8,128)(2,1)S(1)}, bf16[256,256]{1,0:T(8,128)(2,1)S(1)}, u32[]{:S(2)}, u32[]{:S(2)}) collective-permute-start(bf16[256,256]{1,0:T(8,128)(2,1)S(1)} %get-tuple-element.64), channel_id=1, source_target_pairs={{0,2},{1,3},{2,0},{3,1},{4,6},{5,7},{6,4},{7,5},{8,10},{9,11},{10,... | collective-permute-start | bytes 393224 | tf_op jit(solution)/shard_map/ppermute | solution.py:474
  41.3 5.9 %collective-permute-start.16 = (bf16[256,256]{1,0:T(8,128)(2,1)S(1)}, bf16[256,256]{1,0:T(8,128)(2,1)S(1)}, u32[]{:S(2)}, u32[]{:S(2)}) collective-permute-start(bf16[256,256]{1,0:T(8,128)(2,1)S(1)} %get-tuple-element.65), channel_id=1, source_target_pairs={{0,3},{1,2},{2,1},{3,0},{4,7},{5,6},{6,5},{7,4},{8,11},{9,10},{10,... | collective-permute-start | bytes 393224 | tf_op jit(solution)/shard_map/ppermute | solution.py:474
  41.3 5.9 %collective-permute-start.17 = (bf16[256,256]{1,0:T(8,128)(2,1)S(1)}, bf16[256,256]{1,0:T(8,128)(2,1)S(1)}, u32[]{:S(2)}, u32[]{:S(2)}) collective-permute-start(bf16[256,256]{1,0:T(8,128)(2,1)S(1)} %get-tuple-element.66), channel_id=1, source_target_pairs={{0,1},{1,0},{2,3},{3,2},{4,5},{5,4},{6,7},{7,6},{8,9},{9,8},{10,11... | collective-permute-start | bytes 393224 | tf_op jit(solution)/shard_map/ppermute | solution.py:474
  42.5 4.7 %copy-start.2 = (bf16[256,2048]{1,0:T(8,128)(2,1)S(1)}, bf16[256,2048]{1,0:T(8,128)(2,1)}, u32[]{:S(2)}) copy-start(bf16[256,2048]{1,0:T(8,128)(2,1)} %gate_ref.3) | copy-start | bytes 3145732
  44.9 6.6 %collective-permute-start.12 = (bf16[256,256]{1,0:T(8,128)(2,1)S(1)}, bf16[256,256]{1,0:T(8,128)(2,1)S(1)}, u32[]{:S(2)}, u32[]{:S(2)}) collective-permute-start(bf16[256,256]{1,0:T(8,128)(2,1)S(1)} %get-tuple-element.61), channel_id=1, source_target_pairs={{0,2},{1,3},{2,0},{3,1},{4,6},{5,7},{6,4},{7,5},{8,10},{9,11},{10,... | collective-permute-start | bytes 393224 | tf_op jit(solution)/shard_map/ppermute | solution.py:474
  45.9 7.0 %collective-permute-start.13 = (bf16[256,256]{1,0:T(8,128)(2,1)S(1)}, bf16[256,256]{1,0:T(8,128)(2,1)S(1)}, u32[]{:S(2)}, u32[]{:S(2)}) collective-permute-start(bf16[256,256]{1,0:T(8,128)(2,1)S(1)} %get-tuple-element.62), channel_id=1, source_target_pairs={{0,3},{1,2},{2,1},{3,0},{4,7},{5,6},{6,5},{7,4},{8,11},{9,10},{10,... | collective-permute-start | bytes 393224 | tf_op jit(solution)/shard_map/ppermute | solution.py:474
  46.2 6.8 %collective-permute-start.14 = (bf16[256,256]{1,0:T(8,128)(2,1)S(1)}, bf16[256,256]{1,0:T(8,128)(2,1)S(1)}, u32[]{:S(2)}, u32[]{:S(2)}) collective-permute-start(bf16[256,256]{1,0:T(8,128)(2,1)S(1)} %get-tuple-element.63), channel_id=1, source_target_pairs={{0,1},{1,0},{2,3},{3,2},{4,5},{5,4},{6,7},{7,6},{8,9},{9,8},{10,11... | collective-permute-start | bytes 393224 | tf_op jit(solution)/shard_map/ppermute | solution.py:474

commit v8 on v6

--- a/solution.py
+++ b/solution.py
@@ -380,11 +380,8 @@
     skip = skip_of(part)
     for apart, block in enumerate(blocks):
         total = sums[member ^ apart]
-        high = total.astype(BF16)
-        low = (total - high.astype(F32)).astype(BF16)
-        convolved = matmul(back_high_ref[...], high) + (
-            matmul(back_high_ref[...], low) + matmul(back_low_ref[...], high)
-        )
+        total = total.astype(BF16)
+        convolved = matmul(back_high_ref[...], total) + matmul(back_low_ref[...], total)
         mixed = convolved + skip * block.astype(F32)
         out_refs[apart][...] = mixed.astype(BF16)
 

time: 54.1 us -> 54.1 us (level)
  waiting for transfers between devices: 18.8 us -> 19.6 us
  Pallas kernels: 14.7 us -> 14.1 us
  starting transfers between devices: 20.2 us -> 19.6 us
    ppermute x14, waiting for transfers between devices: 10.6 us -> 11.5 us  [to_member(): return lax.ppermute(value, 'ctx', pairs)]
    ppermute x14, starting transfers between devices: 12.4 us -> 11.9 us  [to_member(): return lax.ppermute(value, 'ctx', pairs)]
    pallas_call x2, Pallas kernels: 5.1 us -> 4.52 us  [mixed_pieces(): pl.pallas_call(functools.partial(mix_kernel, members, part), in_specs=[VM...]
  transfers between devices with their start and end apart: 18 -> 18, of which waited for: 9 -> 11; matrix products, arithmetic and copies ran while one was open for 0% -> 0% of each run, Pallas kernels for 24% -> 23%
where the time goes in v8:
time: 54.1 us; the launch traced here: 53.5 us
  starting transfers between devices  19.6 us (36%)
  waiting for transfers between devices  19.6 us (36%)
  Pallas kernels  14.1 us (26%)
    ppermute x14, starting transfers between devices, to_member(): return lax.ppermute(value, 'ctx', pairs)  11.9 us
    ppermute x14, waiting for transfers between devices, to_member(): return lax.ppermute(value, 'ctx', pairs)  11.5 us
    ppermute x3, starting transfers between devices, to_layer(): return lax.ppermute(value, 'ctx', pairs)  6.2 us
    ppermute x3, waiting for transfers between devices, to_layer(): return lax.ppermute(value, 'ctx', pairs)  4.64 us
    pallas_call x2, Pallas kernels, mixed_pieces(): pl.pallas_call(functools.partial(mix_kernel, members, part), in_specs=[VM...  4.52 us
    ppermute x1, waiting for transfers between devices, tap_spectra(): far = lax.ppermute(near, 'groups', [(0, 1), (1, 0)])  3.52 us
    pallas_call x1, Pallas kernels, own_partials(): pl.pallas_call(functools.partial(own_kernel, members), in_specs=[VMEM] *...  3.5 us
    pallas_call x2, Pallas kernels, gated_output(): pl.pallas_call(functools.partial(gate_kernel, layers // CHUNKS, members,...  1.81 us
  transfers between devices with their start and end apart: 18, of which 11 were waited for; matrix products, arithmetic and copies ran while one was open for 0% of the time, Pallas kernels for 23%

profile of v8, /device:TPU:0, one launch (start us, length us, event | category | flops | bytes accessed | tf_op | source)
XLA Modules:
  0.0 53.5 jit_solution(4439805981982127807)
XLA Ops:
  0.0 1.0 %shard_map.91.half_ref = bf16[1,512,128]{2,1,0:T(8,128)(2,1)S(1)} custom-call(bf16[1024,128]{1,0:T(8,128)(2,1)} %own_ref.1), custom_call_target="tpu_custom_call" | custom-call | flops 1000 | bytes 1000 | tf_op jit(solution)/shard_map/pallas_call | solution.py:201
  1.0 3.1 %collective-permute-start = (bf16[1,512,128]{2,1,0:T(8,128)(2,1)S(1)}, bf16[1,512,128]{2,1,0:T(8,128)(2,1)S(1)}, u32[]{:S(2)}, u32[]{:S(2)}) collective-permute-start(bf16[1,512,128]{2,1,0:T(8,128)(2,1)S(1)} %shard_map.91.half_ref), channel_id=1, source_target_pairs={{0,4},{1,5},{2,6},{3,7},{4,0},{5,1},{6,2},{7,3},{8,12},{9,13},{10,... | collective-permute-start | bytes 393224 | tf_op jit(solution)/shard_map/ppermute | solution.py:475
  4.1 2.6 %collective-permute-start.1 = (bf16[1,512,128]{2,1,0:T(8,128)(2,1)S(1)}, bf16[1,512,128]{2,1,0:T(8,128)(2,1)S(1)}, u32[]{:S(2)}, u32[]{:S(2)}) collective-permute-start(bf16[1,512,128]{2,1,0:T(8,128)(2,1)S(1)} %shard_map.91.half_ref), channel_id=1, source_target_pairs={{0,8},{1,9},{2,10},{3,11},{4,12},{5,13},{6,14},{7,15},{8,0},{9,1},... | collective-permute-start | bytes 393224 | tf_op jit(solution)/shard_map/ppermute | solution.py:475
  6.7 1.7 %shard_map.92 = (bf16[2,256,256]{2,1,0:T(8,128)(2,1)S(1)}, bf16[2,256,256]{2,1,0:T(8,128)(2,1)S(1)}, bf16[256,256]{1,0:T(8,128)(2,1)S(1)}, bf16[256,256]{1,0:T(8...) custom-call(bf16[256,2048]{1,0:T(8,128)(2,1)} %gate_hbm.1, bf16[256,2048]{1,0:T(8,128)(2,1)} %values_hbm.1, ...), custom_call_target="tpu_custom_call" | custom-call | flops 1000 | bytes 1000 | tf_op jit(solution)/shard_map/pallas_call | solution.py:113
  8.4 1.0 %collective-permute-done.refs_0_ = bf16[1,512,128]{2,1,0:T(8,128)(2,1)S(1)} collective-permute-done((bf16[1,512,128]{2,1,0:T(8,128)(2,1)S(1)}, bf16[1,512,128]{2,1,0:T(8,128)(2,1)S(1)}, u32[]{:S(2)}, u32[]{:S(2)}) %collective-permute-start) | collective-permute-done | bytes 131104 | tf_op jit(solution)/shard_map/ppermute | solution.py:475
  9.4 0.5 collective-permute-start.3
  10.0 0.5 collective-permute-start.5
  10.5 2.4 %collective-permute-done.1.refs_1_ = bf16[1,512,128]{2,1,0:T(8,128)(2,1)S(1)} collective-permute-done((bf16[1,512,128]{2,1,0:T(8,128)(2,1)S(1)}, bf16[1,512,128]{2,1,0:T(8,128)(2,1)S(1)}, u32[]{:S(2)}, u32[]{:S(2)}) %collective-permute-start.1) | collective-permute-done | bytes 131104 | tf_op jit(solution)/shard_map/ppermute | solution.py:475
  12.8 0.5 collective-permute-start.6
  13.5 1.6 %collective-permute-start.9 = (bf16[2,2,256,256]{3,2,1,0:T(8,128)(2,1)S(1)}, bf16[2,2,256,256]{3,2,1,0:T(8,128)(2,1)S(1)}, u32[]{:S(2)}, u32[]{:S(2)}) collective-permute-start(bf16[2,2,256,256]{3,2,1,0:T(8,128)(2,1)S(1)} %get-tuple-element.53), channel_id=1, source_target_pairs={{0,2},{1,3},{2,0},{3,1},{4,6},{5,7},{6,4},{7,5},{8,10},{9,11},{10,... | collective-permute-start | bytes 1572872 | tf_op jit(solution)/shard_map/ppermute | solution.py:471
  15.0 1.6 %collective-permute-start.8 = (bf16[2,2,256,256]{3,2,1,0:T(8,128)(2,1)S(1)}, bf16[2,2,256,256]{3,2,1,0:T(8,128)(2,1)S(1)}, u32[]{:S(2)}, u32[]{:S(2)}) collective-permute-start(bf16[2,2,256,256]{3,2,1,0:T(8,128)(2,1)S(1)} %get-tuple-element.52.mine_ref), channel_id=1, source_target_pairs={{0,4},{1,5},{2,6},{3,7},{4,8},{5,9},{6,10},{7,11},{8,12},{9,13},{1... | collective-permute-start | bytes 1572872 | tf_op jit(solution)/shard_map/ppermute | solution.py:471
  16.6 1.3 %collective-permute-done.6.refs_2_ = bf16[1,512,128]{2,1,0:T(8,128)(2,1)S(1)} collective-permute-done((bf16[1,512,128]{2,1,0:T(8,128)(2,1)S(1)}, bf16[1,512,128]{2,1,0:T(8,128)(2,1)S(1)}, u32[]{:S(2)}, u32[]{:S(2)}) %collective-permute-start.6) | collective-permute-done | bytes 131104 | tf_op jit(solution)/shard_map/ppermute | solution.py:475
  17.9 1.6 %collective-permute-start.7 = (bf16[3,512,128]{2,1,0:T(8,128)(2,1)S(1)}, bf16[3,512,128]{2,1,0:T(8,128)(2,1)S(1)}, u32[]{:S(2)}, u32[]{:S(2)}) collective-permute-start(bf16[3,512,128]{2,1,0:T(8,128)(2,1)S(1)} %shard_map.93.near_ref), channel_id=1, source_target_pairs={{0,16},{16,0},{1,17},{17,1},{2,18},{18,2},{3,19},{19,3},{4,20},{20... | collective-permute-start | bytes 1179656 | tf_op jit(solution)/shard_map/ppermute | solution.py:228
  19.5 2.8 %collective-permute-start.11 = (bf16[2,256,256]{2,1,0:T(8,128)(2,1)S(1)}, bf16[2,256,256]{2,1,0:T(8,128)(2,1)S(1)}, u32[]{:S(2)}, u32[]{:S(2)}) collective-permute-start(bf16[2,256,256]{2,1,0:T(8,128)(2,1)S(1)} %get-tuple-element.58), channel_id=1, source_target_pairs={{0,6},{1,7},{2,4},{3,5},{4,10},{5,11},{6,8},{7,9},{8,14},{9,15},{1... | collective-permute-start | bytes 786440 | tf_op jit(solution)/shard_map/ppermute | solution.py:471
  22.3 1.0 %collective-permute-start.10 = (bf16[2,256,256]{2,1,0:T(8,128)(2,1)S(1)}, bf16[2,256,256]{2,1,0:T(8,128)(2,1)S(1)}, u32[]{:S(2)}, u32[]{:S(2)}) collective-permute-start(bf16[2,256,256]{2,1,0:T(8,128)(2,1)S(1)} %get-tuple-element.56), channel_id=1, source_target_pairs={{0,6},{1,7},{2,4},{3,5},{4,10},{5,11},{6,8},{7,9},{8,14},{9,15},{1... | collective-permute-start | bytes 786440 | tf_op jit(solution)/shard_map/ppermute | solution.py:471
  23.3 3.5 %collective-permute-done.7.far_ref = bf16[3,512,128]{2,1,0:T(8,128)(2,1)S(1)} collective-permute-done((bf16[3,512,128]{2,1,0:T(8,128)(2,1)S(1)}, bf16[3,512,128]{2,1,0:T(8,128)(2,1)S(1)}, u32[]{:S(2)}, u32[]{:S(2)}) %collective-permute-start.7) | collective-permute-done | bytes 393248 | tf_op jit(solution)/shard_map/ppermute | solution.py:228
  26.8 1.5 %shard_map.94.taps_ref = f32[2,4,512,256]{3,2,1,0:T(8,128)S(1)} custom-call(bf16[512,256]{1,0:T(8,128)(2,1)S(1)} %copy-done.1, bf16[512,256]{1,0:T(8,128)(2,1)S(1)} %copy-done, bf16[1024,128]{1,0:T(8,128)(2,1)S(1)} %copy-done.5, bf16[3,512,128]{2,1,0:T(8,128)(2,1)S(1)} %shard_map.93.near_ref, bf16[3,512,128]{2,1,0:T(8,128)(2,1)S(1)} %collective-permute-done.7.far_ref), custom_call_target="tpu_custom_call" | custom-call | flops 1000 | bytes 1000 | tf_op jit(solution)/shard_map/pallas_call | solution.py:229
  28.4 3.4 %collective-permute-done.8.ahead_ref = bf16[2,2,256,256]{3,2,1,0:T(8,128)(2,1)S(1)} collective-permute-done((bf16[2,2,256,256]{3,2,1,0:T(8,128)(2,1)S(1)}, bf16[2,2,256,256]{3,2,1,0:T(8,128)(2,1)S(1)}, u32[]{:S(2)}, u32[]{:S(2)}) %collective-permute-start.8) | collective-permute-done | bytes 524320 | tf_op jit(solution)/shard_map/ppermute | solution.py:471
  31.7 3.5 %shard_map.96 = (f32[2,3,512,256]{3,2,1,0:T(8,128)S(1)}, f32[2,512,256]{2,1,0:T(8,128)S(1)}, f32[2,2,512,256]{3,2,1,0:T(8,128)S(1)}) custom-call(bf16[512,256]{1,0:T(8,128)(2,1)S(1)} %copy-done.1, bf16[512,256]{1,0:T(8,128)(2,1)S(1)} %copy-done, f32[2,4,512,256]{3,2,1,0:T(8,128)S(1)} %shard_map.94.taps_ref, ...), custom_call_target="tpu_custom_call" | custom-call | flops 1000 | bytes 1000 | tf_op jit(solution)/shard_map/pallas_call | solution.py:305
  35.2 2.3 %collective-permute-done.11.beyond_ref = bf16[2,256,256]{2,1,0:T(8,128)(2,1)S(1)} collective-permute-done((bf16[2,256,256]{2,1,0:T(8,128)(2,1)S(1)}, bf16[2,256,256]{2,1,0:T(8,128)(2,1)S(1)}, u32[]{:S(2)}, u32[]{:S(2)}) %collective-permute-start.11) | collective-permute-done | bytes 262176 | tf_op jit(solution)/shard_map/ppermute | solution.py:471
  37.5 2.3 %shard_map.97 = (bf16[256,256]{1,0:T(8,128)(2,1)S(1)}, bf16[256,256]{1,0:T(8,128)(2,1)S(1)}, bf16[256,256]{1,0:T(8,128)(2,1)S(1)}, bf16[256,256]{1,0:T(8,128)(2,1)S(1)}) custom-call(bf16[512,256]{1,0:T(8,128)(2,1)S(1)} %copy-done.1, bf16[512,256]{1,0:T(8,128)(2,1)S(1)} %copy-done, bf16[256,512]{1,0:T(8,128)(2,1)S(1)} %copy-done.4, ...), custom_call_target="tpu_custom_call" | custom-call | flops 1000 | bytes 1000 | tf_op jit(solution)/shard_map/pallas_call | solution.py:392
  39.8 1.3 %collective-permute-start.15 = (bf16[256,256]{1,0:T(8,128)(2,1)S(1)}, bf16[256,256]{1,0:T(8,128)(2,1)S(1)}, u32[]{:S(2)}, u32[]{:S(2)}) collective-permute-start(bf16[256,256]{1,0:T(8,128)(2,1)S(1)} %get-tuple-element.64), channel_id=1, source_target_pairs={{0,2},{1,3},{2,0},{3,1},{4,6},{5,7},{6,4},{7,5},{8,10},{9,11},{10,... | collective-permute-start | bytes 393224 | tf_op jit(solution)/shard_map/ppermute | solution.py:471
  41.1 0.9 %collective-permute-start.17 = (bf16[256,256]{1,0:T(8,128)(2,1)S(1)}, bf16[256,256]{1,0:T(8,128)(2,1)S(1)}, u32[]{:S(2)}, u32[]{:S(2)}) collective-permute-start(bf16[256,256]{1,0:T(8,128)(2,1)S(1)} %get-tuple-element.66), channel_id=1, source_target_pairs={{0,1},{1,0},{2,3},{3,2},{4,5},{5,4},{6,7},{7,6},{8,9},{9,8},{10,11... | collective-permute-start | bytes 393224 | tf_op jit(solution)/shard_map/ppermute | solution.py:471
  42.0 0.5 collective-permute-done.10.beyond_ref
  42.5 2.3 %shard_map.98 = (bf16[256,256]{1,0:T(8,128)(2,1)S(1)}, bf16[256,256]{1,0:T(8,128)(2,1)S(1)}, bf16[256,256]{1,0:T(8,128)(2,1)S(1)}, bf16[256,256]{1,0:T(8,128)(2,1)S(1)}) custom-call(bf16[512,256]{1,0:T(8,128)(2,1)S(1)} %copy-done.1, bf16[512,256]{1,0:T(8,128)(2,1)S(1)} %copy-done, bf16[256,512]{1,0:T(8,128)(2,1)S(1)} %copy-done.4, ...), custom_call_target="tpu_custom_call" | custom-call | flops 1000 | bytes 1000 | tf_op jit(solution)/shard_map/pallas_call | solution.py:392
  44.8 0.8 %collective-permute-start.12 = (bf16[256,256]{1,0:T(8,128)(2,1)S(1)}, bf16[256,256]{1,0:T(8,128)(2,1)S(1)}, u32[]{:S(2)}, u32[]{:S(2)}) collective-permute-start(bf16[256,256]{1,0:T(8,128)(2,1)S(1)} %get-tuple-element.61), channel_id=1, source_target_pairs={{0,2},{1,3},{2,0},{3,1},{4,6},{5,7},{6,4},{7,5},{8,10},{9,11},{10,... | collective-permute-start | bytes 393224 | tf_op jit(solution)/shard_map/ppermute | solution.py:471
  45.7 0.6 %collective-permute-done.15.refs_1_ = bf16[256,256]{1,0:T(8,128)(2,1)S(1)} collective-permute-done((bf16[256,256]{1,0:T(8,128)(2,1)S(1)}, bf16[256,256]{1,0:T(8,128)(2,1)S(1)}, u32[]{:S(2)}, u32[]{:S(2)}) %collective-permute-start.15) | collective-permute-done | bytes 131104 | tf_op jit(solution)/shard_map/ppermute | solution.py:471
  46.3 0.7 %collective-permute-start.14 = (bf16[256,256]{1,0:T(8,128)(2,1)S(1)}, bf16[256,256]{1,0:T(8,128)(2,1)S(1)}, u32[]{:S(2)}, u32[]{:S(2)}) collective-permute-start(bf16[256,256]{1,0:T(8,128)(2,1)S(1)} %get-tuple-element.63), channel_id=1, source_target_pairs={{0,1},{1,0},{2,3},{3,2},{4,5},{5,4},{6,7},{7,6},{8,9},{9,8},{10,11... | collective-permute-start | bytes 393224 | tf_op jit(solution)/shard_map/ppermute | solution.py:471
  47.1 0.9 %shard_map.99.refs_4_ = bf16[256,2048]{1,0:T(8,128)(2,1)} custom-call(bf16[256,2048]{1,0:T(8,128)(2,1)S(1)} %copy-done.2, bf16[256,256]{1,0:T(8,128)(2,1)S(1)} %get-tuple-element.59._.refs_0_, bf16[256,256]{1,0:T(8,128)(2,1)S(1)} %collective-permute-done.15.refs_1_, bf16[256,256]{1,0:T(8,128)(2,1)S(1)} %collective-permute-done.16.refs_2_, ...), custom_call_target="tpu_custom_call" | custom-call | flops 1000 | bytes 1000 | tf_op jit(solution)/shard_map/pallas_call | solution.py:445
  48.0 3.9 %collective-permute-done.12.refs_1_ = bf16[256,256]{1,0:T(8,128)(2,1)S(1)} collective-permute-done((bf16[256,256]{1,0:T(8,128)(2,1)S(1)}, bf16[256,256]{1,0:T(8,128)(2,1)S(1)}, u32[]{:S(2)}, u32[]{:S(2)}) %collective-permute-start.12) | collective-permute-done | bytes 131104 | tf_op jit(solution)/shard_map/ppermute | solution.py:471
  51.8 0.8 %collective-permute-done.13.refs_2_ = bf16[256,256]{1,0:T(8,128)(2,1)S(1)} collective-permute-done((bf16[256,256]{1,0:T(8,128)(2,1)S(1)}, bf16[256,256]{1,0:T(8,128)(2,1)S(1)}, u32[]{:S(2)}, u32[]{:S(2)}) %collective-permute-start.13) | collective-permute-done | bytes 131104 | tf_op jit(solution)/shard_map/ppermute | solution.py:471
  52.6 0.9 %shard_map.100 = bf16[256,2048]{1,0:T(8,128)(2,1)} custom-call(bf16[256,2048]{1,0:T(8,128)(2,1)S(1)} %copy-done.2, bf16[256,256]{1,0:T(8,128)(2,1)S(1)} %get-tuple-element.60.refs_0_, bf16[256,256]{1,0:T(8,128)(2,1)S(1)} %collective-permute-done.12.refs_1_, bf16[256,256]{1,0:T(8,128)(2,1)S(1)} %collective-permute-done.13.refs_2_, ...), custom_call_target="tpu_custom_call", output_to_operand_aliasing={{}: (5, {})} | custom-call | flops 1000 | bytes 1000 | tf_op jit(solution)/shard_map/pallas_call | solution.py:445
  (28 shorter events, 0.4 us)
Async XLA Ops:
  0.0 26.8 %copy-start = (bf16[512,256]{1,0:T(8,128)(2,1)S(1)}, bf16[512,256]{1,0:T(8,128)(2,1)}, u32[]{:S(2)}) copy-start(bf16[512,256]{1,0:T(8,128)(2,1)} %constant.9.clone.low_ref) | copy-start | bytes 786436
  0.0 26.8 %copy-start.1 = (bf16[512,256]{1,0:T(8,128)(2,1)S(1)}, bf16[512,256]{1,0:T(8,128)(2,1)}, u32[]{:S(2)}) copy-start(bf16[512,256]{1,0:T(8,128)(2,1)} %constant.8.clone.high_ref) | copy-start | bytes 786436
  0.0 26.8 %copy-start.5 = (bf16[1024,128]{1,0:T(8,128)(2,1)S(1)}, bf16[1024,128]{1,0:T(8,128)(2,1)}, u32[]{:S(2)}) copy-start(bf16[1024,128]{1,0:T(8,128)(2,1)} %own_ref.1) | copy-start | bytes 786436
  1.0 8.4 %collective-permute-start = (bf16[1,512,128]{2,1,0:T(8,128)(2,1)S(1)}, bf16[1,512,128]{2,1,0:T(8,128)(2,1)S(1)}, u32[]{:S(2)}, u32[]{:S(2)}) collective-permute-start(bf16[1,512,128]{2,1,0:T(8,128)(2,1)S(1)} %shard_map.91.half_ref), channel_id=1, source_target_pairs={{0,4},{1,5},{2,6},{3,7},{4,0},{5,1},{6,2},{7,3},{8,12},{9,13},{10,... | collective-permute-start | bytes 393224 | tf_op jit(solution)/shard_map/ppermute | solution.py:475
  4.1 8.7 %collective-permute-start.1 = (bf16[1,512,128]{2,1,0:T(8,128)(2,1)S(1)}, bf16[1,512,128]{2,1,0:T(8,128)(2,1)S(1)}, u32[]{:S(2)}, u32[]{:S(2)}) collective-permute-start(bf16[1,512,128]{2,1,0:T(8,128)(2,1)S(1)} %shard_map.91.half_ref), channel_id=1, source_target_pairs={{0,8},{1,9},{2,10},{3,11},{4,12},{5,13},{6,14},{7,15},{8,0},{9,1},... | collective-permute-start | bytes 393224 | tf_op jit(solution)/shard_map/ppermute | solution.py:475
  9.4 3.4 %collective-permute-start.2 = (bf16[256,256]{1,0:T(8,128)(2,1)S(1)}, bf16[256,256]{1,0:T(8,128)(2,1)S(1)}, u32[]{:S(2)}, u32[]{:S(2)}) collective-permute-start(bf16[256,256]{1,0:T(8,128)(2,1)S(1)} %get-tuple-element.41), channel_id=1, source_target_pairs={{0,1},{1,0},{2,3},{3,2},{4,5},{5,4},{6,7},{7,6},{8,9},{9,8},{10,11... | collective-permute-start | bytes 393224 | tf_op jit(solution)/shard_map/ppermute | solution.py:471
  9.4 3.4 %collective-permute-start.3 = (bf16[256,256]{1,0:T(8,128)(2,1)S(1)}, bf16[256,256]{1,0:T(8,128)(2,1)S(1)}, u32[]{:S(2)}, u32[]{:S(2)}) collective-permute-start(bf16[256,256]{1,0:T(8,128)(2,1)S(1)} %get-tuple-element.42), channel_id=1, source_target_pairs={{0,1},{1,0},{2,3},{3,2},{4,5},{5,4},{6,7},{7,6},{8,9},{9,8},{10,11... | collective-permute-start | bytes 393224 | tf_op jit(solution)/shard_map/ppermute | solution.py:471
  10.0 2.9 %collective-permute-start.4 = (bf16[256,256]{1,0:T(8,128)(2,1)S(1)}, bf16[256,256]{1,0:T(8,128)(2,1)S(1)}, u32[]{:S(2)}, u32[]{:S(2)}) collective-permute-start(bf16[256,256]{1,0:T(8,128)(2,1)S(1)} %get-tuple-element.43), channel_id=1, source_target_pairs={{0,1},{1,0},{2,3},{3,2},{4,5},{5,4},{6,7},{7,6},{8,9},{9,8},{10,11... | collective-permute-start | bytes 393224 | tf_op jit(solution)/shard_map/ppermute | solution.py:471
  10.0 2.9 %collective-permute-start.5 = (bf16[256,256]{1,0:T(8,128)(2,1)S(1)}, bf16[256,256]{1,0:T(8,128)(2,1)S(1)}, u32[]{:S(2)}, u32[]{:S(2)}) collective-permute-start(bf16[256,256]{1,0:T(8,128)(2,1)S(1)} %get-tuple-element.44), channel_id=1, source_target_pairs={{0,1},{1,0},{2,3},{3,2},{4,5},{5,4},{6,7},{7,6},{8,9},{9,8},{10,11... | collective-permute-start | bytes 393224 | tf_op jit(solution)/shard_map/ppermute | solution.py:471
  12.8 5.0 %collective-permute-start.6 = (bf16[1,512,128]{2,1,0:T(8,128)(2,1)S(1)}, bf16[1,512,128]{2,1,0:T(8,128)(2,1)S(1)}, u32[]{:S(2)}, u32[]{:S(2)}) collective-permute-start(bf16[1,512,128]{2,1,0:T(8,128)(2,1)S(1)} %collective-permute-done.1.refs_1_), channel_id=1, source_target_pairs={{0,4},{1,5},{2,6},{3,7},{4,0},{5,1},{6,2},{7,3},{8,12},{9,13},{10,... | collective-permute-start | bytes 393224 | tf_op jit(solution)/shard_map/ppermute | solution.py:475
  13.5 14.9 %collective-permute-start.9 = (bf16[2,2,256,256]{3,2,1,0:T(8,128)(2,1)S(1)}, bf16[2,2,256,256]{3,2,1,0:T(8,128)(2,1)S(1)}, u32[]{:S(2)}, u32[]{:S(2)}) collective-permute-start(bf16[2,2,256,256]{3,2,1,0:T(8,128)(2,1)S(1)} %get-tuple-element.53), channel_id=1, source_target_pairs={{0,2},{1,3},{2,0},{3,1},{4,6},{5,7},{6,4},{7,5},{8,10},{9,11},{10,... | collective-permute-start | bytes 1572872 | tf_op jit(solution)/shard_map/ppermute | solution.py:471
  15.0 16.7 %collective-permute-start.8 = (bf16[2,2,256,256]{3,2,1,0:T(8,128)(2,1)S(1)}, bf16[2,2,256,256]{3,2,1,0:T(8,128)(2,1)S(1)}, u32[]{:S(2)}, u32[]{:S(2)}) collective-permute-start(bf16[2,2,256,256]{3,2,1,0:T(8,128)(2,1)S(1)} %get-tuple-element.52.mine_ref), channel_id=1, source_target_pairs={{0,4},{1,5},{2,6},{3,7},{4,8},{5,9},{6,10},{7,11},{8,12},{9,13},{1... | collective-permute-start | bytes 1572872 | tf_op jit(solution)/shard_map/ppermute | solution.py:471
  17.9 8.9 %collective-permute-start.7 = (bf16[3,512,128]{2,1,0:T(8,128)(2,1)S(1)}, bf16[3,512,128]{2,1,0:T(8,128)(2,1)S(1)}, u32[]{:S(2)}, u32[]{:S(2)}) collective-permute-start(bf16[3,512,128]{2,1,0:T(8,128)(2,1)S(1)} %shard_map.93.near_ref), channel_id=1, source_target_pairs={{0,16},{16,0},{1,17},{17,1},{2,18},{18,2},{3,19},{19,3},{4,20},{20... | collective-permute-start | bytes 1179656 | tf_op jit(solution)/shard_map/ppermute | solution.py:228
  19.5 18.0 %collective-permute-start.11 = (bf16[2,256,256]{2,1,0:T(8,128)(2,1)S(1)}, bf16[2,256,256]{2,1,0:T(8,128)(2,1)S(1)}, u32[]{:S(2)}, u32[]{:S(2)}) collective-permute-start(bf16[2,256,256]{2,1,0:T(8,128)(2,1)S(1)} %get-tuple-element.58), channel_id=1, source_target_pairs={{0,6},{1,7},{2,4},{3,5},{4,10},{5,11},{6,8},{7,9},{8,14},{9,15},{1... | collective-permute-start | bytes 786440 | tf_op jit(solution)/shard_map/ppermute | solution.py:471
  22.3 20.2 %collective-permute-start.10 = (bf16[2,256,256]{2,1,0:T(8,128)(2,1)S(1)}, bf16[2,256,256]{2,1,0:T(8,128)(2,1)S(1)}, u32[]{:S(2)}, u32[]{:S(2)}) collective-permute-start(bf16[2,256,256]{2,1,0:T(8,128)(2,1)S(1)} %get-tuple-element.56), channel_id=1, source_target_pairs={{0,6},{1,7},{2,4},{3,5},{4,10},{5,11},{6,8},{7,9},{8,14},{9,15},{1... | collective-permute-start | bytes 786440 | tf_op jit(solution)/shard_map/ppermute | solution.py:471
  28.3 9.2 %copy-start.3 = (bf16[256,512]{1,0:T(8,128)(2,1)S(1)}, bf16[256,512]{1,0:T(8,128)(2,1)}, u32[]{:S(2)}) copy-start(bf16[256,512]{1,0:T(8,128)(2,1)} %constant.11.clone.back_low_ref) | copy-start | bytes 786436
  28.3 9.2 %copy-start.4 = (bf16[256,512]{1,0:T(8,128)(2,1)S(1)}, bf16[256,512]{1,0:T(8,128)(2,1)}, u32[]{:S(2)}) copy-start(bf16[256,512]{1,0:T(8,128)(2,1)} %constant.10.clone.back_high_ref) | copy-start | bytes 786436
  28.3 9.2 %copy-start.6 = (f32[2048]{0:T(1024)S(1)}, f32[2048]{0:T(1024)}, u32[]{:S(2)}) copy-start(f32[2048]{0:T(1024)} %param.13) | copy-start | bytes 24580
  39.8 6.5 %collective-permute-start.15 = (bf16[256,256]{1,0:T(8,128)(2,1)S(1)}, bf16[256,256]{1,0:T(8,128)(2,1)S(1)}, u32[]{:S(2)}, u32[]{:S(2)}) collective-permute-start(bf16[256,256]{1,0:T(8,128)(2,1)S(1)} %get-tuple-element.64), channel_id=1, source_target_pairs={{0,2},{1,3},{2,0},{3,1},{4,6},{5,7},{6,4},{7,5},{8,10},{9,11},{10,... | collective-permute-start | bytes 393224 | tf_op jit(solution)/shard_map/ppermute | solution.py:471
  41.1 5.9 %collective-permute-start.16 = (bf16[256,256]{1,0:T(8,128)(2,1)S(1)}, bf16[256,256]{1,0:T(8,128)(2,1)S(1)}, u32[]{:S(2)}, u32[]{:S(2)}) collective-permute-start(bf16[256,256]{1,0:T(8,128)(2,1)S(1)} %get-tuple-element.65), channel_id=1, source_target_pairs={{0,3},{1,2},{2,1},{3,0},{4,7},{5,6},{6,5},{7,4},{8,11},{9,10},{10,... | collective-permute-start | bytes 393224 | tf_op jit(solution)/shard_map/ppermute | solution.py:471
  41.1 5.9 %collective-permute-start.17 = (bf16[256,256]{1,0:T(8,128)(2,1)S(1)}, bf16[256,256]{1,0:T(8,128)(2,1)S(1)}, u32[]{:S(2)}, u32[]{:S(2)}) collective-permute-start(bf16[256,256]{1,0:T(8,128)(2,1)S(1)} %get-tuple-element.66), channel_id=1, source_target_pairs={{0,1},{1,0},{2,3},{3,2},{4,5},{5,4},{6,7},{7,6},{8,9},{9,8},{10,11... | collective-permute-start | bytes 393224 | tf_op jit(solution)/shard_map/ppermute | solution.py:471
  42.5 4.6 %copy-start.2 = (bf16[256,2048]{1,0:T(8,128)(2,1)S(1)}, bf16[256,2048]{1,0:T(8,128)(2,1)}, u32[]{:S(2)}) copy-start(bf16[256,2048]{1,0:T(8,128)(2,1)} %gate_ref.3) | copy-start | bytes 3145732
  44.8 7.1 %collective-permute-start.12 = (bf16[256,256]{1,0:T(8,128)(2,1)S(1)}, bf16[256,256]{1,0:T(8,128)(2,1)S(1)}, u32[]{:S(2)}, u32[]{:S(2)}) collective-permute-start(bf16[256,256]{1,0:T(8,128)(2,1)S(1)} %get-tuple-element.61), channel_id=1, source_target_pairs={{0,2},{1,3},{2,0},{3,1},{4,6},{5,7},{6,4},{7,5},{8,10},{9,11},{10,... | collective-permute-start | bytes 393224 | tf_op jit(solution)/shard_map/ppermute | solution.py:471
  45.6 7.0 %collective-permute-start.13 = (bf16[256,256]{1,0:T(8,128)(2,1)S(1)}, bf16[256,256]{1,0:T(8,128)(2,1)S(1)}, u32[]{:S(2)}, u32[]{:S(2)}) collective-permute-start(bf16[256,256]{1,0:T(8,128)(2,1)S(1)} %get-tuple-element.62), channel_id=1, source_target_pairs={{0,3},{1,2},{2,1},{3,0},{4,7},{5,6},{6,5},{7,4},{8,11},{9,10},{10,... | collective-permute-start | bytes 393224 | tf_op jit(solution)/shard_map/ppermute | solution.py:471
  46.3 6.3 %collective-permute-start.14 = (bf16[256,256]{1,0:T(8,128)(2,1)S(1)}, bf16[256,256]{1,0:T(8,128)(2,1)S(1)}, u32[]{:S(2)}, u32[]{:S(2)}) collective-permute-start(bf16[256,256]{1,0:T(8,128)(2,1)S(1)} %get-tuple-element.63), channel_id=1, source_target_pairs={{0,1},{1,0},{2,3},{3,2},{4,5},{5,4},{6,7},{7,6},{8,9},{9,8},{10,11... | collective-permute-start | bytes 393224 | tf_op jit(solution)/shard_map/ppermute | solution.py:471
